TPU v7x, 512 devices: a whole 4x4x16 slice. The times are simulated.
512 devices in a mesh: dp: 128 (over z, x, core), mp: 4 (over y).
Axes of the slice: x: 4, y: 4, z: 16, core: 2. Of those that a mesh axis runs over, the one named last changes fastest.
Arguments:
- session_length: int32 [128], P('dp'), may hold values from 1 to 128
- event_owner: int32 [16384, 1], P('dp'), may hold values from 0 to 127; in each aligned block of 128 rows (0 to 127, 128 to 255, ...) at most 2 rows name the same one
- event_row: int32 [16384], P('dp'), may hold values from 0 to 255
- text_rows: bfloat16 [32768, 4096], P('dp', 'mp'), may hold values from -6 to 6
- image_rows: bfloat16 [32768, 4096], P('dp', 'mp'), may hold values from -6 to 6
- price: float32 [32768], P('dp'), may hold values from 0.2 to 5
- price_dir: bfloat16 [4096], P('mp'), may hold values from -4 to 4
- norm_gain: bfloat16 [4096], P('mp'), may hold values from 0.5 to 1.5
- w_query: bfloat16 [4096, 2048], P('dp', 'mp'), may hold values from -1 to 1
- w_key: bfloat16 [4096, 2048], P('dp', 'mp'), may hold values from -1 to 1
- w_value: bfloat16 [4096, 2048], P('dp', 'mp'), may hold values from -0.09375 to 0.09375
- cotangent: bfloat16 [16384, 4096], P('dp', 'mp'), may hold values from -6 to 6
Outputs:
- context: bfloat16 [16384, 2048], P('dp', 'mp')
- text_grad: float32 [32768, 4096], P('dp', 'mp')
- image_grad: float32 [32768, 4096], P('dp', 'mp')
Inputs may be any that keep to these rules, and one draw needn't show every extreme that they name: `event_owner`: among the event slots of one index of dp, no owner is named more than 2 times, a bound that some block reaches.
All inputs are finite; a program needn't handle non-finite values.
Results may differ from a plain program's by a relative error of at most 0.0063.
Values may be sent and summed in bfloat16 or wider, within the bound.
No kernel may reach another device: no remote copies, remote signals or barrier semaphores. Data moves between devices by JAX's collectives and lax.ppermute only.
A program may use at most 64 MiB of HBM per device.

v0:
```python
import math

import jax
import jax.numpy as jnp
from jax import lax
from jax.sharding import PartitionSpec as P

D = 4096
HD = 128
SLOT = 128


def fetch_rows(requests, text_rows, image_rows):
    row_ids = jnp.maximum(requests, 0)
    return (row_ids, text_rows[row_ids], image_rows[row_ids])


def join_rows(row_ids, text_got, image_got, price, price_dir):
    price_got = price[row_ids]
    mixed = text_got.astype(jnp.float32) * image_got.astype(jnp.float32) + price_got[
        ..., None
    ] * price_dir.astype(jnp.float32)
    return mixed.astype(jnp.bfloat16)


def answer(requests, text_rows, image_rows, price, price_dir):
    row_ids, text_got, image_got = fetch_rows(requests, text_rows, image_rows)
    joined_rows = join_rows(row_ids, text_got, image_got, price, price_dir)
    replies = lax.all_to_all(joined_rows, "dp", split_axis=0, concat_axis=0, tiled=True)
    return (replies, row_ids, text_got, image_got)


def credit_rows(row_ids, grad_rows, text_got, image_got, table_rows):
    col_width = grad_rows.shape[-1]
    flat_ids = row_ids.reshape(-1)
    grad_float = grad_rows.astype(jnp.float32)
    text_terms = (grad_float * image_got.astype(jnp.float32)).reshape(-1, col_width)
    image_terms = (grad_float * text_got.astype(jnp.float32)).reshape(-1, col_width)
    text_grad = jax.ops.segment_sum(text_terms, flat_ids, num_segments=table_rows)
    image_grad = jax.ops.segment_sum(image_terms, flat_ids, num_segments=table_rows)
    return (text_grad, image_grad)


def attend(query, keys, values, session_length):
    sessions = session_length.shape[0]
    heads_here = query.shape[1] // HD
    shape4 = (sessions, SLOT, heads_here, HD)
    scores = jnp.einsum(
        "sqhd,skhd->shqk",
        query.reshape(shape4),
        keys.reshape(shape4),
        preferred_element_type=jnp.float32,
    ) / math.sqrt(HD)
    position = jnp.arange(SLOT, dtype=jnp.int32)
    live_mask = position[None, :] < session_length[:, None]
    allowed = (position[None, :] <= position[:, None])[None, None, :, :] & live_mask[
        :, None, None, :
    ]
    scores = jnp.where(allowed, scores, jnp.float32(-1e30))
    row_max = jnp.max(scores, axis=-1, keepdims=True)
    powers = jnp.exp(scores - row_max)
    probs = (powers / jnp.sum(powers, axis=-1, keepdims=True)).astype(jnp.bfloat16)
    context = jnp.einsum(
        "shqk,skhd->sqhd", probs, values.reshape(shape4), preferred_element_type=jnp.float32
    )
    context = jnp.where(live_mask[:, :, None, None], context, jnp.float32(0.0))
    return context.reshape(sessions * SLOT, heads_here * HD).astype(jnp.bfloat16)


def local(
    session_length,
    event_owner,
    event_row,
    text_rows,
    image_rows,
    price,
    price_dir,
    norm_gain,
    w_query,
    w_key,
    w_value,
    cotangent,
):
    peers = lax.axis_size("dp")
    tok_count = event_row.shape[0]
    capacity = 2 * tok_count // peers
    col_width = text_rows.shape[1]
    table_rows = text_rows.shape[0]
    owner_ids = event_owner[:, 0]
    member = (owner_ids[:, None] == jnp.arange(peers, dtype=jnp.int32)[None, :]).astype(jnp.int32)
    earlier = jnp.sum((jnp.cumsum(member, axis=0) - member) * member, axis=1)
    slot_ids = owner_ids * capacity + earlier
    requests = (
        jnp.full((peers * capacity,), -1, jnp.int32)
        .at[slot_ids]
        .set(event_row)
        .reshape(peers, capacity)
    )
    grad_buffer = (
        jnp.zeros((peers * capacity, col_width), jnp.bfloat16)
        .at[slot_ids]
        .set(cotangent)
        .reshape(peers, capacity, col_width)
    )
    replies = answer(
        lax.all_to_all(requests, "dp", split_axis=0, concat_axis=0, tiled=True),
        text_rows,
        image_rows,
        price,
        price_dir,
    )[0]
    got_ids, got_grads = (
        lax.all_to_all(requests, "dp", split_axis=0, concat_axis=0, tiled=True),
        lax.all_to_all(grad_buffer, "dp", split_axis=0, concat_axis=0, tiled=True),
    )
    row_ids, text_got, image_got = fetch_rows(got_ids, text_rows, image_rows)
    text_grad, image_grad = credit_rows(row_ids, got_grads, text_got, image_got, table_rows)
    joined_rows = replies.reshape(peers * capacity, col_width)[slot_ids]
    joined_float = joined_rows.astype(jnp.float32)
    square_sums = lax.psum(jnp.sum(joined_float * joined_float, axis=1), "mp")
    scale = lax.rsqrt(square_sums / D + 1e-06)
    normed = (joined_float * scale[:, None] * norm_gain.astype(jnp.float32)[None, :]).astype(
        jnp.bfloat16
    )
    features_all = lax.all_gather(normed, "mp", axis=1, tiled=True)

    def add_rows(weight_rows):
        return jnp.dot(features_all, weight_rows, preferred_element_type=jnp.float32)

    query_sum = add_rows(lax.all_gather(w_query, "dp", axis=0, tiled=True))
    key_sum = add_rows(lax.all_gather(w_key, "dp", axis=0, tiled=True))
    value_sum = add_rows(lax.all_gather(w_value, "dp", axis=0, tiled=True))
    context = attend(
        query_sum.astype(jnp.bfloat16),
        key_sum.astype(jnp.bfloat16),
        value_sum.astype(jnp.bfloat16),
        session_length,
    )
    return (context, text_grad, image_grad)


def solution(mesh):
    return jax.shard_map(
        local,
        mesh=mesh,
        in_specs=(
            P("dp"),
            P("dp", None),
            P("dp"),
            P("dp", "mp"),
            P("dp", "mp"),
            P("dp"),
            P("mp"),
            P("mp"),
            P("dp", "mp"),
            P("dp", "mp"),
            P("dp", "mp"),
            P("dp", "mp"),
        ),
        out_specs=(P("dp", "mp"), P("dp", "mp"), P("dp", "mp")),
        check_vma=False,
    )
```

profile of v0, /device:TPU:1, one launch (start us, length us, event | category | flops | bytes accessed | tf_op | source)
XLA Modules:
  0.0 602.6 jit_solution(7912905382597587258)
XLA Ops:
  7.2 0.8 fusion.22
  8.0 0.2 reduce_window_sum.11
  8.2 0.8 select_reduce_fusion
  9.0 0.7 fusion.24
  9.7 1.1 scatter_custom_fusion
  10.8 0.8 all_to_all.13
  11.5 20.4 %all-to-all-start = ((s32[128,1,2]{2,1,0:T(1,128)}), s32[128,1,2]{2,1,0:T(1,128)S(1)}, u32[]{:S(2)}, u32[]{:S(2)}) async-start(s32[128,1,2]{2,1,0:T(1,128)} %bitcast.4), calls=%async_computation | async-start | bytes 131072 | tf_op jit(solution)/shard_map/all_to_all | solution.py:106
  31.9 1.7 scatter_custom_fusion.1
  33.7 1.0 reshape.139
  34.7 12.1 %all-to-all-done = s32[128,1,2]{2,1,0:T(1,128)S(1)} async-done(((s32[128,1,2]{2,1,0:T(1,128)}), s32[128,1,2]{2,1,0:T(1,128)S(1)}, u32[]{:S(2)}, u32[]{:S(2)}) %all-to-all-start) | async-done | bytes 1056 | tf_op jit(solution)/shard_map/all_to_all | solution.py:106
  46.8 5.7 all-to-all-start.2
  52.4 0.7 convert_element_type.54
  53.1 0.2 maximum_reduce_fusion
  53.3 0.1 reshape.144
  53.5 1.2 gather_fusion
  54.7 1.6 reshape.214
  56.3 1.9 gather_fusion.2
  58.2 0.1 reshape.159
  58.4 1.2 gather_fusion.1
  59.6 1.6 reshape.215
  61.2 22.5 %all-to-all-done.2 = bf16[128,2,1024]{2,1,0:T(2,128)(2,1)S(1)} async-done(((bf16[128,2,1024]{2,1,0:T(2,128)(2,1)}), bf16[128,2,1024]{2,1,0:T(2,128)(2,1)S(1)}, u32[]{:S(2)}, u32[]{:S(2)}) %all-to-all-start.2) | async-done | bytes 524320 | tf_op jit(solution)/shard_map/all_to_all | solution.py:114
  83.7 3.1 convert_multiply_fusion
  86.9 9.2 %all-to-all-start.1 = ((bf16[128,2,1024]{2,1,0:T(2,128)(2,1)}), bf16[128,2,1024]{2,1,0:T(2,128)(2,1)}, u32[]{:S(2)}, u32[]{:S(2)}) async-start(bf16[128,2,1024]{2,1,0:T(2,128)(2,1)} %get-tuple-element.13), calls=%async_computation.1 | async-start | bytes 1048576 | tf_op jit(solution)/shard_map/all_to_all | solution.py:29
  96.1 0.2 all-gather.5.cloned.1.call-start
  96.4 30.2 %all-to-all-done.1 = bf16[128,2,1024]{2,1,0:T(2,128)(2,1)} async-done(((bf16[128,2,1024]{2,1,0:T(2,128)(2,1)}), bf16[128,2,1024]{2,1,0:T(2,128)(2,1)}, u32[]{:S(2)}, u32[]{:S(2)}) %all-to-all-start.1) | async-done | bytes 524320 | tf_op jit(solution)/shard_map/all_to_all | solution.py:29
  126.6 1.2 reshape.135
  127.8 0.9 gather_fusion.3
  128.7 0.1 fusion.8
  128.8 8.7 %psum.7 = f32[128]{0:T(128)S(1)} all-reduce(f32[128]{0:T(128)S(1)} %fusion.8), channel_id=1, replica_groups=mesh['dp'=128,'mp'=4] {'mp'}, use_global_device_ids=true, to_apply=%region_4.5 | all-reduce | flops 128 | bytes 1024 | tf_op jit(solution)/shard_map/psum | solution.py:120
  137.6 0.8 fusion.10
  138.5 0.7 all-gather.7.cloned.1.call-update
  139.2 0.7 all-gather.11.cloned.1.call-update
  139.9 0.5 all-gather.9.cloned.1.call-update
  141.2 1.7 reshape.194
  142.9 0.7 reshape.202
  143.6 4.3 scatter_custom_fusion.2
  147.9 3.6 scatter_custom_fusion.3
  151.5 11.5 %all-gather.5.cloned.1.call-done = bf16[128,4096]{1,0:T(8,128)(2,1)} async-done(((bf16[128,1024]{1,0:T(8,128)(2,1)}), bf16[128,4096]{1,0:T(8,128)(2,1)}) %all-gather.5.cloned.1.call-update) | async-done | bytes 1048592 | tf_op jit(solution)/shard_map/all_gather | solution.py:125
  163.0 146.8 %all-gather.7.cloned.1.call-done = bf16[4096,512]{1,0:T(8,128)(2,1)} async-done(((bf16[32,512]{1,0:T(8,128)(2,1)}), bf16[4096,512]{1,0:T(8,128)(2,1)}) %all-gather.7.cloned.1.call-update) | async-done | bytes 4194320 | tf_op jit(solution)/shard_map/all_gather | solution.py:132
  309.8 3.2 convolution_convert_fusion.2
  313.1 0.1 copy.32
  313.2 137.7 %all-gather.11.cloned.1.call-done = bf16[4096,512]{1,0:T(8,128)(2,1)} async-done(((bf16[32,512]{1,0:T(8,128)(2,1)}), bf16[4096,512]{1,0:T(8,128)(2,1)}) %all-gather.11.cloned.1.call-update) | async-done | bytes 4194320 | tf_op jit(solution)/shard_map/all_gather | solution.py:131
  450.9 2.9 fusion.7
  453.8 138.0 %all-gather.9.cloned.1.call-done = bf16[4096,512]{1,0:T(8,128)(2,1)} async-done(((bf16[32,512]{1,0:T(8,128)(2,1)}), bf16[4096,512]{1,0:T(8,128)(2,1)}) %all-gather.9.cloned.1.call-update) | async-done | bytes 4194320 | tf_op jit(solution)/shard_map/all_gather | solution.py:130
  591.9 2.9 fusion.6
  594.8 0.2 fusion.2
  595.1 0.2 fusion.5
  595.3 0.8 copy.30
  (21 shorter events, 0.4 us)
Async XLA Ops:
  7.2 46.3 %copy-start = (bf16[256,1024]{1,0:T(8,128)(2,1)S(1)}, bf16[256,1024]{1,0:T(8,128)(2,1)}, u32[]{:S(2)}) copy-start(bf16[256,1024]{1,0:T(8,128)(2,1)} %param.15) | copy-start | bytes 1572868
  11.5 35.2 %all-to-all-start = ((s32[128,1,2]{2,1,0:T(1,128)}), s32[128,1,2]{2,1,0:T(1,128)S(1)}, u32[]{:S(2)}, u32[]{:S(2)}) async-start(s32[128,1,2]{2,1,0:T(1,128)} %bitcast.4), calls=%async_computation | async-start | bytes 131072 | tf_op jit(solution)/shard_map/all_to_all | solution.py:106
  33.7 22.6 %copy-start.1 = (f32[256]{0:T(256)S(1)}, f32[256]{0:T(256)}, u32[]{:S(2)}) copy-start(f32[256]{0:T(256)} %param.17) | copy-start | bytes 3076
  46.8 37.0 %all-to-all-start.2 = ((bf16[128,2,1024]{2,1,0:T(2,128)(2,1)}), bf16[128,2,1024]{2,1,0:T(2,128)(2,1)S(1)}, u32[]{:S(2)}, u32[]{:S(2)}) async-start(bf16[128,2,1024]{2,1,0:T(2,128)(2,1)} %reshape.139), calls=%async_computation.2 | async-start | bytes 1048576 | tf_op jit(solution)/shard_map/all_to_all | solution.py:114
  56.3 2.1 copy-start.2
  59.6 36.8 %copy-start.4 = (bf16[1024]{0:T(1024)(128)(2,1)S(1)}, bf16[1024]{0:T(1024)(128)(2,1)}, u32[]{:S(2)}) copy-start(bf16[1024]{0:T(1024)(128)(2,1)} %param.19) | copy-start | bytes 6148
  86.9 39.7 %all-to-all-start.1 = ((bf16[128,2,1024]{2,1,0:T(2,128)(2,1)}), bf16[128,2,1024]{2,1,0:T(2,128)(2,1)}, u32[]{:S(2)}, u32[]{:S(2)}) async-start(bf16[128,2,1024]{2,1,0:T(2,128)(2,1)} %get-tuple-element.13), calls=%async_computation.1 | async-start | bytes 1048576 | tf_op jit(solution)/shard_map/all_to_all | solution.py:29
  96.1 66.9 %all-gather.5.cloned.1.call-start = ((), (), s32[]{:S(2)}) async-start(), calls=%async_computation.3 | async-start | bytes 1310720 | tf_op jit(solution)/shard_map/all_gather | solution.py:125
  138.4 171.4 %all-gather.7.cloned.1.call-start = ((), (), s32[]{:S(2)}) async-start(), calls=%async_computation.4 | async-start | bytes 4227072 | tf_op jit(solution)/shard_map/all_gather | solution.py:132
  139.2 311.8 %all-gather.11.cloned.1.call-start = ((), (), s32[]{:S(2)}) async-start(), calls=%async_computation.6 | async-start | bytes 4227072 | tf_op jit(solution)/shard_map/all_gather | solution.py:131
  139.9 452.0 %all-gather.9.cloned.1.call-start = ((), (), s32[]{:S(2)}) async-start(), calls=%async_computation.5 | async-start | bytes 4227072 | tf_op jit(solution)/shard_map/all_gather | solution.py:130
  163.0 287.9 %copy-start.3 = (bf16[128,4096]{1,0:T(8,128)(2,1)S(1)}, bf16[128,4096]{1,0:T(8,128)(2,1)}, u32[]{:S(2)}) copy-start(bf16[128,4096]{1,0:T(8,128)(2,1)} %all-gather.5.cloned.1.call-done) | copy-start | bytes 3145732
Sparse Core Ops, SparseCore 0:
  138.5 24.4 all-gather.4
  166.2 143.6 all-gather.6
  313.0 137.8 all-gather.10
  453.9 137.9 all-gather.8
where the time goes:
time: 603 us
  waiting for transfers between devices  501 us (83%)
  starting transfers between devices  35.6 us (6%)
  local copies, waits for them, and re-layouts  17.8 us (3%)
  other arithmetic  15.6 us (3%)
  between operations  14.6 us (2%)
  matrix products  9.46 us (2%)
  blocking collectives  8.72 us (1%)
    all_gather x1, waiting for transfers between devices, local(): value_sum = add_rows(lax.all_gather(w_value, 'dp', axis=0, tiled=True))  147 us
    all_gather x1, waiting for transfers between devices, local(): query_sum = add_rows(lax.all_gather(w_query, 'dp', axis=0, tiled=True))  138 us
    all_gather x1, waiting for transfers between devices, local(): key_sum = add_rows(lax.all_gather(w_key, 'dp', axis=0, tiled=True))  138 us
    all_to_all x1, waiting for transfers between devices, answer(): lax.all_to_all(joined_rows, 'dp', split_axis=0, concat_axis=0, tiled=True)  30.2 us
    all_to_all x1, waiting for transfers between devices, local(): lax.all_to_all(grad_buffer, 'dp', split_axis=0, concat_axis=0, tiled=True)  22.5 us
    all_to_all x1, starting transfers between devices, local(): lax.all_to_all(requests, 'dp', split_axis=0, concat_axis=0, tiled=True)  20.4 us
    all_to_all x1, waiting for transfers between devices, local(): lax.all_to_all(requests, 'dp', split_axis=0, concat_axis=0, tiled=True)  12.1 us
  transfers between devices with their start and end apart: 7, of which 7 were waited for; matrix products, arithmetic and copies ran while one was open for 5% of the time, Pallas kernels for 0%

commit v1 on v0

v1 whole, which is shorter than its diff:
```python
import math

import jax
import jax.numpy as jnp
from jax import lax
from jax.sharding import PartitionSpec as P

HD = 128
SLOT = 128


def one_hot(rows, columns):
    return (rows[:, None] == columns[None, :]).astype(jnp.bfloat16)


def pick(selector, values):
    return jnp.dot(selector, values, preferred_element_type=jnp.float32)


def attend(query, keys, values, session_length):
    heads_here = query.shape[1] // HD
    shape3 = (SLOT, heads_here, HD)
    scores = jnp.einsum(
        "qhd,khd->hqk",
        query.reshape(shape3),
        keys.reshape(shape3),
        preferred_element_type=jnp.float32,
    ) / math.sqrt(HD)
    position = jnp.arange(SLOT, dtype=jnp.int32)
    live_mask = position < session_length[0]
    allowed = (position[None, :] <= position[:, None])[None] & live_mask[None, None, :]
    scores = jnp.where(allowed, scores, jnp.float32(-1e30))
    row_max = jnp.max(scores, axis=-1, keepdims=True)
    powers = jnp.exp(scores - row_max)
    probs = (powers / jnp.sum(powers, axis=-1, keepdims=True)).astype(jnp.bfloat16)
    context = jnp.einsum(
        "hqk,khd->qhd", probs, values.reshape(shape3), preferred_element_type=jnp.float32
    )
    context = jnp.where(live_mask[:, None, None], context, jnp.float32(0.0))
    return context.reshape(SLOT, heads_here * HD).astype(jnp.bfloat16)


def local(
    session_length,
    event_owner,
    event_row,
    text_rows,
    image_rows,
    price,
    price_dir,
    norm_gain,
    w_query,
    w_key,
    w_value,
    cotangent,
):
    peers = lax.axis_size("dp")
    parts = lax.axis_size("mp")
    mine = lax.axis_index("mp")
    tok_count = event_row.shape[0]
    capacity = 2 * tok_count // peers
    col_width = text_rows.shape[1]
    table_rows = text_rows.shape[0]
    slots = jnp.arange(peers * capacity, dtype=jnp.int32)

    weights = lax.all_gather(
        jnp.concatenate([w_query, w_key, w_value], axis=1), "dp", axis=0, tiled=True
    )

    owner_ids = event_owner[:, 0]
    place = jnp.arange(tok_count, dtype=jnp.int32)
    same = (owner_ids[:, None] == owner_ids[None, :]) & (place[None, :] < place[:, None])
    slot_ids = owner_ids * capacity + jnp.sum(same.astype(jnp.int32), axis=1)
    taken = slots[:, None] == slot_ids[None, :]
    requests = (
        jnp.sum(jnp.where(taken, event_row[None, :] + 1, 0), axis=1) - 1
    ).reshape(peers, capacity)
    got_ids = lax.all_to_all(requests, "dp", split_axis=0, concat_axis=0, tiled=True).reshape(-1)

    text_float = text_rows.astype(jnp.float32)
    image_float = image_rows.astype(jnp.float32)
    table = (
        text_float * image_float + price[:, None] * price_dir.astype(jnp.float32)[None, :]
    ).astype(jnp.bfloat16)
    wanted = one_hot(got_ids, jnp.arange(table_rows, dtype=jnp.int32))
    replies = lax.all_to_all(
        pick(wanted, table).astype(jnp.bfloat16).reshape(peers, capacity, col_width),
        "dp",
        split_axis=0,
        concat_axis=0,
        tiled=True,
    ).reshape(peers * capacity, col_width)

    grad_buffer = pick(taken.astype(jnp.bfloat16), cotangent).astype(jnp.bfloat16)
    grad_buffer, replies = lax.optimization_barrier((grad_buffer, replies))
    got_grads = lax.all_to_all(
        grad_buffer.reshape(peers, capacity, col_width),
        "dp",
        split_axis=0,
        concat_axis=0,
        tiled=True,
    ).reshape(peers * capacity, col_width)
    row_sums = pick(wanted.T, got_grads)
    text_grad = row_sums * image_float
    image_grad = row_sums * text_float

    joined = pick(one_hot(slot_ids, slots), replies).astype(jnp.bfloat16)
    turns = [
        joined if k == 0 else lax.ppermute(joined, "mp", [(i, (i + k) % parts) for i in range(parts)])
        for k in range(parts)
    ]
    stacked = jnp.stack(turns)
    features = jnp.concatenate(
        [
            lax.dynamic_index_in_dim(stacked, (mine - s) % parts, 0, keepdims=False)
            for s in range(parts)
        ],
        axis=1,
    ).astype(jnp.float32)
    gain = lax.all_gather(norm_gain, "mp", axis=0, tiled=True).astype(jnp.float32)
    scale = lax.rsqrt(jnp.mean(features * features, axis=1, keepdims=True) + 1e-06)
    normed = (features * scale * gain[None, :]).astype(jnp.bfloat16)
    projected = jnp.dot(normed, weights, preferred_element_type=jnp.float32).astype(jnp.bfloat16)
    width = w_query.shape[1]
    context = attend(
        projected[:, :width],
        projected[:, width : 2 * width],
        projected[:, 2 * width :],
        session_length,
    )
    return (context, text_grad, image_grad)


def solution(mesh):
    return jax.shard_map(
        local,
        mesh=mesh,
        in_specs=(
            P("dp"),
            P("dp", None),
            P("dp"),
            P("dp", "mp"),
            P("dp", "mp"),
            P("dp"),
            P("mp"),
            P("mp"),
            P("dp", "mp"),
            P("dp", "mp"),
            P("dp", "mp"),
            P("dp", "mp"),
        ),
        out_specs=(P("dp", "mp"), P("dp", "mp"), P("dp", "mp")),
        check_vma=False,
    )
```

time: 603 us -> 197 us (0.33)
  waiting for transfers between devices: 501 us -> 101 us
  local copies, waits for them, and re-layouts: 17.8 us -> 4.84 us
  starting transfers between devices: 35.6 us -> 46.2 us
  other arithmetic: 15.6 us -> 5.29 us
    all_gather x4 -> x1, waiting for transfers between devices: 434 us -> 45.6 us  [local(): lax.all_gather(jnp.concatenate([w_query, w_key, w_value], axis=1), 'dp',...]
    all_gather x0 -> x1, blocking collectives: none -> 13 us  [local(): lax.all_gather(norm_gain, 'mp', axis=0, tiled=True).astype(jnp.float32)]
    all_to_all x2, waiting for transfers between devices: 52.7 us -> 41.3 us  [the longest x1 33.6 us: local(): lax.all_to_all(pick(wanted, table).astype(jnp.bfloat16).reshape(peers, ca...]
    ppermute x0 -> x3, starting transfers between devices: none -> 10.6 us  [local(): lax.ppermute(joined, 'mp', [(i, (i + k) % parts) for i in range(parts)])]
    psum x1 -> x0, blocking collectives: 8.72 us -> none  [local(): square_sums = lax.psum(jnp.sum(joined_float * joined_float, axis=1), 'mp')]
    scatter-add x2 -> x0, other arithmetic: 7.9 us -> none  [the longest x1 4.29 us: credit_rows(): jax.ops.segment_sum(text_terms, flat_ids, num_segments=table_rows)]
  transfers between devices with their start and end apart: 7 -> 7, of which waited for: 7 -> 4; matrix products, arithmetic and copies ran while one was open for 5% -> 6% of each run, Pallas kernels for 0% -> 0%
where the time goes in v1:
time: 197 us; the launch traced here: 196 us
  waiting for transfers between devices  101 us (51%)
  starting transfers between devices  46.2 us (23%)
  between operations  15.1 us (8%)
  blocking collectives  13 us (7%)
  matrix products  10.8 us (5%)
  other arithmetic  5.29 us (3%)
  local copies, waits for them, and re-layouts  4.84 us (2%)
    all_gather x1, waiting for transfers between devices, local(): lax.all_gather(jnp.concatenate([w_query, w_key, w_value], axis=1), 'dp',...  45.6 us
    all_to_all x1, waiting for transfers between devices, local(): lax.all_to_all(pick(wanted, table).astype(jnp.bfloat16).reshape(peers, ca...  33.6 us
    all_to_all x1, starting transfers between devices, local(): lax.all_to_all(requests, 'dp', split_axis=0, concat_axis=0, tiled=True)  20.4 us
    all_to_all x1, waiting for transfers between devices, local(): lax.all_to_all(requests, 'dp', split_axis=0, concat_axis=0, tiled=True)  14.1 us
    all_gather x1, blocking collectives, local(): lax.all_gather(norm_gain, 'mp', axis=0, tiled=True).astype(jnp.float32)  13 us
    ppermute x3, starting transfers between devices, local(): lax.ppermute(joined, 'mp', [(i, (i + k) % parts) for i in range(parts)])  10.6 us
    all_to_all x1, starting transfers between devices, local(): lax.all_to_all(grad_buffer.reshape(peers, capacity, col_width), 'dp', spl...  9.53 us
    all_to_all x1, waiting for transfers between devices, local(): lax.all_to_all(grad_buffer.reshape(peers, capacity, col_width), 'dp', spl...  7.74 us
  transfers between devices with their start and end apart: 7, of which 4 were waited for; matrix products, arithmetic and copies ran while one was open for 6% of the time, Pallas kernels for 0%

profile of v1, /device:TPU:1, one launch (start us, length us, event | category | flops | bytes accessed | tf_op | source)
XLA Modules:
  0.0 196.3 jit_solution(1731019495664114980)
XLA Ops:
  7.2 0.0 copy-start
  7.2 0.0 all-gather.2.cloned.1.call-start
  7.2 1.5 pad_maximum_fusion.3
  8.7 0.0 all-gather.2.cloned.1.call-update
  8.7 0.9 convert_reduce_fusion
  9.6 0.7 multiply_add_fusion
  10.3 0.1 select_reduce_fusion
  10.4 0.8 sub.24
  11.2 20.4 %all-to-all-start = ((s32[128,1,2]{2,1,0:T(1,128)}), s32[128,1,2]{2,1,0:T(1,128)S(1)}, u32[]{:S(2)}, u32[]{:S(2)}) async-start(s32[128,1,2]{2,1,0:T(1,128)} %bitcast.4), calls=%async_computation | async-start | bytes 131072 | tf_op jit(solution)/shard_map/all_to_all | solution.py:78
  31.6 0.7 convert_element_type.55
  32.3 14.1 %all-to-all-done = s32[128,1,2]{2,1,0:T(1,128)S(1)} async-done(((s32[128,1,2]{2,1,0:T(1,128)}), s32[128,1,2]{2,1,0:T(1,128)S(1)}, u32[]{:S(2)}, u32[]{:S(2)}) %all-to-all-start) | async-done | bytes 1056 | tf_op jit(solution)/shard_map/all_to_all | solution.py:78
  46.4 0.5 broadcast.75
  47.0 0.8 reduce.3
  47.8 0.1 eq.74
  47.9 1.7 convolution_convert_fusion.1
  49.6 1.0 reshape.110
  50.6 5.7 %all-to-all-start.1 = ((bf16[128,2,1024]{2,1,0:T(2,128)(2,1)}), bf16[128,2,1024]{2,1,0:T(2,128)(2,1)S(1)}, u32[]{:S(2)}, u32[]{:S(2)}) async-start(bf16[128,2,1024]{2,1,0:T(2,128)(2,1)} %reshape.110), calls=%async_computation.1 | async-start | bytes 1048576 | tf_op jit(solution)/shard_map/all_to_all | solution.py:86
  56.3 0.0 copy-start.4
  56.3 0.3 convolution_convert_fusion.2
  56.6 0.0 copy-start.3
  56.6 33.6 %all-to-all-done.1 = bf16[128,2,1024]{2,1,0:T(2,128)(2,1)S(1)} async-done(((bf16[128,2,1024]{2,1,0:T(2,128)(2,1)}), bf16[128,2,1024]{2,1,0:T(2,128)(2,1)S(1)}, u32[]{:S(2)}, u32[]{:S(2)}) %all-to-all-start.1) | async-done | bytes 524320 | tf_op jit(solution)/shard_map/all_to_all | solution.py:86
  90.2 0.2 reshape.111
  90.4 1.0 reshape.115
  91.3 9.5 %all-to-all-start.2 = ((bf16[128,2,1024]{2,1,0:T(2,128)(2,1)}), bf16[128,2,1024]{2,1,0:T(2,128)(2,1)S(1)}, u32[]{:S(2)}, u32[]{:S(2)}) async-start(bf16[128,2,1024]{2,1,0:T(2,128)(2,1)} %reshape.115), calls=%async_computation.2 | async-start | bytes 1048576 | tf_op jit(solution)/shard_map/all_to_all | solution.py:96
  101.6 0.3 convolution_convert_fusion.3
  101.8 3.2 %collective-permute-start = (bf16[128,1024]{1,0:T(8,128)(2,1)S(1)}, bf16[128,1024]{1,0:T(8,128)(2,1)S(1)}, u32[]{:S(2)}, u32[]{:S(2)}) collective-permute-start(bf16[128,1024]{1,0:T(8,128)(2,1)S(1)} %convolution_convert_fusion.3), channel_id=1, source_target_pairs={{0,1},{1,2},{2,3},{3,0},{4,5},{5,6},{6,7},{7,4},{8,9},{9,10},{10,1... | collective-permute-start | bytes 786440 | tf_op jit(solution)/shard_map/ppermute | solution.py:109
  105.0 4.4 %collective-permute-start.1 = (bf16[128,1024]{1,0:T(8,128)(2,1)S(1)}, bf16[128,1024]{1,0:T(8,128)(2,1)S(1)}, u32[]{:S(2)}, u32[]{:S(2)}) collective-permute-start(bf16[128,1024]{1,0:T(8,128)(2,1)S(1)} %convolution_convert_fusion.3), channel_id=1, source_target_pairs={{0,2},{1,3},{2,0},{3,1},{4,6},{5,7},{6,4},{7,5},{8,10},{9,11},{10,... | collective-permute-start | bytes 786440 | tf_op jit(solution)/shard_map/ppermute | solution.py:109
  109.4 3.0 %collective-permute-start.2 = (bf16[128,1024]{1,0:T(8,128)(2,1)S(1)}, bf16[128,1024]{1,0:T(8,128)(2,1)S(1)}, u32[]{:S(2)}, u32[]{:S(2)}) collective-permute-start(bf16[128,1024]{1,0:T(8,128)(2,1)S(1)} %convolution_convert_fusion.3), channel_id=1, source_target_pairs={{0,3},{1,0},{2,1},{3,2},{4,7},{5,4},{6,5},{7,6},{8,11},{9,8},{10,9... | collective-permute-start | bytes 786440 | tf_op jit(solution)/shard_map/ppermute | solution.py:109
  112.5 13.0 %all_gather.6 = bf16[4096]{0:T(1024)(128)(2,1)S(1)} all-gather(bf16[1024]{0:T(1024)(128)(2,1)S(1)} %copy-done.3), channel_id=1, replica_groups=mesh['dp'=128,'mp'=4] {'mp'}, dimensions={0}, use_global_device_ids=true | all-gather | bytes 10240 | tf_op jit(solution)/shard_map/all_gather | solution.py:120
  125.6 0.1 fusion.27
  125.7 0.0 collective-permute-done
  125.7 0.0 collective-permute-done.1
  125.7 0.0 collective-permute-done.2
  125.7 0.1 pad_maximum_fusion
  125.9 0.0 copy-start.1
  125.9 0.0 copy-start.2
  125.9 0.1 dynamic-slice_bitcast_fusion.3
  126.0 0.3 fusion.1
  126.3 7.7 %all-to-all-done.2 = bf16[128,2,1024]{2,1,0:T(2,128)(2,1)S(1)} async-done(((bf16[128,2,1024]{2,1,0:T(2,128)(2,1)}), bf16[128,2,1024]{2,1,0:T(2,128)(2,1)S(1)}, u32[]{:S(2)}, u32[]{:S(2)}) %all-to-all-start.2) | async-done | bytes 524320 | tf_op jit(solution)/shard_map/all_to_all | solution.py:96
  134.0 0.2 reshape.116
  134.3 1.7 convert_multiply_fusion.4
  136.0 45.6 %all-gather.2.cloned.1.call-done = bf16[4096,1536]{1,0:T(8,128)(2,1)} async-done(((bf16[32,1536]{1,0:T(8,128)(2,1)}), bf16[4096,1536]{1,0:T(8,128)(2,1)}) %all-gather.2.cloned.1.call-update) | async-done | bytes 12582928 | tf_op jit(solution)/shard_map/all_gather | solution.py:66
  181.6 6.4 %convolution_convert_fusion = bf16[128,1536]{1,0:T(8,128)(2,1)S(1)} fusion(bf16[4096,1536]{1,0:T(8,128)(2,1)} %all-gather.2.cloned.1.call-done, f32[4096]{0:T(1024)S(1)} %convert_element_type.60, f32[128]{0:T(128)S(1)} %add_rsqrt_fusion, bf16[128,1024]{1,0:T(8,128)(2,1)S(1)} %get-tuple-element.22, bf16[128,1024]{1,0:T(8,128)(2,1)S(1)} %get-tuple-element.23, ...), kind=kOutput, calls=%fused_computation.3 | convolution fusion | flops 1616576512 | bytes 14041600 | tf_op jit(solution)/shard_map/dot_general | solution.py:123
  188.0 0.2 fusion.5
  188.2 0.1 fusion.31
  188.3 0.1 copy.38
  188.4 0.2 fusion.7
  188.7 0.8 copy.36
  (11 shorter events, 0.1 us)
Async XLA Ops:
  7.2 49.1 %copy-start = (bf16[128,1024]{1,0:T(8,128)(2,1)S(1)}, bf16[128,1024]{1,0:T(8,128)(2,1)}, u32[]{:S(2)}) copy-start(bf16[128,1024]{1,0:T(8,128)(2,1)} %param.23) | copy-start | bytes 786436
  7.2 174.4 %all-gather.2.cloned.1.call-start = ((), (), s32[]{:S(2)}) async-start(), calls=%async_computation.3 | async-start | bytes 12681216 | tf_op jit(solution)/shard_map/all_gather | solution.py:66
  11.2 35.2 %all-to-all-start = ((s32[128,1,2]{2,1,0:T(1,128)}), s32[128,1,2]{2,1,0:T(1,128)S(1)}, u32[]{:S(2)}, u32[]{:S(2)}) async-start(s32[128,1,2]{2,1,0:T(1,128)} %bitcast.4), calls=%async_computation | async-start | bytes 131072 | tf_op jit(solution)/shard_map/all_to_all | solution.py:78
  50.6 39.6 %all-to-all-start.1 = ((bf16[128,2,1024]{2,1,0:T(2,128)(2,1)}), bf16[128,2,1024]{2,1,0:T(2,128)(2,1)S(1)}, u32[]{:S(2)}, u32[]{:S(2)}) async-start(bf16[128,2,1024]{2,1,0:T(2,128)(2,1)} %reshape.110), calls=%async_computation.1 | async-start | bytes 1048576 | tf_op jit(solution)/shard_map/all_to_all | solution.py:86
  56.3 45.3 %copy-start.4 = (s32[128,1]{0,1:T(1,128)S(1)}, s32[128,1]{0,1:T(1,128)}, u32[]{:S(2)}) copy-start(s32[128,1]{0,1:T(1,128)} %param.13) | copy-start | bytes 1540
  56.6 56.0 %copy-start.3 = (bf16[1024]{0:T(1024)(128)(2,1)S(1)}, bf16[1024]{0:T(1024)(128)(2,1)}, u32[]{:S(2)}) copy-start(bf16[1024]{0:T(1024)(128)(2,1)} %param.19) | copy-start | bytes 6148
  91.3 42.7 %all-to-all-start.2 = ((bf16[128,2,1024]{2,1,0:T(2,128)(2,1)}), bf16[128,2,1024]{2,1,0:T(2,128)(2,1)S(1)}, u32[]{:S(2)}, u32[]{:S(2)}) async-start(bf16[128,2,1024]{2,1,0:T(2,128)(2,1)} %reshape.115), calls=%async_computation.2 | async-start | bytes 1048576 | tf_op jit(solution)/shard_map/all_to_all | solution.py:96
  101.8 23.9 %collective-permute-start = (bf16[128,1024]{1,0:T(8,128)(2,1)S(1)}, bf16[128,1024]{1,0:T(8,128)(2,1)S(1)}, u32[]{:S(2)}, u32[]{:S(2)}) collective-permute-start(bf16[128,1024]{1,0:T(8,128)(2,1)S(1)} %convolution_convert_fusion.3), channel_id=1, source_target_pairs={{0,1},{1,2},{2,3},{3,0},{4,5},{5,6},{6,7},{7,4},{8,9},{9,10},{10,1... | collective-permute-start | bytes 786440 | tf_op jit(solution)/shard_map/ppermute | solution.py:109
  105.0 20.7 %collective-permute-start.1 = (bf16[128,1024]{1,0:T(8,128)(2,1)S(1)}, bf16[128,1024]{1,0:T(8,128)(2,1)S(1)}, u32[]{:S(2)}, u32[]{:S(2)}) collective-permute-start(bf16[128,1024]{1,0:T(8,128)(2,1)S(1)} %convolution_convert_fusion.3), channel_id=1, source_target_pairs={{0,2},{1,3},{2,0},{3,1},{4,6},{5,7},{6,4},{7,5},{8,10},{9,11},{10,... | collective-permute-start | bytes 786440 | tf_op jit(solution)/shard_map/ppermute | solution.py:109
  109.4 16.3 %collective-permute-start.2 = (bf16[128,1024]{1,0:T(8,128)(2,1)S(1)}, bf16[128,1024]{1,0:T(8,128)(2,1)S(1)}, u32[]{:S(2)}, u32[]{:S(2)}) collective-permute-start(bf16[128,1024]{1,0:T(8,128)(2,1)S(1)} %convolution_convert_fusion.3), channel_id=1, source_target_pairs={{0,3},{1,0},{2,1},{3,2},{4,7},{5,4},{6,5},{7,6},{8,11},{9,8},{10,9... | collective-permute-start | bytes 786440 | tf_op jit(solution)/shard_map/ppermute | solution.py:109
  125.9 8.4 %copy-start.1 = (bf16[256,1024]{1,0:T(8,128)(2,1)S(1)}, bf16[256,1024]{1,0:T(8,128)(2,1)}, u32[]{:S(2)}) copy-start(bf16[256,1024]{1,0:T(8,128)(2,1)} %param.16) | copy-start | bytes 1572868
  125.9 8.4 %copy-start.2 = (bf16[256,1024]{1,0:T(8,128)(2,1)S(1)}, bf16[256,1024]{1,0:T(8,128)(2,1)}, u32[]{:S(2)}) copy-start(bf16[256,1024]{1,0:T(8,128)(2,1)} %param.15) | copy-start | bytes 1572868
Sparse Core Ops, SparseCore 0:
  11.7 169.7 all-gather.1

commit v2 on v1

v2 whole, which is shorter than its diff:
```python
import math

import jax
import jax.numpy as jnp
from jax import lax
from jax.experimental import pallas as pl
from jax.experimental.pallas import tpu as pltpu
from jax.sharding import Mesh
from jax.sharding import PartitionSpec as P

HD = 128
GAIN_ROWS = 8
DP = ("zh", "zl", "x", "c")


def one_hot(rows, columns):
    return (rows[:, None] == columns[None, :]).astype(jnp.bfloat16)


def pick(selector, values):
    return jnp.dot(selector, values, preferred_element_type=jnp.float32)


def select_kernel(slot_ref, replies_ref, gain_ref, out_ref):
    tok_count, slot_count = slot_ref.shape[0], replies_ref.shape[0]
    slots = lax.broadcasted_iota(jnp.int32, (tok_count, slot_count), 1)
    chosen = (slot_ref[...] == slots).astype(jnp.bfloat16)
    out_ref[:tok_count, :] = pick(chosen, replies_ref[...]).astype(jnp.bfloat16)
    out_ref[tok_count:, :] = jnp.broadcast_to(
        gain_ref[...], (out_ref.shape[0] - tok_count, gain_ref.shape[1])
    )


def select(slot_ids, replies, gain):
    tok_count, col_width = slot_ids.shape[0], replies.shape[1]
    return pl.pallas_call(
        select_kernel,
        out_shape=jax.ShapeDtypeStruct((tok_count + GAIN_ROWS, col_width), jnp.bfloat16),
        name="select",
    )(slot_ids.reshape(tok_count, 1), replies, gain.reshape(1, col_width))


def project_kernel(
    order_ref, length_ref, f0, f1, f2, f3, w_ref, out_ref, acc_ref, normed_ref
):
    step = pl.program_id(0)
    tok_count, width = out_ref.shape
    parts = (f0, f1, f2, f3)

    @pl.when(step == 0)
    def _():
        total = jnp.zeros((tok_count, 1), jnp.float32)
        for part in parts:
            value = part[:tok_count, :].astype(jnp.float32)
            total = total + jnp.sum(value * value, axis=1, keepdims=True)
        scale = lax.rsqrt(total / (len(parts) * f0.shape[1]) + 1e-06)
        for k, part in enumerate(parts):
            gain = part[tok_count : tok_count + 1, :].astype(jnp.float32)
            value = part[:tok_count, :].astype(jnp.float32)
            normed_ref[k] = (value * scale * gain).astype(jnp.bfloat16)

    weights = w_ref[...].reshape(normed_ref.shape[2], 3 * width)
    product = jnp.dot(normed_ref[step], weights, preferred_element_type=jnp.float32)

    @pl.when(step == 0)
    def _():
        acc_ref[...] = product

    @pl.when(step > 0)
    def _():
        acc_ref[...] += product

    @pl.when(step == pl.num_programs(0) - 1)
    def _():
        length = length_ref[0]
        row = lax.broadcasted_iota(jnp.int32, (tok_count, tok_count), 0)
        column = lax.broadcasted_iota(jnp.int32, (tok_count, tok_count), 1)
        allowed = (column <= row) & (column < length)
        live = lax.broadcasted_iota(jnp.int32, (tok_count, HD), 0) < length
        for at in range(0, width, HD):
            query, keys, values = (
                acc_ref[:, k * width + at : k * width + at + HD].astype(jnp.bfloat16)
                for k in range(3)
            )
            scores = lax.dot_general(
                query, keys, (((1,), (1,)), ((), ())), preferred_element_type=jnp.float32
            ) / math.sqrt(HD)
            scores = jnp.where(allowed, scores, jnp.float32(-1e30))
            powers = jnp.exp(scores - jnp.max(scores, axis=-1, keepdims=True))
            probs = (powers / jnp.sum(powers, axis=-1, keepdims=True)).astype(jnp.bfloat16)
            context = jnp.dot(probs, values, preferred_element_type=jnp.float32)
            out_ref[:, at : at + HD] = jnp.where(live, context, 0.0).astype(jnp.bfloat16)


def project_and_attend(order, session_length, turns, weights):
    rows, col_width = turns[0].shape
    tok_count = rows - GAIN_ROWS
    inner, quarters, depth, columns = weights.shape
    whole = pl.BlockSpec((rows, col_width), lambda s, order, length: (0, 0))
    return pl.pallas_call(
        project_kernel,
        out_shape=jax.ShapeDtypeStruct((tok_count, columns // 3), jnp.bfloat16),
        grid_spec=pltpu.PrefetchScalarGridSpec(
            num_scalar_prefetch=2,
            grid=(quarters,),
            in_specs=[whole] * 4
            + [
                pl.BlockSpec(
                    (inner, 1, depth, columns), lambda s, order, length: (0, order[s], 0, 0)
                )
            ],
            out_specs=pl.BlockSpec(
                (tok_count, columns // 3), lambda s, order, length: (0, 0)
            ),
            scratch_shapes=[
                pltpu.VMEM((tok_count, columns), jnp.float32),
                pltpu.VMEM((quarters, tok_count, col_width), jnp.bfloat16),
            ],
        ),
        compiler_params=pltpu.CompilerParams(vmem_limit_bytes=56 * 1024 * 1024),
        name="project_and_attend",
    )(order, session_length, *turns, weights)


def local(
    session_length,
    event_owner,
    event_row,
    text_rows,
    image_rows,
    price,
    price_dir,
    norm_gain,
    w_query,
    w_key,
    w_value,
    cotangent,
):
    peers = lax.axis_size(DP)
    parts = lax.axis_size("mp")
    mine = lax.axis_index("mp")
    tok_count = event_row.shape[0]
    capacity = 2 * tok_count // peers
    col_width = text_rows.shape[1]
    table_rows = text_rows.shape[0]
    slots = jnp.arange(peers * capacity, dtype=jnp.int32)

    quarter = lax.all_gather(
        jnp.concatenate([w_query, w_key, w_value], axis=1), "zh", axis=0, tiled=True
    )
    weights = lax.all_gather(quarter, ("zl", "x", "c"), axis=0, tiled=True).reshape(
        -1, lax.axis_size("zh"), *w_query.shape[:1], 3 * w_query.shape[1]
    )

    owner_ids = event_owner[:, 0]
    place = jnp.arange(tok_count, dtype=jnp.int32)
    same = (owner_ids[:, None] == owner_ids[None, :]) & (place[None, :] < place[:, None])
    slot_ids = owner_ids * capacity + jnp.sum(same.astype(jnp.int32), axis=1)
    taken = slots[:, None] == slot_ids[None, :]
    requests = (
        jnp.sum(jnp.where(taken, event_row[None, :] + 1, 0), axis=1) - 1
    ).reshape(peers, capacity)
    requests, _ = lax.optimization_barrier((requests, quarter))
    got_ids = lax.all_to_all(requests, DP, split_axis=0, concat_axis=0, tiled=True).reshape(-1)

    text_float = text_rows.astype(jnp.float32)
    image_float = image_rows.astype(jnp.float32)
    table = (
        text_float * image_float + price[:, None] * price_dir.astype(jnp.float32)[None, :]
    ).astype(jnp.bfloat16)
    wanted = one_hot(got_ids, jnp.arange(table_rows, dtype=jnp.int32))
    replies = lax.all_to_all(
        pick(wanted, table).astype(jnp.bfloat16).reshape(peers, capacity, col_width),
        DP,
        split_axis=0,
        concat_axis=0,
        tiled=True,
    ).reshape(peers * capacity, col_width)

    grad_buffer = pick(taken.astype(jnp.bfloat16), cotangent).astype(jnp.bfloat16)
    grad_buffer, replies = lax.optimization_barrier((grad_buffer, replies))
    got_grads = lax.all_to_all(
        grad_buffer.reshape(peers, capacity, col_width),
        DP,
        split_axis=0,
        concat_axis=0,
        tiled=True,
    ).reshape(peers * capacity, col_width)
    row_sums = pick(wanted.T, got_grads)
    text_grad = row_sums * image_float
    image_grad = row_sums * text_float

    joined = select(slot_ids, replies, norm_gain)
    turns = [
        joined if k == 0 else lax.ppermute(joined, "mp", [(i, (i + k) % parts) for i in range(parts)])
        for k in range(parts)
    ]
    order = (mine - jnp.arange(parts, dtype=jnp.int32)) % parts
    context = project_and_attend(order, session_length, turns, weights)
    return (context, text_grad, image_grad)


def solution(mesh):
    fine = Mesh(mesh.devices.reshape(4, -1, 4, 2, mesh.shape["mp"]), (*DP, "mp"))
    return jax.shard_map(
        local,
        mesh=fine,
        in_specs=(
            P(DP),
            P(DP, None),
            P(DP),
            P(DP, "mp"),
            P(DP, "mp"),
            P(DP),
            P("mp"),
            P("mp"),
            P(DP, "mp"),
            P(DP, "mp"),
            P(DP, "mp"),
            P(DP, "mp"),
        ),
        out_specs=(P(DP, "mp"), P(DP, "mp"), P(DP, "mp")),
        check_vma=False,
    )
```

time: 197 us -> 185 us (0.939)
  waiting for transfers between devices: 101 us -> 75.2 us
  blocking collectives: 13 us -> 28.1 us
  Pallas kernels: 0 us -> 11.8 us
  starting transfers between devices: 46.2 us -> 37.8 us
  matrix products: 10.8 us -> 4.91 us
    all_gather x1, waiting for transfers between devices: 45.6 us -> 1.09 us  [local(): lax.all_gather(quarter, ('zl', 'x', 'c'), axis=0, tiled=True)]
    all_gather x1, blocking collectives: 13 us -> 28.1 us  [local(): lax.all_gather(jnp.concatenate([w_query, w_key, w_value], axis=1), 'zh',...]
    all_to_all x2, waiting for transfers between devices: 21.9 us -> 36.7 us  [the longest x1 22.5 us: local(): lax.all_to_all(grad_buffer.reshape(peers, capacity, col_width), DP, split...]
    pallas_call x0 -> x2, Pallas kernels: none -> 11.8 us  [the longest x1 9.72 us: project_and_attend(): pl.pallas_call(project_kernel, out_shape=jax.ShapeDtypeStruct((tok_count,...]
    all_to_all x2, starting transfers between devices: 29.9 us -> 22.3 us  [the longest x1 14.6 us: local(): lax.all_to_all(requests, DP, split_axis=0, concat_axis=0, tiled=True)]
    dot_general x3 -> x0, matrix products: 6.85 us -> none  [the longest x1 6.41 us: local(): jnp.dot(normed, weights, preferred_element_type=jnp.float32)]
    all_to_all x1, waiting for transfers between devices: 33.6 us -> 37.4 us  [local(): lax.all_to_all(pick(wanted, table).astype(jnp.bfloat16).reshape(peers, ca...]
    dot_general x4 -> x3, matrix products: 3.94 us -> 4.91 us  [pick(): return jnp.dot(selector, values, preferred_element_type=jnp.float32)]
  transfers between devices with their start and end apart: 7 -> 7, of which waited for: 4 -> 4; matrix products, arithmetic and copies ran while one was open for 6% -> 9% of each run, Pallas kernels for 0% -> 1%
where the time goes in v2:
time: 185 us; the launch traced here: 184 us
  waiting for transfers between devices  75.2 us (41%)
  starting transfers between devices  37.8 us (20%)
  blocking collectives  28.1 us (15%)
  between operations  14.8 us (8%)
  Pallas kernels  11.8 us (6%)
  local copies, waits for them, and re-layouts  6.64 us (4%)
  other arithmetic  5.26 us (3%)
  matrix products  4.91 us (3%)
    all_to_all x1, waiting for transfers between devices, local(): lax.all_to_all(pick(wanted, table).astype(jnp.bfloat16).reshape(peers, ca...  37.4 us
    all_gather x1, blocking collectives, local(): lax.all_gather(jnp.concatenate([w_query, w_key, w_value], axis=1), 'zh',...  28.1 us
    all_to_all x1, waiting for transfers between devices, local(): lax.all_to_all(grad_buffer.reshape(peers, capacity, col_width), DP, split...  22.5 us
    all_to_all x1, starting transfers between devices, local(): lax.all_to_all(requests, DP, split_axis=0, concat_axis=0, tiled=True)  14.6 us
    all_to_all x1, waiting for transfers between devices, local(): lax.all_to_all(requests, DP, split_axis=0, concat_axis=0, tiled=True)  14.2 us
    pallas_call x1, Pallas kernels, project_and_attend(): pl.pallas_call(project_kernel, out_shape=jax.ShapeDtypeStruct((tok_count,...  9.72 us
    ppermute x3, starting transfers between devices, local(): lax.ppermute(joined, 'mp', [(i, (i + k) % parts) for i in range(parts)])  9.27 us
    all_to_all x1, starting transfers between devices, local(): lax.all_to_all(grad_buffer.reshape(peers, capacity, col_width), DP, split...  7.68 us
  transfers between devices with their start and end apart: 7, of which 4 were waited for; matrix products, arithmetic and copies ran while one was open for 9% of the time, Pallas kernels for 1%

profile of v2, /device:TPU:1, one launch (start us, length us, event | category | flops | bytes accessed | tf_op | source)
XLA Modules:
  0.0 184.5 jit_solution(16539014421042874472)
XLA Ops:
  7.2 0.0 copy-start
  7.2 0.0 all-gather.2.cloned.1.call-start
  7.2 0.8 pad_maximum_fusion
  8.1 28.1 %all_gather.6 = bf16[128,1536]{1,0:T(8,128)(2,1)} all-gather(bf16[32,1536]{1,0:T(8,128)(2,1)S(1)} %pad_maximum_fusion), channel_id=1, replica_groups=mesh['zh'=4,'zl'=4,'x'=4,'c'=2,'mp'=4] {'zh'}, dimensions={0}, use_global_device_ids=true | all-gather | bytes 491520 | tf_op jit(solution)/shard_map/all_gather | solution.py:148
  36.2 0.0 all-gather.2.cloned.1.call-update
  36.2 0.9 convert_reduce_fusion
  37.1 0.7 multiply_add_fusion
  37.8 0.1 select_reduce_fusion
  37.9 0.8 sub.15
  38.7 14.6 %all-to-all-start = ((s32[128,1,2]{2,1,0:T(1,128)}), s32[128,1,2]{2,1,0:T(1,128)S(1)}, u32[]{:S(2)}, u32[]{:S(2)}) async-start(s32[128,1,2]{2,1,0:T(1,128)} %bitcast.3), calls=%async_computation | async-start | bytes 131072 | tf_op jit(solution)/shard_map/all_to_all | solution.py:164
  53.3 0.7 convert_element_type.27
  54.0 14.2 %all-to-all-done = s32[128,1,2]{2,1,0:T(1,128)S(1)} async-done(((s32[128,1,2]{2,1,0:T(1,128)}), s32[128,1,2]{2,1,0:T(1,128)S(1)}, u32[]{:S(2)}, u32[]{:S(2)}) %all-to-all-start) | async-done | bytes 1056 | tf_op jit(solution)/shard_map/all_to_all | solution.py:164
  68.2 0.5 broadcast.28
  68.7 0.8 reduce.3
  69.5 0.1 eq.52
  69.7 1.7 convolution_convert_fusion
  71.4 1.0 reshape.47
  72.4 6.2 %all-to-all-start.1 = ((bf16[128,2,1024]{2,1,0:T(2,128)(2,1)}), bf16[128,2,1024]{2,1,0:T(2,128)(2,1)S(1)}, u32[]{:S(2)}, u32[]{:S(2)}) async-start(bf16[128,2,1024]{2,1,0:T(2,128)(2,1)} %reshape.47), calls=%async_computation.1 | async-start | bytes 1048576 | tf_op jit(solution)/shard_map/all_to_all | solution.py:172
  78.5 0.0 copy-done
  78.5 0.3 convolution_convert_fusion.1
  78.8 37.4 %all-to-all-done.1 = bf16[128,2,1024]{2,1,0:T(2,128)(2,1)S(1)} async-done(((bf16[128,2,1024]{2,1,0:T(2,128)(2,1)}), bf16[128,2,1024]{2,1,0:T(2,128)(2,1)S(1)}, u32[]{:S(2)}, u32[]{:S(2)}) %all-to-all-start.1) | async-done | bytes 524320 | tf_op jit(solution)/shard_map/all_to_all | solution.py:172
  116.2 1.0 reshape.48.replies_ref
  117.2 1.0 reshape.51
  118.2 7.7 %all-to-all-start.2 = ((bf16[128,2,1024]{2,1,0:T(2,128)(2,1)}), bf16[128,2,1024]{2,1,0:T(2,128)(2,1)S(1)}, u32[]{:S(2)}, u32[]{:S(2)}) async-start(bf16[128,2,1024]{2,1,0:T(2,128)(2,1)} %reshape.51), calls=%async_computation.2 | async-start | bytes 1048576 | tf_op jit(solution)/shard_map/all_to_all | solution.py:182
  126.6 1.3 reshape.49.gain_ref
  127.8 0.7 bitcast_add_fusion
  128.5 0.7 copy.30.slot_ref
  129.2 0.6 and_select_fusion.order_ref
  129.8 2.0 %select.3.f0 = bf16[136,1024]{1,0:T(8,128)(2,1)} custom-call(s32[128,1]{1,0:T(8,128)} %copy.30.slot_ref, bf16[256,1024]{1,0:T(8,128)(2,1)} %reshape.48.replies_ref, bf16[1,1024]{1,0:T(2,128)(2,1)} %reshape.49.gain_ref), custom_call_target="tpu_custom_call" | custom-call | tf_op jit(solution)/shard_map/select/pallas_call | solution.py:36
  131.9 4.3 %collective-permute-start.2 = (bf16[136,1024]{1,0:T(8,128)(2,1)}, bf16[136,1024]{1,0:T(8,128)(2,1)S(1)}, u32[]{:S(2)}, u32[]{:S(2)}) collective-permute-start(bf16[136,1024]{1,0:T(8,128)(2,1)} %select.3.f0), channel_id=1, source_target_pairs={{0,3},{1,0},{2,1},{3,2},{4,7},{5,4},{6,5},{7,6},{8,11},{9,8},{10,9... | collective-permute-start | bytes 835592 | tf_op jit(solution)/shard_map/ppermute | solution.py:195
  136.2 2.4 %collective-permute-start.1 = (bf16[136,1024]{1,0:T(8,128)(2,1)}, bf16[136,1024]{1,0:T(8,128)(2,1)S(1)}, u32[]{:S(2)}, u32[]{:S(2)}) collective-permute-start(bf16[136,1024]{1,0:T(8,128)(2,1)} %select.3.f0), channel_id=1, source_target_pairs={{0,2},{1,3},{2,0},{3,1},{4,6},{5,7},{6,4},{7,5},{8,10},{9,11},{10,... | collective-permute-start | bytes 835592 | tf_op jit(solution)/shard_map/ppermute | solution.py:195
  138.6 2.6 %collective-permute-start = (bf16[136,1024]{1,0:T(8,128)(2,1)}, bf16[136,1024]{1,0:T(8,128)(2,1)S(1)}, u32[]{:S(2)}, u32[]{:S(2)}) collective-permute-start(bf16[136,1024]{1,0:T(8,128)(2,1)} %select.3.f0), channel_id=1, source_target_pairs={{0,1},{1,2},{2,3},{3,0},{4,5},{5,6},{6,7},{7,4},{8,9},{9,10},{10,1... | collective-permute-start | bytes 835592 | tf_op jit(solution)/shard_map/ppermute | solution.py:195
  141.2 22.5 %all-to-all-done.2 = bf16[128,2,1024]{2,1,0:T(2,128)(2,1)S(1)} async-done(((bf16[128,2,1024]{2,1,0:T(2,128)(2,1)}), bf16[128,2,1024]{2,1,0:T(2,128)(2,1)S(1)}, u32[]{:S(2)}, u32[]{:S(2)}) %all-to-all-start.2) | async-done | bytes 524320 | tf_op jit(solution)/shard_map/all_to_all | solution.py:182
  163.6 0.2 reshape.52
  163.8 3.0 %convert_multiply_fusion.2 = (f32[256,1024]{1,0:T(8,128)}, f32[256,1024]{1,0:T(8,128)}) fusion(bf16[256,1024]{1,0:T(8,128)(2,1)} %param.15, bf16[256,1024]{1,0:T(8,128)(2,1)} %param.16, bf16[256,1024]{1,0:T(8,128)(2,1)S(1)} %reshape.52, s32[256]{0:T(256)S(1)} %eq.52), kind=kOutput, calls=%fused_computation.2 | convolution fusion | flops 135331840 | bytes 3671040 | tf_op jit(solution)/shard_map/dot_general | solution.py:21
  166.8 0.0 collective-permute-done.2.f3
  166.8 0.0 copy-start.1
  166.8 0.0 collective-permute-done.1.f2
  166.8 0.0 copy-start.2
  166.8 0.0 collective-permute-done.f1
  166.8 0.0 copy-start.3
  166.8 1.1 all-gather.2.cloned.1.call-done
  167.9 0.0 copy-done.1
  167.9 0.0 copy-done.2
  167.9 0.0 copy-done.3
  167.9 9.7 %project_and_attend.1 = bf16[128,512]{1,0:T(8,128)(2,1)} custom-call(s32[4]{0:T(128)} %and_select_fusion.order_ref, s32[1]{0:T(128)S(6)} %copy.31.length_ref, bf16[136,1024]{1,0:T(8,128)(2,1)} %select.3.f0, bf16[136,1024]{1,0:T(8,128)(2,1)} %copy-done.3, bf16[136,1024]{1,0:T(8,128)(2,1)} %copy-done.2, bf16[136,1024]{1,0:T(8,128)(2,1)} %copy-done.1, ...), custom_call_target="tpu_custom_call" | custom-call | tf_op jit(solution)/shard_map/project_and_attend/pallas_call | solution.py:100
  (1 shorter events, 0.0 us)
Async XLA Ops:
  7.2 71.4 %copy-start = (bf16[128,1024]{1,0:T(8,128)(2,1)S(1)}, bf16[128,1024]{1,0:T(8,128)(2,1)}, u32[]{:S(2)}) copy-start(bf16[128,1024]{1,0:T(8,128)(2,1)} %param.23) | copy-start | bytes 786436
  7.2 160.7 %all-gather.2.cloned.1.call-start = ((), (), s32[]{:S(2)}) async-start(), calls=%async_computation.3 | async-start | bytes 12976128 | tf_op jit(solution)/shard_map/all_gather | solution.py:151
  38.7 29.5 %all-to-all-start = ((s32[128,1,2]{2,1,0:T(1,128)}), s32[128,1,2]{2,1,0:T(1,128)S(1)}, u32[]{:S(2)}, u32[]{:S(2)}) async-start(s32[128,1,2]{2,1,0:T(1,128)} %bitcast.3), calls=%async_computation | async-start | bytes 131072 | tf_op jit(solution)/shard_map/all_to_all | solution.py:164
  72.4 43.9 %all-to-all-start.1 = ((bf16[128,2,1024]{2,1,0:T(2,128)(2,1)}), bf16[128,2,1024]{2,1,0:T(2,128)(2,1)S(1)}, u32[]{:S(2)}, u32[]{:S(2)}) async-start(bf16[128,2,1024]{2,1,0:T(2,128)(2,1)} %reshape.47), calls=%async_computation.1 | async-start | bytes 1048576 | tf_op jit(solution)/shard_map/all_to_all | solution.py:172
  118.2 45.4 %all-to-all-start.2 = ((bf16[128,2,1024]{2,1,0:T(2,128)(2,1)}), bf16[128,2,1024]{2,1,0:T(2,128)(2,1)S(1)}, u32[]{:S(2)}, u32[]{:S(2)}) async-start(bf16[128,2,1024]{2,1,0:T(2,128)(2,1)} %reshape.51), calls=%async_computation.2 | async-start | bytes 1048576 | tf_op jit(solution)/shard_map/all_to_all | solution.py:182
  131.9 34.9 %collective-permute-start.2 = (bf16[136,1024]{1,0:T(8,128)(2,1)}, bf16[136,1024]{1,0:T(8,128)(2,1)S(1)}, u32[]{:S(2)}, u32[]{:S(2)}) collective-permute-start(bf16[136,1024]{1,0:T(8,128)(2,1)} %select.3.f0), channel_id=1, source_target_pairs={{0,3},{1,0},{2,1},{3,2},{4,7},{5,4},{6,5},{7,6},{8,11},{9,8},{10,9... | collective-permute-start | bytes 835592 | tf_op jit(solution)/shard_map/ppermute | solution.py:195
  136.2 30.6 %collective-permute-start.1 = (bf16[136,1024]{1,0:T(8,128)(2,1)}, bf16[136,1024]{1,0:T(8,128)(2,1)S(1)}, u32[]{:S(2)}, u32[]{:S(2)}) collective-permute-start(bf16[136,1024]{1,0:T(8,128)(2,1)} %select.3.f0), channel_id=1, source_target_pairs={{0,2},{1,3},{2,0},{3,1},{4,6},{5,7},{6,4},{7,5},{8,10},{9,11},{10,... | collective-permute-start | bytes 835592 | tf_op jit(solution)/shard_map/ppermute | solution.py:195
  138.6 28.2 %collective-permute-start = (bf16[136,1024]{1,0:T(8,128)(2,1)}, bf16[136,1024]{1,0:T(8,128)(2,1)S(1)}, u32[]{:S(2)}, u32[]{:S(2)}) collective-permute-start(bf16[136,1024]{1,0:T(8,128)(2,1)} %select.3.f0), channel_id=1, source_target_pairs={{0,1},{1,2},{2,3},{3,0},{4,5},{5,6},{6,7},{7,4},{8,9},{9,10},{10,1... | collective-permute-start | bytes 835592 | tf_op jit(solution)/shard_map/ppermute | solution.py:195
  166.8 1.1 copy-start.1
  166.8 1.1 copy-start.2
  166.8 1.1 copy-start.3
Sparse Core Ops, SparseCore 0:
  36.3 131.5 all-gather.1

commit v3 on v2

v3 whole, which is shorter than its diff:
```python
import math

import jax
import jax.numpy as jnp
from jax import lax
from jax.experimental import pallas as pl
from jax.experimental.pallas import tpu as pltpu
from jax.sharding import Mesh
from jax.sharding import PartitionSpec as P

HD = 128
GAIN_ROWS = 8
XS = 4
CS = 2
DP = ("z", "x", "c")


def pick(selector, values):
    return jnp.dot(selector, values, preferred_element_type=jnp.float32)


def iota(shape, axis):
    return lax.broadcasted_iota(jnp.int32, shape, axis)


def answer_kernel(ids_ref, table_ref, out_ref):
    count, table_rows = ids_ref.shape[1], table_ref.shape[0]
    width = table_ref.shape[1] // XS
    group = 2 * XS * CS
    target = iota((count, count), 0)
    source = iota((count, count), 1)
    at = lax.rem(target, group)
    moved = (
        target - at + lax.rem(at // 2, XS) * (2 * CS) + (at // (2 * XS)) * 2 + lax.rem(at, 2)
    )
    ids = jnp.sum(
        jnp.where(moved == source, ids_ref[...].astype(jnp.float32), 0.0), axis=1, keepdims=True
    ).astype(jnp.int32)
    wanted = (ids == iota((count, table_rows), 1)).astype(jnp.bfloat16)
    for block in range(XS):
        rows = pick(wanted, table_ref[:, block * width : (block + 1) * width]).astype(
            jnp.bfloat16
        )
        for z in range(count // group):
            to = (z * XS + block) * group
            out_ref[to : to + group, :] = rows[z * group : (z + 1) * group, :]


def answer(ids, table):
    count, columns = ids.shape[0], table.shape[1]
    return pl.pallas_call(
        answer_kernel,
        out_shape=jax.ShapeDtypeStruct((count * XS, columns // XS), jnp.bfloat16),
        name="answer",
    )(ids.reshape(1, count), table)


def select_kernel(code_ref, replies_ref, gain_ref, out_ref):
    tokens = code_ref.shape[0]
    chosen = (code_ref[...] == iota((tokens, replies_ref.shape[0]), 1)).astype(jnp.bfloat16)
    out_ref[:tokens, :] = pick(chosen, replies_ref[...]).astype(jnp.bfloat16)
    out_ref[tokens:, :] = jnp.broadcast_to(gain_ref[...], (GAIN_ROWS, gain_ref.shape[1]))


def select(codes, replies, gain):
    tokens, width = codes.shape[0], replies.shape[1]
    return pl.pallas_call(
        select_kernel,
        out_shape=jax.ShapeDtypeStruct((tokens + GAIN_ROWS, width), jnp.bfloat16),
        name="select",
    )(codes.reshape(tokens, 1), replies, gain.reshape(1, width))


def project_kernel(order_ref, f0, f1, f2, f3, w_ref, own_ref, s1, s2, s3, acc_ref, normed_ref, sum_ref):
    step = pl.program_id(0)
    tokens = acc_ref.shape[0] // XS
    columns = acc_ref.shape[1]

    @pl.when(step == 0)
    def _():
        total = jnp.zeros((XS * tokens, 1), jnp.float32)
        for k, part in enumerate((f0, f1, f2, f3)):
            value = part[: XS * tokens, :].astype(jnp.float32)
            gain = part[XS * tokens : XS * tokens + 1, :].astype(jnp.float32)
            total = total + jnp.sum(value * value, axis=1, keepdims=True)
            normed_ref[k] = (value * gain).astype(jnp.bfloat16)
        sum_ref[...] = jnp.broadcast_to(total, sum_ref.shape)

    product = pick(normed_ref[step], w_ref[...])

    @pl.when(step == 0)
    def _():
        acc_ref[...] = product

    @pl.when(step > 0)
    def _():
        acc_ref[...] += product

    @pl.when(step == pl.num_programs(0) - 1)
    def _():
        mine = order_ref[XS]
        lane = iota((tokens, HD), 1)
        here = pl.ds(pl.multiple_of(mine * tokens, tokens), tokens)
        own_ref[:, :columns] = acc_ref[here, :]
        own_ref[:, columns:] = sum_ref[here, :]
        for k, out_ref in ((1, s1), (2, s2), (3, s3)):
            there = pl.ds(pl.multiple_of(lax.rem(mine + k, XS) * tokens, tokens), tokens)
            out_ref[:, :columns] = acc_ref[there, :].astype(jnp.bfloat16)
            total = sum_ref[there, :]
            high = total.astype(jnp.bfloat16).astype(jnp.float32)
            middle = (total - high).astype(jnp.bfloat16).astype(jnp.float32)
            low = total - high - middle
            out_ref[:, columns:] = jnp.where(
                lane == 0, high, jnp.where(lane == 1, middle, low)
            ).astype(jnp.bfloat16)


def project(order, turns, weights):
    rows, width = turns[0].shape
    tokens = (rows - GAIN_ROWS) // XS
    columns = weights.shape[1]
    whole = pl.BlockSpec((rows, width), lambda s, order: (0, 0))
    out = pl.BlockSpec((tokens, columns + HD), lambda s, order: (0, 0))
    return pl.pallas_call(
        project_kernel,
        out_shape=[jax.ShapeDtypeStruct((tokens, columns + HD), jnp.float32)]
        + [jax.ShapeDtypeStruct((tokens, columns + HD), jnp.bfloat16)] * 3,
        grid_spec=pltpu.PrefetchScalarGridSpec(
            num_scalar_prefetch=1,
            grid=(len(turns),),
            in_specs=[whole] * 4 + [pl.BlockSpec((width, columns), lambda s, order: (order[s], 0))],
            out_specs=[out] * 4,
            scratch_shapes=[
                pltpu.VMEM((XS * tokens, columns), jnp.float32),
                pltpu.VMEM((len(turns), XS * tokens, width), jnp.bfloat16),
                pltpu.VMEM((XS * tokens, HD), jnp.float32),
            ],
        ),
        compiler_params=pltpu.CompilerParams(vmem_limit_bytes=32 * 1024 * 1024),
        name="project",
    )(order, *turns, weights)


def attend_kernel(length_ref, own_ref, p1, p2, p3, out_ref):
    tokens, width = out_ref.shape
    columns = 3 * width
    total = own_ref[:, columns : columns + 1]
    for part in (p1, p2, p3):
        pieces = part[:, columns : columns + HD].astype(jnp.float32)
        total = total + ((pieces[:, 0:1] + pieces[:, 1:2]) + pieces[:, 2:3])
    scale = lax.rsqrt(total / (8 * width) + 1e-06)
    length = length_ref[0]
    row = iota((tokens, tokens), 0)
    column = iota((tokens, tokens), 1)
    allowed = (column <= row) & (column < length)
    live = iota((tokens, HD), 0) < length
    for at in range(0, width, HD):
        query, keys, values = (
            (
                (
                    own_ref[:, a : a + HD]
                    + p1[:, a : a + HD].astype(jnp.float32)
                    + p2[:, a : a + HD].astype(jnp.float32)
                    + p3[:, a : a + HD].astype(jnp.float32)
                )
                * scale
            ).astype(jnp.bfloat16)
            for a in (at, width + at, 2 * width + at)
        )
        scores = lax.dot_general(
            query, keys, (((1,), (1,)), ((), ())), preferred_element_type=jnp.float32
        ) / math.sqrt(HD)
        scores = jnp.where(allowed, scores, jnp.float32(-1e30))
        powers = jnp.exp(scores - jnp.max(scores, axis=-1, keepdims=True))
        probs = (powers / jnp.sum(powers, axis=-1, keepdims=True)).astype(jnp.bfloat16)
        context = pick(probs, values)
        out_ref[:, at : at + HD] = jnp.where(live, context, 0.0).astype(jnp.bfloat16)


def attend(session_length, own, parts):
    tokens, columns = own.shape
    vmem = pl.BlockSpec(memory_space=pltpu.VMEM)
    return pl.pallas_call(
        attend_kernel,
        out_shape=jax.ShapeDtypeStruct((tokens, (columns - HD) // 3), jnp.bfloat16),
        in_specs=[pl.BlockSpec(memory_space=pltpu.SMEM)] + [vmem] * 4,
        out_specs=vmem,
        name="attend",
    )(session_length, own, *parts)


def turn(value, axis, k):
    size = lax.axis_size(axis)
    return lax.ppermute(value, axis, [(i, (i + k) % size) for i in range(size)])


def exchange(value):
    return lax.all_to_all(value, DP, split_axis=0, concat_axis=0, tiled=True)


def local(
    session_length,
    event_owner,
    event_row,
    text_rows,
    image_rows,
    price,
    price_dir,
    norm_gain,
    w_query,
    w_key,
    w_value,
    cotangent,
):
    peers = lax.axis_size(DP)
    parts = lax.axis_size("mp")
    mine, across = lax.axis_index("mp"), lax.axis_index("x")
    tok_count = event_row.shape[0]
    capacity = 2 * tok_count // peers
    table_rows, col_width = text_rows.shape
    slots = jnp.arange(peers * capacity, dtype=jnp.int32)
    block = CS * w_query.shape[0]

    weights = lax.all_gather(
        jnp.concatenate([w_query, w_key, w_value], axis=1), ("z", "c"), axis=0, tiled=True
    )

    owner_ids = event_owner[:, 0]
    place = jnp.arange(tok_count, dtype=jnp.int32)
    same = (owner_ids[:, None] == owner_ids[None, :]) & (place[None, :] < place[:, None])
    earlier = jnp.sum(same.astype(jnp.int32), axis=1)
    slot_ids = owner_ids * capacity + earlier
    taken = slots[:, None] == slot_ids[None, :]
    requests = (
        jnp.sum(jnp.where(taken, event_row[None, :] + 1, 0), axis=1) - 1
    ).reshape(peers, capacity)
    got_ids = exchange(requests).reshape(-1)

    codes = lax.all_gather(owner_ids * (XS * capacity) + earlier, "x", axis=0)
    codes = (codes + capacity * jnp.arange(XS, dtype=jnp.int32)[:, None]).reshape(-1)

    text_float = text_rows.astype(jnp.float32)
    image_float = image_rows.astype(jnp.float32)
    table = (
        text_float * image_float + price[:, None] * price_dir.astype(jnp.float32)[None, :]
    ).astype(jnp.bfloat16)
    table = (
        table.reshape(table_rows, -1, XS, block).transpose(0, 2, 1, 3).reshape(table_rows, col_width)
    )
    got_ids, table, codes = lax.optimization_barrier((got_ids, table, codes))
    replies = exchange(
        answer(got_ids, table).reshape(peers, XS * capacity, col_width // XS)
    ).reshape(peers * XS * capacity, col_width // XS)

    grad_buffer = pick(taken.astype(jnp.bfloat16), cotangent).astype(jnp.bfloat16)
    grad_buffer, replies = lax.optimization_barrier((grad_buffer, replies))
    got_grads = exchange(grad_buffer.reshape(peers, capacity, col_width)).reshape(
        peers * capacity, col_width
    )
    wanted = (jnp.arange(table_rows, dtype=jnp.int32)[:, None] == got_ids[None, :]).astype(
        jnp.bfloat16
    )
    row_sums = pick(wanted, got_grads)
    text_grad = row_sums * image_float
    image_grad = row_sums * text_float

    gain = lax.dynamic_index_in_dim(
        norm_gain.reshape(-1, XS, block), across, 1, keepdims=False
    ).reshape(-1)
    joined = select(codes, replies, gain)
    turns = [joined] + [turn(joined, "mp", k) for k in range(1, parts)]
    order = jnp.concatenate(
        [(mine - jnp.arange(parts, dtype=jnp.int32)) % parts, across[None]]
    ).astype(jnp.int32)
    own, *sends = project(order, turns, weights)
    context = attend(
        session_length, own, [turn(part, "x", k) for k, part in enumerate(sends, 1)]
    )
    return (context, text_grad, image_grad)


def solution(mesh):
    fine = Mesh(mesh.devices.reshape(-1, XS, CS, mesh.shape["mp"]), (*DP, "mp"))
    return jax.shard_map(
        local,
        mesh=fine,
        in_specs=(
            P(DP),
            P(DP, None),
            P(DP),
            P(DP, "mp"),
            P(DP, "mp"),
            P(DP),
            P("mp"),
            P("mp"),
            P(DP, "mp"),
            P(DP, "mp"),
            P(DP, "mp"),
            P(DP, "mp"),
        ),
        out_specs=(P(DP, "mp"), P(DP, "mp"), P(DP, "mp")),
        check_vma=False,
    )
```

time: 185 us -> 181 us (0.978)
  the two profiles are of different devices: /device:TPU:1 before, /device:TPU:11 now
where the time goes in v3:
time: 181 us; the launch traced here: 180 us
  waiting for transfers between devices  66.3 us (37%)
  starting transfers between devices  59.3 us (33%)
  between operations  14.9 us (8%)
  Pallas kernels  13 us (7%)
  local copies, waits for them, and re-layouts  9.83 us (5%)
  other arithmetic  7.55 us (4%)
  blocking collectives  6.53 us (4%)
  matrix products  2.96 us (2%)
    all_to_all x3, waiting for transfers between devices, exchange(): return lax.all_to_all(value, DP, split_axis=0, concat_axis=0, tiled=True)  41.1 us
    all_to_all x3, starting transfers between devices, exchange(): return lax.all_to_all(value, DP, split_axis=0, concat_axis=0, tiled=True)  39.8 us
    ppermute x6, waiting for transfers between devices, turn(): return lax.ppermute(value, axis, [(i, (i + k) % size) for i in range(size)])  25.2 us
    ppermute x6, starting transfers between devices, turn(): return lax.ppermute(value, axis, [(i, (i + k) % size) for i in range(size)])  19.4 us
    all_gather x1, blocking collectives, local(): codes = lax.all_gather(owner_ids * (XS * capacity) + earlier, 'x', axis=0)  6.53 us
    pallas_call x1, Pallas kernels, project(): pl.pallas_call(project_kernel, out_shape=[jax.ShapeDtypeStruct((tokens, c...  4.54 us
    unnamed x16, local copies, waits for them, and re-layouts  3.78 us
    pallas_call x1, Pallas kernels, attend(): pl.pallas_call(attend_kernel, out_shape=jax.ShapeDtypeStruct((tokens, (co...  3.76 us
  transfers between devices with their start and end apart: 10, of which 6 were waited for; matrix products, arithmetic and copies ran while one was open for 8% of the time, Pallas kernels for 5%

profile of v3, /device:TPU:11, one launch (start us, length us, event | category | flops | bytes accessed | tf_op | source)
XLA Modules:
  0.0 180.4 jit_solution(14455151596460815853)
XLA Ops:
  7.2 0.0 all-gather.3.cloned.1.call-start
  7.2 1.5 pad_maximum_fusion
  8.7 0.0 all-gather.3.cloned.1.call-update
  8.7 0.9 convert_reduce_fusion
  9.6 0.7 broadcast_add_fusion.1
  10.3 0.7 multiply_add_fusion
  11.0 0.1 select_reduce_fusion
  11.1 0.8 sub.15
  11.9 19.7 %all-to-all-start = ((s32[128,1,2]{2,1,0:T(1,128)}), s32[128,1,2]{2,1,0:T(1,128)S(1)}, u32[]{:S(2)}, u32[]{:S(2)}) async-start(s32[128,1,2]{2,1,0:T(1,128)} %bitcast.2), calls=%async_computation | async-start | bytes 131072 | tf_op jit(solution)/shard_map/all_to_all | solution.py:198
  31.6 0.7 convert_element_type.23
  32.3 0.7 fusion.7
  32.9 6.5 %all-gather = s32[4,1,128]{2,1,0:T(1,128)S(1)} all-gather(s32[1,1,128]{2,1,0:T(1,128)S(1)} %fusion.7), channel_id=1, replica_groups=mesh['z'=16,'x'=4,'c'=2,'mp'=4] {'x'}, dimensions={0}, use_global_device_ids=true | all-gather | bytes 2560 | tf_op jit(solution)/shard_map/all_gather | solution.py:239
  39.5 1.4 fusion.1
  40.9 0.1 add_bitcast_fusion
  41.0 0.2 copy.30
  41.2 4.5 %all-to-all-done = s32[128,1,2]{2,1,0:T(1,128)S(1)} async-done(((s32[128,1,2]{2,1,0:T(1,128)}), s32[128,1,2]{2,1,0:T(1,128)S(1)}, u32[]{:S(2)}, u32[]{:S(2)}) %all-to-all-start) | async-done | bytes 1056 | tf_op jit(solution)/shard_map/all_to_all | solution.py:198
  45.7 0.5 broadcast.55
  46.2 0.8 reduce.5
  47.1 0.7 reshape.95
  47.8 1.0 copy.32.table_ref
  48.8 2.2 %answer.1 = bf16[1024,256]{1,0:T(8,128)(2,1)} custom-call(s32[1,256]{1,0:T(1,128)} %bitcast.29, bf16[256,1024]{1,0:T(8,128)(2,1)} %copy.32.table_ref), custom_call_target="tpu_custom_call" | custom-call | tf_op jit(solution)/shard_map/answer/pallas_call | solution.py:51
  51.0 12.6 %all-to-all-start.1 = ((bf16[128,8,256]{2,1,0:T(8,128)(2,1)}), bf16[128,8,256]{2,1,0:T(8,128)(2,1)S(1)}, u32[]{:S(2)}, u32[]{:S(2)}) async-start(bf16[128,8,256]{2,1,0:T(8,128)(2,1)} %bitcast.26), calls=%async_computation.1 | async-start | bytes 1048576 | tf_op jit(solution)/shard_map/all_to_all | solution.py:198
  63.6 0.3 convolution_convert_fusion
  63.9 36.6 %all-to-all-done.1 = bf16[128,8,256]{2,1,0:T(8,128)(2,1)S(1)} async-done(((bf16[128,8,256]{2,1,0:T(8,128)(2,1)}), bf16[128,8,256]{2,1,0:T(8,128)(2,1)S(1)}, u32[]{:S(2)}, u32[]{:S(2)}) %all-to-all-start.1) | async-done | bytes 524320 | tf_op jit(solution)/shard_map/all_to_all | solution.py:198
  100.5 1.0 reshape.104
  101.5 7.5 %all-to-all-start.2 = ((bf16[128,2,1024]{2,1,0:T(2,128)(2,1)}), bf16[128,2,1024]{2,1,0:T(2,128)(2,1)S(1)}, u32[]{:S(2)}, u32[]{:S(2)}) async-start(bf16[128,2,1024]{2,1,0:T(2,128)(2,1)} %reshape.104), calls=%async_computation.2 | async-start | bytes 1048576 | tf_op jit(solution)/shard_map/all_to_all | solution.py:198
  109.0 0.1 reshape.103
  109.1 0.7 reshape_reshape.3.gain_ref
  109.8 0.9 copy.33.code_ref
  110.7 2.5 %select.3.f0 = bf16[520,256]{1,0:T(8,128)(2,1)} custom-call(s32[512,1]{1,0:T(8,128)} %copy.33.code_ref, bf16[1024,256]{1,0:T(8,128)(2,1)} %bitcast.25, bf16[1,256]{1,0:T(2,128)(2,1)} %reshape_reshape.3.gain_ref), custom_call_target="tpu_custom_call" | custom-call | tf_op jit(solution)/shard_map/select/pallas_call | solution.py:67
  113.1 3.2 %collective-permute-start = (bf16[520,256]{1,0:T(8,128)(2,1)}, bf16[520,256]{1,0:T(8,128)(2,1)S(1)}, u32[]{:S(2)}, u32[]{:S(2)}) collective-permute-start(bf16[520,256]{1,0:T(8,128)(2,1)} %select.3.f0), channel_id=1, source_target_pairs={{0,1},{1,2},{2,3},{3,0},{4,5},{5,6},{6,7},{7,4},{8,9},{9,10},{10,1... | collective-permute-start | bytes 798728 | tf_op jit(solution)/shard_map/ppermute | solution.py:194
  116.4 2.9 %collective-permute-start.1 = (bf16[520,256]{1,0:T(8,128)(2,1)}, bf16[520,256]{1,0:T(8,128)(2,1)S(1)}, u32[]{:S(2)}, u32[]{:S(2)}) collective-permute-start(bf16[520,256]{1,0:T(8,128)(2,1)} %select.3.f0), channel_id=1, source_target_pairs={{0,2},{1,3},{2,0},{3,1},{4,6},{5,7},{6,4},{7,5},{8,10},{9,11},{10,... | collective-permute-start | bytes 798728 | tf_op jit(solution)/shard_map/ppermute | solution.py:194
  119.2 3.7 %collective-permute-start.2 = (bf16[520,256]{1,0:T(8,128)(2,1)}, bf16[520,256]{1,0:T(8,128)(2,1)S(1)}, u32[]{:S(2)}, u32[]{:S(2)}) collective-permute-start(bf16[520,256]{1,0:T(8,128)(2,1)} %select.3.f0), channel_id=1, source_target_pairs={{0,3},{1,0},{2,1},{3,2},{4,7},{5,4},{6,5},{7,6},{8,11},{9,8},{10,9... | collective-permute-start | bytes 798728 | tf_op jit(solution)/shard_map/ppermute | solution.py:194
  123.0 0.1 pad_add_fusion.order_ref
  123.1 4.3 %collective-permute-done.1.f2 = bf16[520,256]{1,0:T(8,128)(2,1)S(1)} collective-permute-done((bf16[520,256]{1,0:T(8,128)(2,1)}, bf16[520,256]{1,0:T(8,128)(2,1)S(1)}, u32[]{:S(2)}, u32[]{:S(2)}) %collective-permute-start.1) | collective-permute-done | bytes 266272 | tf_op jit(solution)/shard_map/ppermute | solution.py:194
  127.3 6.7 %collective-permute-done.2.f3 = bf16[520,256]{1,0:T(8,128)(2,1)S(1)} collective-permute-done((bf16[520,256]{1,0:T(8,128)(2,1)}, bf16[520,256]{1,0:T(8,128)(2,1)S(1)}, u32[]{:S(2)}, u32[]{:S(2)}) %collective-permute-start.2) | collective-permute-done | bytes 266272 | tf_op jit(solution)/shard_map/ppermute | solution.py:194
  134.0 1.9 %copy-done.1 = bf16[1024,1536]{1,0:T(8,128)(2,1)S(1)} copy-done((bf16[1024,1536]{1,0:T(8,128)(2,1)S(1)}, bf16[1024,1536]{1,0:T(8,128)(2,1)}, u32[]{:S(2)}) %copy-start.1) | copy-done | bytes 3145752
  135.9 0.9 copy-done.2
  136.9 4.5 %project.1 = (f32[128,1664]{1,0:T(8,128)S(1)}, bf16[128,1664]{1,0:T(8,128)(2,1)S(1)}, bf16[128,1664]{1,0:T(8,128)(2,1)S(1)}, bf16[128,1664]{1,0:T(8,128)(2,1)S(1)}) custom-call(s32[5]{0:T(128)S(1)} %pad_add_fusion.order_ref, bf16[520,256]{1,0:T(8,128)(2,1)S(1)} %copy-done.2, bf16[520,256]{1,0:T(8,128)(2,1)S(1)} %collective-permute-done.f1, ...), custom_call_target="tpu_custom_call" | custom-call | tf_op jit(solution)/shard_map/project/pallas_call | solution.py:124
  141.4 0.9 copy-done.3
  142.3 3.1 %collective-permute-start.3 = (bf16[128,1664]{1,0:T(8,128)(2,1)S(1)}, bf16[128,1664]{1,0:T(8,128)(2,1)}, u32[]{:S(2)}, u32[]{:S(2)}) collective-permute-start(bf16[128,1664]{1,0:T(8,128)(2,1)S(1)} %get-tuple-element.17), channel_id=1, source_target_pairs={{0,8},{8,16},{16,24},{24,0},{1,9},{9,17},{17,25},{25,1},{2,10},{10... | collective-permute-start | bytes 1277960 | tf_op jit(solution)/shard_map/ppermute | solution.py:194
  145.4 2.6 %collective-permute-start.4 = (bf16[128,1664]{1,0:T(8,128)(2,1)S(1)}, bf16[128,1664]{1,0:T(8,128)(2,1)}, u32[]{:S(2)}, u32[]{:S(2)}) collective-permute-start(bf16[128,1664]{1,0:T(8,128)(2,1)S(1)} %get-tuple-element.18), channel_id=1, source_target_pairs={{0,16},{8,24},{16,0},{24,8},{1,17},{9,25},{17,1},{25,9},{2,18},{10... | collective-permute-start | bytes 1277960 | tf_op jit(solution)/shard_map/ppermute | solution.py:194
  148.0 3.9 %collective-permute-start.5 = (bf16[128,1664]{1,0:T(8,128)(2,1)S(1)}, bf16[128,1664]{1,0:T(8,128)(2,1)}, u32[]{:S(2)}, u32[]{:S(2)}) collective-permute-start(bf16[128,1664]{1,0:T(8,128)(2,1)S(1)} %get-tuple-element.19), channel_id=1, source_target_pairs={{0,24},{8,0},{16,8},{24,16},{1,25},{9,1},{17,9},{25,17},{2,26},{10... | collective-permute-start | bytes 1277960 | tf_op jit(solution)/shard_map/ppermute | solution.py:194
  152.6 0.2 reshape.105
  152.8 2.7 %convert_multiply_fusion.2 = (f32[256,1024]{1,0:T(8,128)}, f32[256,1024]{1,0:T(8,128)}) fusion(bf16[256,1024]{1,0:T(8,128)(2,1)} %param.15, bf16[256,1024]{1,0:T(8,128)(2,1)S(1)} %copy-done.5, bf16[256,1024]{1,0:T(8,128)(2,1)S(1)} %reshape.105, s32[256]{0:T(256)S(1)} %copy-done.6), kind=kOutput, calls=%fused_computation.2 | convolution fusion | flops 135331840 | bytes 3671040 | tf_op jit(solution)/shard_map/dot_general | solution.py:19
  155.5 4.0 %collective-permute-done.4.p2 = bf16[128,1664]{1,0:T(8,128)(2,1)} collective-permute-done((bf16[128,1664]{1,0:T(8,128)(2,1)S(1)}, bf16[128,1664]{1,0:T(8,128)(2,1)}, u32[]{:S(2)}, u32[]{:S(2)}) %collective-permute-start.4) | collective-permute-done | bytes 426016 | tf_op jit(solution)/shard_map/ppermute | solution.py:194
  159.5 10.3 %collective-permute-done.5.p3 = bf16[128,1664]{1,0:T(8,128)(2,1)} collective-permute-done((bf16[128,1664]{1,0:T(8,128)(2,1)S(1)}, bf16[128,1664]{1,0:T(8,128)(2,1)}, u32[]{:S(2)}, u32[]{:S(2)}) %collective-permute-start.5) | collective-permute-done | bytes 426016 | tf_op jit(solution)/shard_map/ppermute | solution.py:194
  169.8 3.8 %attend.1 = bf16[128,512]{1,0:T(8,128)(2,1)} custom-call(s32[1]{0:T(128)S(6)} %copy.34.length_ref, f32[128,1664]{1,0:T(8,128)} %copy-done.3, bf16[128,1664]{1,0:T(8,128)(2,1)} %collective-permute-done.3.p1, bf16[128,1664]{1,0:T(8,128)(2,1)} %collective-permute-done.4.p2, bf16[128,1664]{1,0:T(8,128)(2,1)} %collective-permute-done.5.p3), custom_call_target="tpu_custom_call" | custom-call | tf_op jit(solution)/shard_map/attend/pallas_call | solution.py:183
  (22 shorter events, 0.1 us)
Async XLA Ops:
  7.2 56.4 %copy-start = (bf16[128,1024]{1,0:T(8,128)(2,1)S(1)}, bf16[128,1024]{1,0:T(8,128)(2,1)}, u32[]{:S(2)}) copy-start(bf16[128,1024]{1,0:T(8,128)(2,1)} %param.23) | copy-start | bytes 786436
  7.2 126.8 %all-gather.3.cloned.1.call-start = ((), (), s32[]{:S(2)}) async-start(), calls=%async_computation.3 | async-start | bytes 3244032 | tf_op jit(solution)/shard_map/all_gather | solution.py:224
  11.9 33.9 %all-to-all-start = ((s32[128,1,2]{2,1,0:T(1,128)}), s32[128,1,2]{2,1,0:T(1,128)S(1)}, u32[]{:S(2)}, u32[]{:S(2)}) async-start(s32[128,1,2]{2,1,0:T(1,128)} %bitcast.2), calls=%async_computation | async-start | bytes 131072 | tf_op jit(solution)/shard_map/all_to_all | solution.py:198
  41.2 67.8 %copy-start.7 = (bf16[1024]{0:T(1024)(128)(2,1)S(1)}, bf16[1024]{0:T(1024)(128)(2,1)}, u32[]{:S(2)}) copy-start(bf16[1024]{0:T(1024)(128)(2,1)} %param.19) | copy-start | bytes 6148
  51.0 49.4 %all-to-all-start.1 = ((bf16[128,8,256]{2,1,0:T(8,128)(2,1)}), bf16[128,8,256]{2,1,0:T(8,128)(2,1)S(1)}, u32[]{:S(2)}, u32[]{:S(2)}) async-start(bf16[128,8,256]{2,1,0:T(8,128)(2,1)} %bitcast.26), calls=%async_computation.1 | async-start | bytes 1048576 | tf_op jit(solution)/shard_map/all_to_all | solution.py:198
  100.5 10.2 %copy-start.4 = (bf16[128,8,256]{2,1,0:T(8,128)(2,1)}, bf16[128,8,256]{2,1,0:T(8,128)(2,1)S(1)}, u32[]{:S(2)}) copy-start(bf16[128,8,256]{2,1,0:T(8,128)(2,1)S(1)} %all-to-all-done.1) | copy-start | bytes 1572868
  101.5 51.1 %all-to-all-start.2 = ((bf16[128,2,1024]{2,1,0:T(2,128)(2,1)}), bf16[128,2,1024]{2,1,0:T(2,128)(2,1)S(1)}, u32[]{:S(2)}, u32[]{:S(2)}) async-start(bf16[128,2,1024]{2,1,0:T(2,128)(2,1)} %reshape.104), calls=%async_computation.2 | async-start | bytes 1048576 | tf_op jit(solution)/shard_map/all_to_all | solution.py:198
  110.6 42.1 %copy-start.5 = (bf16[256,1024]{1,0:T(8,128)(2,1)S(1)}, bf16[256,1024]{1,0:T(8,128)(2,1)}, u32[]{:S(2)}) copy-start(bf16[256,1024]{1,0:T(8,128)(2,1)} %param.16) | copy-start | bytes 1572868
  110.7 42.1 %copy-start.6 = (s32[256]{0:T(256)S(1)}, s32[256]{0:T(256)}, u32[]{:S(2)}) copy-start(s32[256]{0:T(256)} %reshape.95) | copy-start | bytes 3076
  113.1 9.9 %collective-permute-start = (bf16[520,256]{1,0:T(8,128)(2,1)}, bf16[520,256]{1,0:T(8,128)(2,1)S(1)}, u32[]{:S(2)}, u32[]{:S(2)}) collective-permute-start(bf16[520,256]{1,0:T(8,128)(2,1)} %select.3.f0), channel_id=1, source_target_pairs={{0,1},{1,2},{2,3},{3,0},{4,5},{5,6},{6,7},{7,4},{8,9},{9,10},{10,1... | collective-permute-start | bytes 798728 | tf_op jit(solution)/shard_map/ppermute | solution.py:194
  116.4 11.0 %collective-permute-start.1 = (bf16[520,256]{1,0:T(8,128)(2,1)}, bf16[520,256]{1,0:T(8,128)(2,1)S(1)}, u32[]{:S(2)}, u32[]{:S(2)}) collective-permute-start(bf16[520,256]{1,0:T(8,128)(2,1)} %select.3.f0), channel_id=1, source_target_pairs={{0,2},{1,3},{2,0},{3,1},{4,6},{5,7},{6,4},{7,5},{8,10},{9,11},{10,... | collective-permute-start | bytes 798728 | tf_op jit(solution)/shard_map/ppermute | solution.py:194
  119.2 14.8 %collective-permute-start.2 = (bf16[520,256]{1,0:T(8,128)(2,1)}, bf16[520,256]{1,0:T(8,128)(2,1)S(1)}, u32[]{:S(2)}, u32[]{:S(2)}) collective-permute-start(bf16[520,256]{1,0:T(8,128)(2,1)} %select.3.f0), channel_id=1, source_target_pairs={{0,3},{1,0},{2,1},{3,2},{4,7},{5,4},{6,5},{7,6},{8,11},{9,8},{10,9... | collective-permute-start | bytes 798728 | tf_op jit(solution)/shard_map/ppermute | solution.py:194
  134.0 1.9 %copy-start.1 = (bf16[1024,1536]{1,0:T(8,128)(2,1)S(1)}, bf16[1024,1536]{1,0:T(8,128)(2,1)}, u32[]{:S(2)}) copy-start(bf16[1024,1536]{1,0:T(8,128)(2,1)} %all-gather.3.cloned.1.call-done.w_ref) | copy-start | bytes 9437188
  135.9 1.0 copy-start.2
  141.4 0.9 copy-start.3
  142.3 13.2 %collective-permute-start.3 = (bf16[128,1664]{1,0:T(8,128)(2,1)S(1)}, bf16[128,1664]{1,0:T(8,128)(2,1)}, u32[]{:S(2)}, u32[]{:S(2)}) collective-permute-start(bf16[128,1664]{1,0:T(8,128)(2,1)S(1)} %get-tuple-element.17), channel_id=1, source_target_pairs={{0,8},{8,16},{16,24},{24,0},{1,9},{9,17},{17,25},{25,1},{2,10},{10... | collective-permute-start | bytes 1277960 | tf_op jit(solution)/shard_map/ppermute | solution.py:194
  145.4 14.1 %collective-permute-start.4 = (bf16[128,1664]{1,0:T(8,128)(2,1)S(1)}, bf16[128,1664]{1,0:T(8,128)(2,1)}, u32[]{:S(2)}, u32[]{:S(2)}) collective-permute-start(bf16[128,1664]{1,0:T(8,128)(2,1)S(1)} %get-tuple-element.18), channel_id=1, source_target_pairs={{0,16},{8,24},{16,0},{24,8},{1,17},{9,25},{17,1},{25,9},{2,18},{10... | collective-permute-start | bytes 1277960 | tf_op jit(solution)/shard_map/ppermute | solution.py:194
  148.0 21.8 %collective-permute-start.5 = (bf16[128,1664]{1,0:T(8,128)(2,1)S(1)}, bf16[128,1664]{1,0:T(8,128)(2,1)}, u32[]{:S(2)}, u32[]{:S(2)}) collective-permute-start(bf16[128,1664]{1,0:T(8,128)(2,1)S(1)} %get-tuple-element.19), channel_id=1, source_target_pairs={{0,24},{8,0},{16,8},{24,16},{1,25},{9,1},{17,9},{25,17},{2,26},{10... | collective-permute-start | bytes 1277960 | tf_op jit(solution)/shard_map/ppermute | solution.py:194
Sparse Core Ops, SparseCore 0:
  10.7 89.7 all-gather.2

commit v4 on v3

v4 whole, which is shorter than its diff:
```python
import math

import jax
import jax.numpy as jnp
from jax import lax
from jax.experimental import pallas as pl
from jax.experimental.pallas import tpu as pltpu
from jax.sharding import Mesh
from jax.sharding import PartitionSpec as P

HD = 128
GAIN_ROWS = 8
VMEM_BYTES = 24 * 1024 * 1024
XS = 4
CS = 2
DP = ("z", "x", "c")


def pick(selector, values):
    return jnp.dot(selector, values, preferred_element_type=jnp.float32)


def iota(shape, axis):
    return lax.broadcasted_iota(jnp.int32, shape, axis)


def turned(row):
    count = row.shape[1]
    diagonal = iota((count, count), 0) == iota((count, count), 1)
    return jnp.sum(jnp.where(diagonal, row.astype(jnp.float32), 0.0), axis=1, keepdims=True)


def request_kernel(owner_ref, row_ref, requests_ref, codes_ref):
    count = owner_ref.shape[1]
    owner_row = owner_ref[...]
    owner_column = turned(owner_row).astype(jnp.int32)
    first, second = iota((count, count), 0), iota((count, count), 1)
    same = owner_row == owner_column
    earlier_column = jnp.sum(
        jnp.where(same & (second < first), 1.0, 0.0), axis=1, keepdims=True
    ).astype(jnp.int32)
    earlier_row = jnp.sum(
        jnp.where(same & (first < second), 1.0, 0.0), axis=0, keepdims=True
    ).astype(jnp.int32)
    asked = jnp.where(earlier_column == second, turned(row_ref[...]) + 1.0, 0.0)
    named = jnp.where(owner_row == first, 1.0, 0.0)
    found = pick(named.astype(jnp.bfloat16), asked.astype(jnp.bfloat16))
    requests_ref[...] = found.astype(jnp.int32) - 1
    codes_ref[...] = owner_row * (2 * XS) + earlier_row


def request(event_owner, event_row):
    count = event_row.shape[0]
    return pl.pallas_call(
        request_kernel,
        out_shape=[
            jax.ShapeDtypeStruct((count, HD), jnp.int32),
            jax.ShapeDtypeStruct((1, count), jnp.int32),
        ],
        compiler_params=pltpu.CompilerParams(vmem_limit_bytes=VMEM_BYTES),
        name="request",
    )(event_owner.reshape(1, count), event_row.reshape(1, count))


def join_kernel(text_ref, image_ref, price_ref, dir_ref, out_ref):
    columns = text_ref.shape[1]
    joined = (
        text_ref[...].astype(jnp.float32) * image_ref[...].astype(jnp.float32)
        + turned(price_ref[...]) * dir_ref[...].astype(jnp.float32)
    )
    width, depth = columns // XS, columns // XS // XS
    for x in range(XS):
        out_ref[:, x * width : (x + 1) * width] = jnp.concatenate(
            [joined[:, z * width + x * depth : z * width + (x + 1) * depth] for z in range(XS)],
            axis=1,
        ).astype(jnp.bfloat16)


def join(text_rows, image_rows, price, price_dir):
    return pl.pallas_call(
        join_kernel,
        out_shape=jax.ShapeDtypeStruct(text_rows.shape, jnp.bfloat16),
        compiler_params=pltpu.CompilerParams(vmem_limit_bytes=VMEM_BYTES),
        name="join",
    )(text_rows, image_rows, price.reshape(1, -1), price_dir.reshape(1, -1))


def answer_kernel(ids_ref, table_ref, out_ref):
    peers, table_rows = ids_ref.shape[0], table_ref.shape[0]
    count = 2 * peers
    width = table_ref.shape[1] // XS
    group = 2 * XS * CS
    target = iota((count, peers), 0)
    at = lax.rem(target, group)
    peer = (target - at) // 2 + lax.rem(at // 2, XS) * CS + at // (2 * XS)
    moved = jnp.where(peer == iota((count, peers), 1), 1.0, 0.0).astype(jnp.bfloat16)
    both = pick(moved, ids_ref[...].astype(jnp.float32).astype(jnp.bfloat16))
    lane, turn_of = iota(both.shape, 1), lax.rem(iota(both.shape, 0), 2)
    ids = jnp.sum(jnp.where(lane == turn_of, both, 0.0), axis=1, keepdims=True).astype(jnp.int32)
    wanted = jnp.where(ids == iota((count, table_rows), 1), 1.0, 0.0).astype(jnp.bfloat16)
    for block in range(XS):
        rows = pick(wanted, table_ref[:, block * width : (block + 1) * width]).astype(
            jnp.bfloat16
        )
        for z in range(count // group):
            to = (z * XS + block) * group
            out_ref[to : to + group, :] = rows[z * group : (z + 1) * group, :]


def answer(ids, table):
    return pl.pallas_call(
        answer_kernel,
        out_shape=jax.ShapeDtypeStruct(
            (2 * ids.shape[0] * XS, table.shape[1] // XS), jnp.bfloat16
        ),
        compiler_params=pltpu.CompilerParams(vmem_limit_bytes=VMEM_BYTES),
        name="answer",
    )(ids, table)


def select_kernel(codes_ref, replies_ref, gain_ref, out_ref):
    tokens, rows = codes_ref.shape[1], replies_ref.shape[0]
    replies = replies_ref[...]
    for x in range(XS):
        code = turned(codes_ref[x : x + 1, :]).astype(jnp.int32) + 2 * x
        chosen = jnp.where(code == iota((tokens, rows), 1), 1.0, 0.0).astype(jnp.bfloat16)
        out_ref[x * tokens : (x + 1) * tokens, :] = pick(chosen, replies).astype(jnp.bfloat16)
    out_ref[XS * tokens :, :] = jnp.broadcast_to(gain_ref[...], (GAIN_ROWS, gain_ref.shape[1]))


def select(codes, replies, gain):
    tokens, width = codes.size, replies.shape[1]
    return pl.pallas_call(
        select_kernel,
        out_shape=jax.ShapeDtypeStruct((tokens + GAIN_ROWS, width), jnp.bfloat16),
        compiler_params=pltpu.CompilerParams(vmem_limit_bytes=VMEM_BYTES),
        name="select",
    )(codes, replies, gain)


def project_kernel(
    order_ref, f0, f1, f2, f3, w_ref, own_ref, s1, s2, s3, acc_ref, normed_ref, held_ref, sum_ref, sem
):
    tokens = acc_ref.shape[0] // XS
    columns = acc_ref.shape[1]
    width = f0.shape[1]
    parts = (f0, f1, f2, f3)
    copies = []
    for k in range(len(parts)):
        there = pl.ds(pl.multiple_of(order_ref[k] * width, width), width)
        copies.append(
            pltpu.make_async_copy(
                w_ref.at[there, :], held_ref.at[k * width : (k + 1) * width, :], sem.at[k]
            )
        )
        copies[-1].start()

    total = jnp.zeros((XS * tokens, 1), jnp.float32)
    for k, part in enumerate(parts):
        value = part[: XS * tokens, :].astype(jnp.float32)
        gain = part[XS * tokens : XS * tokens + 1, :].astype(jnp.float32)
        total = total + jnp.sum(value * value, axis=1, keepdims=True)
        normed_ref[:, k * width : (k + 1) * width] = (value * gain).astype(jnp.bfloat16)
    sum_ref[...] = jnp.broadcast_to(total, sum_ref.shape)

    for copy in copies:
        copy.wait()
    tile = columns // 6
    for at in range(0, columns, tile):
        acc_ref[:, at : at + tile] = pick(normed_ref[...], held_ref[:, at : at + tile])

    mine = order_ref[XS]
    lane = iota((tokens, HD), 1)
    here = pl.ds(pl.multiple_of(mine * tokens, tokens), tokens)
    own_ref[:, :columns] = acc_ref[here, :]
    own_ref[:, columns:] = sum_ref[here, :]
    for k, out_ref in ((1, s1), (2, s2), (3, s3)):
        there = pl.ds(pl.multiple_of(lax.rem(mine + k, XS) * tokens, tokens), tokens)
        out_ref[:, :columns] = acc_ref[there, :].astype(jnp.bfloat16)
        total = sum_ref[there, :]
        high = total.astype(jnp.bfloat16).astype(jnp.float32)
        middle = (total - high).astype(jnp.bfloat16).astype(jnp.float32)
        low = total - high - middle
        out_ref[:, columns:] = jnp.where(
            lane == 0, high, jnp.where(lane == 1, middle, low)
        ).astype(jnp.bfloat16)


def project(order, turns, weights):
    rows, width = turns[0].shape
    tokens = (rows - GAIN_ROWS) // XS
    columns = weights.shape[1]
    vmem = pl.BlockSpec(memory_space=pltpu.VMEM)
    return pl.pallas_call(
        project_kernel,
        out_shape=[jax.ShapeDtypeStruct((tokens, columns + HD), jnp.float32)]
        + [jax.ShapeDtypeStruct((tokens, columns + HD), jnp.bfloat16)] * 3,
        in_specs=[pl.BlockSpec(memory_space=pltpu.SMEM)]
        + [vmem] * 4
        + [pl.BlockSpec(memory_space=pltpu.HBM)],
        out_specs=[vmem] * 4,
        scratch_shapes=[
            pltpu.VMEM((XS * tokens, columns), jnp.float32),
            pltpu.VMEM((XS * tokens, len(turns) * width), jnp.bfloat16),
            pltpu.VMEM(weights.shape, jnp.bfloat16),
            pltpu.VMEM((XS * tokens, HD), jnp.float32),
            pltpu.SemaphoreType.DMA((len(turns),)),
        ],
        compiler_params=pltpu.CompilerParams(vmem_limit_bytes=VMEM_BYTES),
        name="project",
    )(order, *turns, pltpu.with_memory_space_constraint(weights, pltpu.HBM))


def attend_kernel(length_ref, own_ref, p1, p2, p3, out_ref):
    tokens, width = out_ref.shape
    columns = 3 * width
    total = own_ref[:, columns : columns + 1]
    for part in (p1, p2, p3):
        pieces = part[:, columns : columns + HD].astype(jnp.float32)
        total = total + ((pieces[:, 0:1] + pieces[:, 1:2]) + pieces[:, 2:3])
    scale = lax.rsqrt(total / (8 * width) + 1e-06)
    length = length_ref[0]
    row = iota((tokens, tokens), 0)
    column = iota((tokens, tokens), 1)
    allowed = (column <= row) & (column < length)
    live = iota((tokens, HD), 0) < length
    for at in range(0, width, HD):
        query, keys, values = (
            (
                (
                    own_ref[:, a : a + HD]
                    + p1[:, a : a + HD].astype(jnp.float32)
                    + p2[:, a : a + HD].astype(jnp.float32)
                    + p3[:, a : a + HD].astype(jnp.float32)
                )
                * scale
            ).astype(jnp.bfloat16)
            for a in (at, width + at, 2 * width + at)
        )
        scores = lax.dot_general(
            query, keys, (((1,), (1,)), ((), ())), preferred_element_type=jnp.float32
        ) / math.sqrt(HD)
        scores = jnp.where(allowed, scores, jnp.float32(-1e30))
        powers = jnp.exp(scores - jnp.max(scores, axis=-1, keepdims=True))
        probs = (powers / jnp.sum(powers, axis=-1, keepdims=True)).astype(jnp.bfloat16)
        context = pick(probs, values)
        out_ref[:, at : at + HD] = jnp.where(live, context, 0.0).astype(jnp.bfloat16)


def attend(session_length, own, parts):
    tokens, columns = own.shape
    vmem = pl.BlockSpec(memory_space=pltpu.VMEM)
    return pl.pallas_call(
        attend_kernel,
        out_shape=jax.ShapeDtypeStruct((tokens, (columns - HD) // 3), jnp.bfloat16),
        in_specs=[pl.BlockSpec(memory_space=pltpu.SMEM)] + [vmem] * 4,
        out_specs=vmem,
        compiler_params=pltpu.CompilerParams(vmem_limit_bytes=VMEM_BYTES),
        name="attend",
    )(session_length, own, *parts)


def turn(value, axis, k):
    size = lax.axis_size(axis)
    return lax.ppermute(value, axis, [(i, (i + k) % size) for i in range(size)])


def exchange(value):
    return lax.all_to_all(value, DP, split_axis=0, concat_axis=0, tiled=True)


def local(
    session_length,
    event_owner,
    event_row,
    text_rows,
    image_rows,
    price,
    price_dir,
    norm_gain,
    w_query,
    w_key,
    w_value,
    cotangent,
):
    peers = lax.axis_size(DP)
    parts = lax.axis_size("mp")
    mine, across = lax.axis_index("mp"), lax.axis_index("x")
    tok_count = event_row.shape[0]
    capacity = 2 * tok_count // peers
    table_rows, col_width = text_rows.shape
    block = CS * w_query.shape[0]

    requests, codes = request(event_owner, event_row)
    got_ids = exchange(requests)
    w_query, w_key, w_value, _ = lax.optimization_barrier((w_query, w_key, w_value, requests))
    weights = lax.all_gather(
        jnp.concatenate([w_query, w_key, w_value], axis=1), ("z", "c"), axis=0, tiled=True
    )
    gain = lax.dynamic_index_in_dim(
        norm_gain.reshape(-1, XS, block), across, 1, keepdims=False
    ).reshape(1, -1)
    table = join(text_rows, image_rows, price, price_dir)
    all_codes = lax.all_gather(codes, "x", axis=0, tiled=True)
    got_ids, table, all_codes, gain = lax.optimization_barrier((got_ids, table, all_codes, gain))
    replies = exchange(
        answer(got_ids, table).reshape(peers, XS * capacity, col_width // XS)
    ).reshape(peers * XS * capacity, col_width // XS)

    slot_ids = codes[0] // (XS * capacity) * capacity + codes[0] % (XS * capacity)
    taken = jnp.arange(peers * capacity, dtype=jnp.int32)[:, None] == slot_ids[None, :]
    grad_buffer = (
        pick(taken.astype(jnp.bfloat16), cotangent)
        .astype(jnp.bfloat16)
        .reshape(peers, capacity, col_width)
    )
    grad_buffer, replies = lax.optimization_barrier((grad_buffer, replies))
    joined = select(all_codes, replies, gain)
    turns = [joined] + [turn(joined, "mp", k) for k in range(1, parts)]
    got_grads = exchange(grad_buffer).reshape(peers * capacity, col_width)
    ids = got_ids[:, :capacity].reshape(-1)
    wanted = (jnp.arange(table_rows, dtype=jnp.int32)[:, None] == ids[None, :]).astype(
        jnp.bfloat16
    )
    row_sums = pick(wanted, got_grads)
    text_grad = row_sums * image_rows.astype(jnp.float32)
    image_grad = row_sums * text_rows.astype(jnp.float32)

    order = jnp.concatenate(
        [(mine - jnp.arange(parts, dtype=jnp.int32)) % parts, across[None]]
    ).astype(jnp.int32)
    own, *sends = project(order, turns, weights)
    context = attend(
        session_length, own, [turn(part, "x", k) for k, part in enumerate(sends, 1)]
    )
    return (context, text_grad, image_grad)


def solution(mesh):
    fine = Mesh(mesh.devices.reshape(-1, XS, CS, mesh.shape["mp"]), (*DP, "mp"))
    return jax.shard_map(
        local,
        mesh=fine,
        in_specs=(
            P(DP),
            P(DP, None),
            P(DP),
            P(DP, "mp"),
            P(DP, "mp"),
            P(DP),
            P("mp"),
            P("mp"),
            P(DP, "mp"),
            P(DP, "mp"),
            P(DP, "mp"),
            P(DP, "mp"),
        ),
        out_specs=(P(DP, "mp"), P(DP, "mp"), P(DP, "mp")),
        check_vma=False,
    )
```

time: 181 us -> 173 us (0.956)
  the two profiles are of different devices: /device:TPU:11 before, /device:TPU:1 now
where the time goes in v4:
time: 173 us; the launch traced here: 171 us
  starting transfers between devices  64.6 us (37%)
  waiting for transfers between devices  58.2 us (34%)
  between operations  14.9 us (9%)
  Pallas kernels  12.2 us (7%)
  local copies, waits for them, and re-layouts  8.85 us (5%)
  blocking collectives  7.77 us (4%)
  matrix products  2.96 us (2%)
    all_to_all x3, starting transfers between devices, exchange(): return lax.all_to_all(value, DP, split_axis=0, concat_axis=0, tiled=True)  44.3 us
    all_to_all x3, waiting for transfers between devices, exchange(): return lax.all_to_all(value, DP, split_axis=0, concat_axis=0, tiled=True)  36.2 us
    ppermute x6, waiting for transfers between devices, turn(): return lax.ppermute(value, axis, [(i, (i + k) % size) for i in range(size)])  22 us
    ppermute x6, starting transfers between devices, turn(): return lax.ppermute(value, axis, [(i, (i + k) % size) for i in range(size)])  20.3 us
    all_gather x1, blocking collectives, local(): all_codes = lax.all_gather(codes, 'x', axis=0, tiled=True)  7.77 us
    pallas_call x1, Pallas kernels, project(): pl.pallas_call(project_kernel, out_shape=[jax.ShapeDtypeStruct((tokens, c...  5.82 us
    unnamed x16, local copies, waits for them, and re-layouts  4.12 us
  transfers between devices with their start and end apart: 10, of which 7 were waited for; matrix products, arithmetic and copies ran while one was open for 5% of the time, Pallas kernels for 5%

profile of v4, /device:TPU:1, one launch (start us, length us, event | category | flops | bytes accessed | tf_op | source)
XLA Modules:
  0.0 171.0 jit_solution(192984428840257839)
XLA Ops:
  7.2 0.0 copy-start
  7.2 0.0 all-gather.3.cloned.1.call-start
  7.2 0.0 copy-start.6
  7.2 0.7 copy-done.6
  7.9 0.7 copy-done.7
  8.6 0.9 request.1
  9.5 1.4 pad_maximum_fusion
  10.9 0.0 all-gather.3.cloned.1.call-update
  11.0 20.4 %all-to-all-start = ((s32[128,1,128]{2,1,0:T(1,128)}), s32[128,1,128]{2,1,0:T(1,128)S(1)}, u32[]{:S(2)}, u32[]{:S(2)}) async-start(s32[128,1,128]{2,1,0:T(1,128)} %bitcast.4), calls=%async_computation | async-start | bytes 131072 | tf_op jit(solution)/shard_map/all_to_all | solution.py:269
  31.4 0.7 reshape.43.dir_ref
  32.1 0.8 reshape.44
  32.9 0.1 reshape.45.gain_ref
  32.9 1.0 copy-done.1
  34.0 1.0 copy-done.3
  35.0 0.7 copy-done.5
  35.7 0.4 join.1.table_ref
  36.1 7.8 %all-gather = s32[4,1,128]{2,1,0:T(1,128)S(1)} all-gather(s32[1,1,128]{2,1,0:T(1,128)S(1)} %bitcast.22), channel_id=1, replica_groups=mesh['z'=16,'x'=4,'c'=2,'mp'=4] {'x'}, dimensions={0}, use_global_device_ids=true | all-gather | bytes 2560 | tf_op jit(solution)/shard_map/all_gather | solution.py:304
  43.9 2.4 %all-to-all-done = s32[128,1,128]{2,1,0:T(1,128)S(1)} async-done(((s32[128,1,128]{2,1,0:T(1,128)}), s32[128,1,128]{2,1,0:T(1,128)S(1)}, u32[]{:S(2)}, u32[]{:S(2)}) %all-to-all-start) | async-done | bytes 65568 | tf_op jit(solution)/shard_map/all_to_all | solution.py:269
  46.2 1.3 answer.1
  47.5 13.5 %all-to-all-start.1 = ((bf16[128,8,256]{2,1,0:T(8,128)(2,1)}), bf16[128,8,256]{2,1,0:T(8,128)(2,1)S(1)}, u32[]{:S(2)}, u32[]{:S(2)}) async-start(bf16[128,8,256]{2,1,0:T(8,128)(2,1)} %bitcast.10), calls=%async_computation.1 | async-start | bytes 1048576 | tf_op jit(solution)/shard_map/all_to_all | solution.py:269
  61.0 0.0 copy-done
  61.0 0.3 convolution_convert_fusion
  61.3 1.0 reshape.46
  62.3 33.8 %all-to-all-done.1 = bf16[128,8,256]{2,1,0:T(8,128)(2,1)S(1)} async-done(((bf16[128,8,256]{2,1,0:T(8,128)(2,1)}), bf16[128,8,256]{2,1,0:T(8,128)(2,1)S(1)}, u32[]{:S(2)}, u32[]{:S(2)}) %all-to-all-start.1) | async-done | bytes 524320 | tf_op jit(solution)/shard_map/all_to_all | solution.py:269
  96.1 10.4 %all-to-all-start.2 = ((bf16[128,2,1024]{2,1,0:T(2,128)(2,1)}), bf16[128,2,1024]{2,1,0:T(2,128)(2,1)}, u32[]{:S(2)}, u32[]{:S(2)}) async-start(bf16[128,2,1024]{2,1,0:T(2,128)(2,1)} %reshape.46), calls=%async_computation.2 | async-start | bytes 1048576 | tf_op jit(solution)/shard_map/all_to_all | solution.py:269
  106.5 0.0 copy-start.2
  106.5 0.0 copy-start.4
  106.5 0.5 select.13.f0
  107.1 4.7 %collective-permute-start.2 = (bf16[520,256]{1,0:T(8,128)(2,1)S(1)}, bf16[520,256]{1,0:T(8,128)(2,1)S(1)}, u32[]{:S(2)}, u32[]{:S(2)}) collective-permute-start(bf16[520,256]{1,0:T(8,128)(2,1)S(1)} %select.13.f0), channel_id=1, source_target_pairs={{0,3},{1,0},{2,1},{3,2},{4,7},{5,4},{6,5},{7,6},{8,11},{9,8},{10,9... | collective-permute-start | bytes 798728 | tf_op jit(solution)/shard_map/ppermute | solution.py:265
  111.8 2.4 %collective-permute-start.1 = (bf16[520,256]{1,0:T(8,128)(2,1)S(1)}, bf16[520,256]{1,0:T(8,128)(2,1)S(1)}, u32[]{:S(2)}, u32[]{:S(2)}) collective-permute-start(bf16[520,256]{1,0:T(8,128)(2,1)S(1)} %select.13.f0), channel_id=1, source_target_pairs={{0,2},{1,3},{2,0},{3,1},{4,6},{5,7},{6,4},{7,5},{8,10},{9,11},{10,... | collective-permute-start | bytes 798728 | tf_op jit(solution)/shard_map/ppermute | solution.py:265
  114.2 2.5 %collective-permute-start = (bf16[520,256]{1,0:T(8,128)(2,1)S(1)}, bf16[520,256]{1,0:T(8,128)(2,1)S(1)}, u32[]{:S(2)}, u32[]{:S(2)}) collective-permute-start(bf16[520,256]{1,0:T(8,128)(2,1)S(1)} %select.13.f0), channel_id=1, source_target_pairs={{0,1},{1,2},{2,3},{3,0},{4,5},{5,6},{6,7},{7,4},{8,9},{9,10},{10,1... | collective-permute-start | bytes 798728 | tf_op jit(solution)/shard_map/ppermute | solution.py:265
  116.7 0.1 pad_add_fusion.order_ref
  116.8 0.7 collective-permute-done.2.f3
  117.5 4.5 %collective-permute-done.1.f2 = bf16[520,256]{1,0:T(8,128)(2,1)S(1)} collective-permute-done((bf16[520,256]{1,0:T(8,128)(2,1)S(1)}, bf16[520,256]{1,0:T(8,128)(2,1)S(1)}, u32[]{:S(2)}, u32[]{:S(2)}) %collective-permute-start.1) | collective-permute-done | bytes 266272 | tf_op jit(solution)/shard_map/ppermute | solution.py:265
  122.0 7.3 %collective-permute-done.f1 = bf16[520,256]{1,0:T(8,128)(2,1)S(1)} collective-permute-done((bf16[520,256]{1,0:T(8,128)(2,1)S(1)}, bf16[520,256]{1,0:T(8,128)(2,1)S(1)}, u32[]{:S(2)}, u32[]{:S(2)}) %collective-permute-start) | collective-permute-done | bytes 266272 | tf_op jit(solution)/shard_map/ppermute | solution.py:265
  129.3 5.8 %project.1 = (f32[128,1664]{1,0:T(8,128)S(1)}, bf16[128,1664]{1,0:T(8,128)(2,1)}, bf16[128,1664]{1,0:T(8,128)(2,1)}, bf16[128,1664]{1,0:T(8,128)(2,1)}) custom-call(s32[5]{0:T(128)S(1)} %pad_add_fusion.order_ref, bf16[520,256]{1,0:T(8,128)(2,1)S(1)} %select.13.f0, bf16[520,256]{1,0:T(8,128)(2,1)S(1)} %collective-permute-done.f1, ...), custom_call_target="tpu_custom_call" | custom-call | tf_op jit(solution)/shard_map/project/pallas_call | solution.py:194
  135.1 3.3 %collective-permute-start.3 = (bf16[128,1664]{1,0:T(8,128)(2,1)}, bf16[128,1664]{1,0:T(8,128)(2,1)S(1)}, u32[]{:S(2)}, u32[]{:S(2)}) collective-permute-start(bf16[128,1664]{1,0:T(8,128)(2,1)} %get-tuple-element.29), channel_id=1, source_target_pairs={{0,8},{8,16},{16,24},{24,0},{1,9},{9,17},{17,25},{25,1},{2,10},{10... | collective-permute-start | bytes 1277960 | tf_op jit(solution)/shard_map/ppermute | solution.py:265
  138.5 4.3 %collective-permute-start.4 = (bf16[128,1664]{1,0:T(8,128)(2,1)}, bf16[128,1664]{1,0:T(8,128)(2,1)S(1)}, u32[]{:S(2)}, u32[]{:S(2)}) collective-permute-start(bf16[128,1664]{1,0:T(8,128)(2,1)} %get-tuple-element.30), channel_id=1, source_target_pairs={{0,16},{8,24},{16,0},{24,8},{1,17},{9,25},{17,1},{25,9},{2,18},{10... | collective-permute-start | bytes 1277960 | tf_op jit(solution)/shard_map/ppermute | solution.py:265
  142.8 3.1 %collective-permute-start.5 = (bf16[128,1664]{1,0:T(8,128)(2,1)}, bf16[128,1664]{1,0:T(8,128)(2,1)}, u32[]{:S(2)}, u32[]{:S(2)}) collective-permute-start(bf16[128,1664]{1,0:T(8,128)(2,1)} %get-tuple-element.31), channel_id=1, source_target_pairs={{0,24},{8,0},{16,8},{24,16},{1,25},{9,1},{17,9},{25,17},{2,26},{10... | collective-permute-start | bytes 1277960 | tf_op jit(solution)/shard_map/ppermute | solution.py:265
  146.5 0.1 eq.39
  146.7 0.0 all-to-all-done.2
  146.7 2.0 %reshape.49 = bf16[256,1024]{1,0:T(8,128)(2,1)} reshape(bf16[128,2,1024]{2,1,0:T(2,128)(2,1)} %all-to-all-done.2) | data formatting | bytes 1048576 | tf_op jit(solution)/shard_map/reshape | solution.py:320
  148.7 0.0 copy-done.4
  148.7 2.7 %convert_multiply_fusion = (f32[256,1024]{1,0:T(8,128)}, f32[256,1024]{1,0:T(8,128)}) fusion(bf16[256,1024]{1,0:T(8,128)(2,1)S(1)} %copy-done.2, bf16[256,1024]{1,0:T(8,128)(2,1)S(1)} %copy-done.4, bf16[256,1024]{1,0:T(8,128)(2,1)} %reshape.49, s32[256]{0:T(256)S(1)} %eq.39), kind=kOutput, calls=%fused_computation.1 | convolution fusion | flops 135331840 | bytes 3671040 | tf_op jit(solution)/shard_map/dot_general | solution.py:20
  151.4 0.0 collective-permute-done.3.p1
  151.4 8.3 %collective-permute-done.4.p2 = bf16[128,1664]{1,0:T(8,128)(2,1)S(1)} collective-permute-done((bf16[128,1664]{1,0:T(8,128)(2,1)}, bf16[128,1664]{1,0:T(8,128)(2,1)S(1)}, u32[]{:S(2)}, u32[]{:S(2)}) %collective-permute-start.4) | collective-permute-done | bytes 426016 | tf_op jit(solution)/shard_map/ppermute | solution.py:265
  159.7 1.2 collective-permute-done.5.p3
  160.9 3.2 %attend.1 = bf16[128,512]{1,0:T(8,128)(2,1)} custom-call(s32[1]{0:T(128)S(6)} %copy.19.length_ref, f32[128,1664]{1,0:T(8,128)S(1)} %get-tuple-element.28.own_ref, bf16[128,1664]{1,0:T(8,128)(2,1)S(1)} %collective-permute-done.3.p1, bf16[128,1664]{1,0:T(8,128)(2,1)S(1)} %collective-permute-done.4.p2, bf16[128,1664]{1,0:T(8,128)(2,1)} %collective-permute-done.5.p3), custom_call_target="tpu_custom_call" | custom-call | tf_op jit(solution)/shard_map/attend/pallas_call | solution.py:253
  (9 shorter events, 0.1 us)
Async XLA Ops:
  7.2 53.8 %copy-start = (bf16[128,1024]{1,0:T(8,128)(2,1)S(1)}, bf16[128,1024]{1,0:T(8,128)(2,1)}, u32[]{:S(2)}) copy-start(bf16[128,1024]{1,0:T(8,128)(2,1)} %param.23) | copy-start | bytes 786436
  7.2 122.1 %all-gather.3.cloned.1.call-start = ((), (), s32[]{:S(2)}) async-start(), calls=%async_computation.3 | async-start | bytes 3244032 | tf_op jit(solution)/shard_map/all_gather | solution.py:297
  7.2 0.7 copy-start.6
  7.9 0.7 copy-start.7
  11.0 35.3 %all-to-all-start = ((s32[128,1,128]{2,1,0:T(1,128)}), s32[128,1,128]{2,1,0:T(1,128)S(1)}, u32[]{:S(2)}, u32[]{:S(2)}) async-start(s32[128,1,128]{2,1,0:T(1,128)} %bitcast.4), calls=%async_computation | async-start | bytes 131072 | tf_op jit(solution)/shard_map/all_to_all | solution.py:269
  32.9 1.0 copy-start.1
  34.0 1.0 copy-start.3
  35.0 0.7 copy-start.5
  47.5 48.6 %all-to-all-start.1 = ((bf16[128,8,256]{2,1,0:T(8,128)(2,1)}), bf16[128,8,256]{2,1,0:T(8,128)(2,1)S(1)}, u32[]{:S(2)}, u32[]{:S(2)}) async-start(bf16[128,8,256]{2,1,0:T(8,128)(2,1)} %bitcast.10), calls=%async_computation.1 | async-start | bytes 1048576 | tf_op jit(solution)/shard_map/all_to_all | solution.py:269
  96.1 50.6 %all-to-all-start.2 = ((bf16[128,2,1024]{2,1,0:T(2,128)(2,1)}), bf16[128,2,1024]{2,1,0:T(2,128)(2,1)}, u32[]{:S(2)}, u32[]{:S(2)}) async-start(bf16[128,2,1024]{2,1,0:T(2,128)(2,1)} %reshape.46), calls=%async_computation.2 | async-start | bytes 1048576 | tf_op jit(solution)/shard_map/all_to_all | solution.py:269
  106.5 42.2 %copy-start.2 = (bf16[256,1024]{1,0:T(8,128)(2,1)S(1)}, bf16[256,1024]{1,0:T(8,128)(2,1)}, u32[]{:S(2)}) copy-start(bf16[256,1024]{1,0:T(8,128)(2,1)} %text_ref.1) | copy-start | bytes 1572868
  106.5 42.2 %copy-start.4 = (bf16[256,1024]{1,0:T(8,128)(2,1)S(1)}, bf16[256,1024]{1,0:T(8,128)(2,1)}, u32[]{:S(2)}) copy-start(bf16[256,1024]{1,0:T(8,128)(2,1)} %image_ref.1) | copy-start | bytes 1572868
  107.1 10.4 %collective-permute-start.2 = (bf16[520,256]{1,0:T(8,128)(2,1)S(1)}, bf16[520,256]{1,0:T(8,128)(2,1)S(1)}, u32[]{:S(2)}, u32[]{:S(2)}) collective-permute-start(bf16[520,256]{1,0:T(8,128)(2,1)S(1)} %select.13.f0), channel_id=1, source_target_pairs={{0,3},{1,0},{2,1},{3,2},{4,7},{5,4},{6,5},{7,6},{8,11},{9,8},{10,9... | collective-permute-start | bytes 798728 | tf_op jit(solution)/shard_map/ppermute | solution.py:265
  111.8 10.2 %collective-permute-start.1 = (bf16[520,256]{1,0:T(8,128)(2,1)S(1)}, bf16[520,256]{1,0:T(8,128)(2,1)S(1)}, u32[]{:S(2)}, u32[]{:S(2)}) collective-permute-start(bf16[520,256]{1,0:T(8,128)(2,1)S(1)} %select.13.f0), channel_id=1, source_target_pairs={{0,2},{1,3},{2,0},{3,1},{4,6},{5,7},{6,4},{7,5},{8,10},{9,11},{10,... | collective-permute-start | bytes 798728 | tf_op jit(solution)/shard_map/ppermute | solution.py:265
  114.2 15.1 %collective-permute-start = (bf16[520,256]{1,0:T(8,128)(2,1)S(1)}, bf16[520,256]{1,0:T(8,128)(2,1)S(1)}, u32[]{:S(2)}, u32[]{:S(2)}) collective-permute-start(bf16[520,256]{1,0:T(8,128)(2,1)S(1)} %select.13.f0), channel_id=1, source_target_pairs={{0,1},{1,2},{2,3},{3,0},{4,5},{5,6},{6,7},{7,4},{8,9},{9,10},{10,1... | collective-permute-start | bytes 798728 | tf_op jit(solution)/shard_map/ppermute | solution.py:265
  135.1 16.2 %collective-permute-start.3 = (bf16[128,1664]{1,0:T(8,128)(2,1)}, bf16[128,1664]{1,0:T(8,128)(2,1)S(1)}, u32[]{:S(2)}, u32[]{:S(2)}) collective-permute-start(bf16[128,1664]{1,0:T(8,128)(2,1)} %get-tuple-element.29), channel_id=1, source_target_pairs={{0,8},{8,16},{16,24},{24,0},{1,9},{9,17},{17,25},{25,1},{2,10},{10... | collective-permute-start | bytes 1277960 | tf_op jit(solution)/shard_map/ppermute | solution.py:265
  138.5 21.2 %collective-permute-start.4 = (bf16[128,1664]{1,0:T(8,128)(2,1)}, bf16[128,1664]{1,0:T(8,128)(2,1)S(1)}, u32[]{:S(2)}, u32[]{:S(2)}) collective-permute-start(bf16[128,1664]{1,0:T(8,128)(2,1)} %get-tuple-element.30), channel_id=1, source_target_pairs={{0,16},{8,24},{16,0},{24,8},{1,17},{9,25},{17,1},{25,9},{2,18},{10... | collective-permute-start | bytes 1277960 | tf_op jit(solution)/shard_map/ppermute | solution.py:265
  142.8 18.2 %collective-permute-start.5 = (bf16[128,1664]{1,0:T(8,128)(2,1)}, bf16[128,1664]{1,0:T(8,128)(2,1)}, u32[]{:S(2)}, u32[]{:S(2)}) collective-permute-start(bf16[128,1664]{1,0:T(8,128)(2,1)} %get-tuple-element.31), channel_id=1, source_target_pairs={{0,24},{8,0},{16,8},{24,16},{1,25},{9,1},{17,9},{25,17},{2,26},{10... | collective-permute-start | bytes 1277960 | tf_op jit(solution)/shard_map/ppermute | solution.py:265
Sparse Core Ops, SparseCore 0:
  11.1 89.2 all-gather.2

commit v5 on v4

--- a/solution.py
+++ b/solution.py
@@ -30,7 +30,7 @@
     return jnp.sum(jnp.where(diagonal, row.astype(jnp.float32), 0.0), axis=1, keepdims=True)
 
 
-def request_kernel(owner_ref, row_ref, requests_ref, codes_ref):
+def request_kernel(owner_ref, row_ref, wq_ref, wk_ref, wv_ref, requests_ref, codes_ref, w_ref):
     count = owner_ref.shape[1]
     owner_row = owner_ref[...]
     owner_column = turned(owner_row).astype(jnp.int32)
@@ -47,19 +47,23 @@
     found = pick(named.astype(jnp.bfloat16), asked.astype(jnp.bfloat16))
     requests_ref[...] = found.astype(jnp.int32) - 1
     codes_ref[...] = owner_row * (2 * XS) + earlier_row
-
-
-def request(event_owner, event_row):
+    width = wq_ref.shape[1]
+    for k, part in enumerate((wq_ref, wk_ref, wv_ref)):
+        w_ref[:, k * width : (k + 1) * width] = part[...]
+
+
+def request(event_owner, event_row, *projections):
     count = event_row.shape[0]
+    depth, width = projections[0].shape
     return pl.pallas_call(
         request_kernel,
         out_shape=[
             jax.ShapeDtypeStruct((count, HD), jnp.int32),
             jax.ShapeDtypeStruct((1, count), jnp.int32),
+            jax.ShapeDtypeStruct((depth, 3 * width), jnp.bfloat16),
         ],
-        compiler_params=pltpu.CompilerParams(vmem_limit_bytes=VMEM_BYTES),
         name="request",
-    )(event_owner.reshape(1, count), event_row.reshape(1, count))
+    )(event_owner.reshape(1, count), event_row.reshape(1, count), *projections)
 
 
 def join_kernel(text_ref, image_ref, price_ref, dir_ref, out_ref):
@@ -138,6 +142,66 @@
     )(codes, replies, gain)
 
 
+def pack_kernel(codes_ref, grads_ref, out_ref):
+    rows, width = out_ref.shape
+    tokens = codes_ref.shape[1]
+    number = iota((rows, tokens), 0)
+    code = number // (2 * XS) * (2 * XS) + lax.rem(number, 2 * XS) // XS
+    block = lax.rem(number, XS)
+    total = jnp.zeros((rows, width), jnp.float32)
+    for q in range(XS):
+        chosen = jnp.where((codes_ref[...] == code) & (block == q), 1.0, 0.0).astype(jnp.bfloat16)
+        total = total + pick(chosen, grads_ref[:, q * width : (q + 1) * width])
+    out_ref[...] = total.astype(jnp.bfloat16)
+
+
+def pack(codes, grads):
+    rows, width = 2 * XS * grads.shape[0], grads.shape[1] // XS
+    return pl.pallas_call(
+        pack_kernel,
+        out_shape=jax.ShapeDtypeStruct((rows, width), jnp.bfloat16),
+        compiler_params=pltpu.CompilerParams(vmem_limit_bytes=VMEM_BYTES),
+        cost_estimate=pl.CostEstimate(
+            flops=16 * rows * grads.size, bytes_accessed=2 * rows * width, transcendentals=0
+        ),
+        name="pack",
+    )(codes, grads)
+
+
+def credit_kernel(ids_ref, grads_ref, text_ref, image_ref, text_out, image_out):
+    peers, table_rows = ids_ref.shape[0], text_ref.shape[0]
+    rows, width = grads_ref.shape
+    spread = jnp.where(
+        iota((peers, rows), 0) == iota((peers, rows), 1) // (2 * XS), 1.0, 0.0
+    ).astype(jnp.bfloat16)
+    both = lax.dot_general(
+        ids_ref[...].astype(jnp.float32).astype(jnp.bfloat16),
+        spread,
+        (((0,), (0,)), ((), ())),
+        preferred_element_type=jnp.float32,
+    )
+    turn_of = lax.rem(iota(both.shape, 1), 2 * XS) // XS
+    ids = jnp.sum(jnp.where(iota(both.shape, 0) == turn_of, both, 0.0), axis=0, keepdims=True)
+    number = iota((table_rows, rows), 1)
+    named = iota((table_rows, rows), 0) == ids.astype(jnp.int32)
+    for q in range(XS):
+        at = slice(q * width, (q + 1) * width)
+        chosen = jnp.where(named & (lax.rem(number, XS) == q), 1.0, 0.0).astype(jnp.bfloat16)
+        total = pick(chosen, grads_ref[...])
+        text_out[:, at] = total * image_ref[:, at].astype(jnp.float32)
+        image_out[:, at] = total * text_ref[:, at].astype(jnp.float32)
+
+
+def credit(ids, grads, text_rows, image_rows):
+    out = jax.ShapeDtypeStruct(text_rows.shape, jnp.float32)
+    return pl.pallas_call(
+        credit_kernel,
+        out_shape=[out, out],
+        compiler_params=pltpu.CompilerParams(vmem_limit_bytes=VMEM_BYTES),
+        name="credit",
+    )(ids, grads, text_rows, image_rows)
+
+
 def project_kernel(
     order_ref, f0, f1, f2, f3, w_ref, own_ref, s1, s2, s3, acc_ref, normed_ref, held_ref, sum_ref, sem
 ):
@@ -207,6 +271,9 @@
             pltpu.SemaphoreType.DMA((len(turns),)),
         ],
         compiler_params=pltpu.CompilerParams(vmem_limit_bytes=VMEM_BYTES),
+        cost_estimate=pl.CostEstimate(
+            flops=64 * XS * tokens * weights.size, bytes_accessed=2 * weights.size, transcendentals=0
+        ),
         name="project",
     )(order, *turns, pltpu.with_memory_space_constraint(weights, pltpu.HBM))
 
@@ -288,51 +355,40 @@
     mine, across = lax.axis_index("mp"), lax.axis_index("x")
     tok_count = event_row.shape[0]
     capacity = 2 * tok_count // peers
-    table_rows, col_width = text_rows.shape
+    col_width = text_rows.shape[1]
     block = CS * w_query.shape[0]
 
-    requests, codes = request(event_owner, event_row)
+    requests, codes, joint = request(event_owner, event_row, w_query, w_key, w_value)
     got_ids = exchange(requests)
-    w_query, w_key, w_value, _ = lax.optimization_barrier((w_query, w_key, w_value, requests))
-    weights = lax.all_gather(
-        jnp.concatenate([w_query, w_key, w_value], axis=1), ("z", "c"), axis=0, tiled=True
+    weights = lax.all_gather(joint, ("z", "c"), axis=0, tiled=True)
+    table = join(text_rows, image_rows, price, price_dir)
+    got_ids, table = lax.optimization_barrier((got_ids, table))
+    replies, codes, norm_gain = lax.optimization_barrier(
+        (answer(got_ids, table), codes, norm_gain)
     )
+    packed = (peers, XS * capacity, col_width // XS)
+    flat = (peers * XS * capacity, col_width // XS)
+    replies = exchange(replies.reshape(packed)).reshape(flat)
     gain = lax.dynamic_index_in_dim(
         norm_gain.reshape(-1, XS, block), across, 1, keepdims=False
     ).reshape(1, -1)
-    table = join(text_rows, image_rows, price, price_dir)
     all_codes = lax.all_gather(codes, "x", axis=0, tiled=True)
-    got_ids, table, all_codes, gain = lax.optimization_barrier((got_ids, table, all_codes, gain))
-    replies = exchange(
-        answer(got_ids, table).reshape(peers, XS * capacity, col_width // XS)
-    ).reshape(peers * XS * capacity, col_width // XS)
-
-    slot_ids = codes[0] // (XS * capacity) * capacity + codes[0] % (XS * capacity)
-    taken = jnp.arange(peers * capacity, dtype=jnp.int32)[:, None] == slot_ids[None, :]
-    grad_buffer = (
-        pick(taken.astype(jnp.bfloat16), cotangent)
-        .astype(jnp.bfloat16)
-        .reshape(peers, capacity, col_width)
-    )
-    grad_buffer, replies = lax.optimization_barrier((grad_buffer, replies))
-    joined = select(all_codes, replies, gain)
-    turns = [joined] + [turn(joined, "mp", k) for k in range(1, parts)]
-    got_grads = exchange(grad_buffer).reshape(peers * capacity, col_width)
-    ids = got_ids[:, :capacity].reshape(-1)
-    wanted = (jnp.arange(table_rows, dtype=jnp.int32)[:, None] == ids[None, :]).astype(
-        jnp.bfloat16
-    )
-    row_sums = pick(wanted, got_grads)
-    text_grad = row_sums * image_rows.astype(jnp.float32)
-    image_grad = row_sums * text_rows.astype(jnp.float32)
-
     order = jnp.concatenate(
         [(mine - jnp.arange(parts, dtype=jnp.int32)) % parts, across[None]]
     ).astype(jnp.int32)
+    replies, all_codes, gain, order = lax.optimization_barrier((replies, all_codes, gain, order))
+    joined = select(all_codes, replies, gain)
+    turns = [joined] + [turn(joined, "mp", k) for k in range(1, parts)]
+    codes, cotangent, _ = lax.optimization_barrier((codes, cotangent, joined))
+    got_grads = exchange(pack(codes, cotangent).reshape(packed)).reshape(flat)
+
     own, *sends = project(order, turns, weights)
+    far = turn(sends[1], "x", 2)
     context = attend(
-        session_length, own, [turn(part, "x", k) for k, part in enumerate(sends, 1)]
+        session_length, own, [turn(sends[0], "x", 1), far, turn(sends[2], "x", 3)]
     )
+    context, got_grads = lax.optimization_barrier((context, got_grads))
+    text_grad, image_grad = credit(got_ids, got_grads, text_rows, image_rows)
     return (context, text_grad, image_grad)
 
 

time: 173 us -> 157 us (0.908)
  starting transfers between devices: 64.6 us -> 58.1 us
  local copies, waits for them, and re-layouts: 8.85 us -> 3.66 us
  matrix products: 2.96 us -> 0 us
  Pallas kernels: 12.2 us -> 14.8 us
  waiting for transfers between devices: 58.2 us -> 56 us
    all_to_all x3, starting transfers between devices: 44.3 us -> 37.3 us  [exchange(): return lax.all_to_all(value, DP, split_axis=0, concat_axis=0, tiled=True)]
    pallas_call x0 -> x2, Pallas kernels: none -> 3.8 us  [the longest x1 2.24 us: credit(): pl.pallas_call(credit_kernel, out_shape=[out, out], compiler_params=pltpu...]
    ppermute x6, waiting for transfers between devices: 22 us -> 18.4 us  [turn(): return lax.ppermute(value, axis, [(i, (i + k) % size) for i in range(size)])]
    reshape x2 -> x0, local copies, waits for them, and re-layouts: 3.04 us -> none  [the longest x1 2.04 us: local(): got_grads = exchange(grad_buffer).reshape(peers * capacity, col_width)]
    dot_general x2 -> x0, matrix products: 2.96 us -> none  [pick(): return jnp.dot(selector, values, preferred_element_type=jnp.float32)]
  transfers between devices with their start and end apart: 10 -> 10, of which waited for: 7 -> 5; matrix products, arithmetic and copies ran while one was open for 5% -> 1% of each run, Pallas kernels for 5% -> 7%
where the time goes in v5:
time: 157 us; the launch traced here: 156 us
  starting transfers between devices  58.1 us (37%)
  waiting for transfers between devices  56 us (36%)
  between operations  14.9 us (9%)
  Pallas kernels  14.8 us (9%)
  blocking collectives  8.55 us (5%)
  local copies, waits for them, and re-layouts  3.66 us (2%)
    all_to_all x3, waiting for transfers between devices, exchange(): return lax.all_to_all(value, DP, split_axis=0, concat_axis=0, tiled=True)  37.5 us
    all_to_all x3, starting transfers between devices, exchange(): return lax.all_to_all(value, DP, split_axis=0, concat_axis=0, tiled=True)  37.3 us
    ppermute x6, starting transfers between devices, turn(): return lax.ppermute(value, axis, [(i, (i + k) % size) for i in range(size)])  20.8 us
    ppermute x6, waiting for transfers between devices, turn(): return lax.ppermute(value, axis, [(i, (i + k) % size) for i in range(size)])  18.4 us
    all_gather x1, blocking collectives, local(): all_codes = lax.all_gather(codes, 'x', axis=0, tiled=True)  8.55 us
    pallas_call x1, Pallas kernels, project(): pl.pallas_call(project_kernel, out_shape=[jax.ShapeDtypeStruct((tokens, c...  4.78 us
  transfers between devices with their start and end apart: 10, of which 5 were waited for; matrix products, arithmetic and copies ran while one was open for 1% of the time, Pallas kernels for 7%

profile of v5, /device:TPU:1, one launch (start us, length us, event | category | flops | bytes accessed | tf_op | source)
XLA Modules:
  0.0 156.1 jit_solution(5318164378518247859)
XLA Ops:
  7.2 0.0 copy-start.7
  7.2 0.0 copy-start.6
  7.2 0.0 all-gather.3.cloned.1.call-start
  7.2 1.8 %request.1 = (s32[128,128]{1,0:T(8,128)}, s32[1,128]{1,0:T(1,128)}, bf16[32,1536]{1,0:T(8,128)(2,1)}) custom-call(s32[1,128]{1,0:T(1,128)} %bitcast.22, s32[1,128]{1,0:T(1,128)} %bitcast.23, bf16[32,512]{1,0:T(8,128)(2,1)} %wq_ref.1, bf16[32,512]{1,0:T(8,128)(2,1)} %wk_ref.1, bf16[32,512]{1,0:T(8,128)(2,1)} %wv_ref.1), custom_call_target="tpu_custom_call" | custom-call | tf_op jit(solution)/shard_map/request/pallas_call | solution.py:58
  9.0 0.0 copy-start.5
  9.0 0.0 all-gather.3.cloned.1.call-update
  9.1 20.4 %all-to-all-start = ((s32[128,1,128]{2,1,0:T(1,128)}), s32[128,1,128]{2,1,0:T(1,128)S(1)}, u32[]{:S(2)}, u32[]{:S(2)}) async-start(s32[128,1,128]{2,1,0:T(1,128)} %bitcast.21), calls=%async_computation | async-start | bytes 131072 | tf_op jit(solution)/shard_map/all_to_all | solution.py:336
  29.5 0.7 reshape.42.dir_ref
  30.2 0.0 copy-start
  30.2 1.0 copy-done
  31.2 1.0 copy-done.2
  32.3 0.7 copy-done.4
  32.9 0.4 join.1.table_ref
  33.3 11.0 %all-to-all-done = s32[128,1,128]{2,1,0:T(1,128)S(1)} async-done(((s32[128,1,128]{2,1,0:T(1,128)}), s32[128,1,128]{2,1,0:T(1,128)S(1)}, u32[]{:S(2)}, u32[]{:S(2)}) %all-to-all-start) | async-done | bytes 65568 | tf_op jit(solution)/shard_map/all_to_all | solution.py:336
  44.3 1.3 answer.1
  45.6 5.7 %all-to-all-start.1 = ((bf16[128,8,256]{2,1,0:T(8,128)(2,1)}), bf16[128,8,256]{2,1,0:T(8,128)(2,1)S(1)}, u32[]{:S(2)}, u32[]{:S(2)}) async-start(bf16[128,8,256]{2,1,0:T(8,128)(2,1)} %bitcast.6), calls=%async_computation.1 | async-start | bytes 1048576 | tf_op jit(solution)/shard_map/all_to_all | solution.py:336
  51.3 0.1 pad_add_fusion.order_ref
  51.4 0.0 copy-done.7
  51.4 0.1 reshape.45
  51.5 0.1 reshape.46.gain_ref
  51.6 0.0 copy-done.5
  51.6 8.5 %all-gather = s32[4,1,128]{2,1,0:T(1,128)S(1)} all-gather(s32[1,1,128]{2,1,0:T(1,128)S(1)} %bitcast.20), channel_id=1, replica_groups=mesh['z'=16,'x'=4,'c'=2,'mp'=4] {'x'}, dimensions={0}, use_global_device_ids=true | all-gather | bytes 2560 | tf_op jit(solution)/shard_map/all_gather | solution.py:375
  60.1 26.5 %all-to-all-done.1 = bf16[128,8,256]{2,1,0:T(8,128)(2,1)S(1)} async-done(((bf16[128,8,256]{2,1,0:T(8,128)(2,1)}), bf16[128,8,256]{2,1,0:T(8,128)(2,1)S(1)}, u32[]{:S(2)}, u32[]{:S(2)}) %all-to-all-start.1) | async-done | bytes 524320 | tf_op jit(solution)/shard_map/all_to_all | solution.py:336
  86.7 0.5 select.3.f0
  87.2 4.3 %collective-permute-start.2 = (bf16[520,256]{1,0:T(8,128)(2,1)S(1)}, bf16[520,256]{1,0:T(8,128)(2,1)S(1)}, u32[]{:S(2)}, u32[]{:S(2)}) collective-permute-start(bf16[520,256]{1,0:T(8,128)(2,1)S(1)} %select.3.f0), channel_id=1, source_target_pairs={{0,3},{1,0},{2,1},{3,2},{4,7},{5,4},{6,5},{7,6},{8,11},{9,8},{10,9... | collective-permute-start | bytes 798728 | tf_op jit(solution)/shard_map/ppermute | solution.py:332
  91.5 2.4 %collective-permute-start.1 = (bf16[520,256]{1,0:T(8,128)(2,1)S(1)}, bf16[520,256]{1,0:T(8,128)(2,1)S(1)}, u32[]{:S(2)}, u32[]{:S(2)}) collective-permute-start(bf16[520,256]{1,0:T(8,128)(2,1)S(1)} %select.3.f0), channel_id=1, source_target_pairs={{0,2},{1,3},{2,0},{3,1},{4,6},{5,7},{6,4},{7,5},{8,10},{9,11},{10,... | collective-permute-start | bytes 798728 | tf_op jit(solution)/shard_map/ppermute | solution.py:332
  94.0 2.8 %collective-permute-start = (bf16[520,256]{1,0:T(8,128)(2,1)S(1)}, bf16[520,256]{1,0:T(8,128)(2,1)S(1)}, u32[]{:S(2)}, u32[]{:S(2)}) collective-permute-start(bf16[520,256]{1,0:T(8,128)(2,1)S(1)} %select.3.f0), channel_id=1, source_target_pairs={{0,1},{1,2},{2,3},{3,0},{4,5},{5,6},{6,7},{7,4},{8,9},{9,10},{10,1... | collective-permute-start | bytes 798728 | tf_op jit(solution)/shard_map/ppermute | solution.py:332
  96.7 0.0 copy-done.6
  96.7 1.6 %pack.1 = bf16[1024,256]{1,0:T(8,128)(2,1)} custom-call(s32[1,128]{1,0:T(1,128)S(1)} %copy-done.5, bf16[128,1024]{1,0:T(8,128)(2,1)S(1)} %copy-done.6), custom_call_target="tpu_custom_call" | custom-call | flops 2147483648 | bytes 524288 | tf_op jit(solution)/shard_map/pack/pallas_call | solution.py:160
  98.3 11.2 %all-to-all-start.2 = ((bf16[128,8,256]{2,1,0:T(8,128)(2,1)}), bf16[128,8,256]{2,1,0:T(8,128)(2,1)S(1)}, u32[]{:S(2)}, u32[]{:S(2)}) async-start(bf16[128,8,256]{2,1,0:T(8,128)(2,1)} %bitcast.11), calls=%async_computation.2 | async-start | bytes 1048576 | tf_op jit(solution)/shard_map/all_to_all | solution.py:336
  109.5 0.0 copy-start.1
  109.5 0.0 copy-start.3
  109.5 0.0 collective-permute-done.2.f3
  109.6 0.0 collective-permute-done.1.f2
  109.6 0.0 collective-permute-done.f1
  109.6 0.0 all-gather.3.cloned.1.call-done.w_ref
  109.6 4.8 %project.1 = (f32[128,1664]{1,0:T(8,128)S(1)}, bf16[128,1664]{1,0:T(8,128)(2,1)S(1)}, bf16[128,1664]{1,0:T(8,128)(2,1)S(1)}, bf16[128,1664]{1,0:T(8,128)(2,1)S(1)}) custom-call(s32[5]{0:T(128)S(1)} %pad_add_fusion.order_ref, bf16[520,256]{1,0:T(8,128)(2,1)S(1)} %select.3.f0, bf16[520,256]{1,0:T(8,128)(2,1)S(1)} %collective-permute-done.f1, ...), custom_call_target="tpu_custom_call" | custom-call | flops 51539607552 | bytes 3145728 | tf_op jit(solution)/shard_map/project/pallas_call | solution.py:258
  114.4 3.7 %collective-permute-start.3 = (bf16[128,1664]{1,0:T(8,128)(2,1)S(1)}, bf16[128,1664]{1,0:T(8,128)(2,1)S(1)}, u32[]{:S(2)}, u32[]{:S(2)}) collective-permute-start(bf16[128,1664]{1,0:T(8,128)(2,1)S(1)} %get-tuple-element.38), channel_id=1, source_target_pairs={{0,8},{8,16},{16,24},{24,0},{1,9},{9,17},{17,25},{25,1},{2,10},{10... | collective-permute-start | bytes 1277960 | tf_op jit(solution)/shard_map/ppermute | solution.py:332
  118.1 4.9 %collective-permute-start.4 = (bf16[128,1664]{1,0:T(8,128)(2,1)S(1)}, bf16[128,1664]{1,0:T(8,128)(2,1)S(1)}, u32[]{:S(2)}, u32[]{:S(2)}) collective-permute-start(bf16[128,1664]{1,0:T(8,128)(2,1)S(1)} %get-tuple-element.39), channel_id=1, source_target_pairs={{0,16},{8,24},{16,0},{24,8},{1,17},{9,25},{17,1},{25,9},{2,18},{10... | collective-permute-start | bytes 1277960 | tf_op jit(solution)/shard_map/ppermute | solution.py:332
  123.0 2.7 %collective-permute-start.5 = (bf16[128,1664]{1,0:T(8,128)(2,1)S(1)}, bf16[128,1664]{1,0:T(8,128)(2,1)S(1)}, u32[]{:S(2)}, u32[]{:S(2)}) collective-permute-start(bf16[128,1664]{1,0:T(8,128)(2,1)S(1)} %get-tuple-element.40), channel_id=1, source_target_pairs={{0,24},{8,0},{16,8},{24,16},{1,25},{9,1},{17,9},{25,17},{2,26},{10... | collective-permute-start | bytes 1277960 | tf_op jit(solution)/shard_map/ppermute | solution.py:332
  126.4 6.6 %collective-permute-done.3.p1 = bf16[128,1664]{1,0:T(8,128)(2,1)S(1)} collective-permute-done((bf16[128,1664]{1,0:T(8,128)(2,1)S(1)}, bf16[128,1664]{1,0:T(8,128)(2,1)S(1)}, u32[]{:S(2)}, u32[]{:S(2)}) %collective-permute-start.3) | collective-permute-done | bytes 426016 | tf_op jit(solution)/shard_map/ppermute | solution.py:332
  132.9 10.8 %collective-permute-done.4.p2 = bf16[128,1664]{1,0:T(8,128)(2,1)S(1)} collective-permute-done((bf16[128,1664]{1,0:T(8,128)(2,1)S(1)}, bf16[128,1664]{1,0:T(8,128)(2,1)S(1)}, u32[]{:S(2)}, u32[]{:S(2)}) %collective-permute-start.4) | collective-permute-done | bytes 426016 | tf_op jit(solution)/shard_map/ppermute | solution.py:332
  143.7 1.1 collective-permute-done.5.p3
  144.8 2.2 %attend.1 = bf16[128,512]{1,0:T(8,128)(2,1)} custom-call(s32[1]{0:T(128)S(6)} %copy.19.length_ref, f32[128,1664]{1,0:T(8,128)S(1)} %get-tuple-element.37.own_ref, bf16[128,1664]{1,0:T(8,128)(2,1)S(1)} %collective-permute-done.3.p1, bf16[128,1664]{1,0:T(8,128)(2,1)S(1)} %collective-permute-done.4.p2, bf16[128,1664]{1,0:T(8,128)(2,1)S(1)} %collective-permute-done.5.p3), custom_call_target="tpu_custom_call" | custom-call | tf_op jit(solution)/shard_map/attend/pallas_call | solution.py:320
  147.0 0.0 all-to-all-done.2
  147.0 0.0 copy-done.1
  147.0 0.0 copy-done.3
  147.0 2.2 %credit.1 = (f32[256,1024]{1,0:T(8,128)}, f32[256,1024]{1,0:T(8,128)}) custom-call(s32[128,128]{1,0:T(8,128)S(1)} %bitcast.17, bf16[1024,256]{1,0:T(8,128)(2,1)S(1)} %bitcast.14, bf16[256,1024]{1,0:T(8,128)(2,1)S(1)} %copy-done.1, bf16[256,1024]{1,0:T(8,128)(2,1)S(1)} %copy-done.3), custom_call_target="tpu_custom_call" | custom-call | tf_op jit(solution)/shard_map/credit/pallas_call | solution.py:197
  (4 shorter events, 0.0 us)
Async XLA Ops:
  7.2 44.2 %copy-start.7 = (bf16[1024]{0:T(1024)(128)(2,1)S(1)}, bf16[1024]{0:T(1024)(128)(2,1)}, u32[]{:S(2)}) copy-start(bf16[1024]{0:T(1024)(128)(2,1)} %param.19) | copy-start | bytes 6148
  7.2 89.6 %copy-start.6 = (bf16[128,1024]{1,0:T(8,128)(2,1)S(1)}, bf16[128,1024]{1,0:T(8,128)(2,1)}, u32[]{:S(2)}) copy-start(bf16[128,1024]{1,0:T(8,128)(2,1)} %grads_ref) | copy-start | bytes 786436
  7.2 102.4 %all-gather.3.cloned.1.call-start = ((), (), s32[]{:S(2)}) async-start(), calls=%async_computation.3 | async-start | bytes 3244032 | tf_op jit(solution)/shard_map/all_gather | solution.py:363
  9.0 42.6 %copy-start.5 = (s32[1,128]{1,0:T(1,128)S(1)}, s32[1,128]{1,0:T(1,128)}, u32[]{:S(2)}) copy-start(s32[1,128]{1,0:T(1,128)} %get-tuple-element.41.codes_ref) | copy-start | bytes 1540
  9.1 35.3 %all-to-all-start = ((s32[128,1,128]{2,1,0:T(1,128)}), s32[128,1,128]{2,1,0:T(1,128)S(1)}, u32[]{:S(2)}, u32[]{:S(2)}) async-start(s32[128,1,128]{2,1,0:T(1,128)} %bitcast.21), calls=%async_computation | async-start | bytes 131072 | tf_op jit(solution)/shard_map/all_to_all | solution.py:336
  30.2 1.0 copy-start
  31.2 1.0 copy-start.2
  32.2 0.7 copy-start.4
  45.6 41.1 %all-to-all-start.1 = ((bf16[128,8,256]{2,1,0:T(8,128)(2,1)}), bf16[128,8,256]{2,1,0:T(8,128)(2,1)S(1)}, u32[]{:S(2)}, u32[]{:S(2)}) async-start(bf16[128,8,256]{2,1,0:T(8,128)(2,1)} %bitcast.6), calls=%async_computation.1 | async-start | bytes 1048576 | tf_op jit(solution)/shard_map/all_to_all | solution.py:336
  87.2 22.3 %collective-permute-start.2 = (bf16[520,256]{1,0:T(8,128)(2,1)S(1)}, bf16[520,256]{1,0:T(8,128)(2,1)S(1)}, u32[]{:S(2)}, u32[]{:S(2)}) collective-permute-start(bf16[520,256]{1,0:T(8,128)(2,1)S(1)} %select.3.f0), channel_id=1, source_target_pairs={{0,3},{1,0},{2,1},{3,2},{4,7},{5,4},{6,5},{7,6},{8,11},{9,8},{10,9... | collective-permute-start | bytes 798728 | tf_op jit(solution)/shard_map/ppermute | solution.py:332
  91.5 18.0 %collective-permute-start.1 = (bf16[520,256]{1,0:T(8,128)(2,1)S(1)}, bf16[520,256]{1,0:T(8,128)(2,1)S(1)}, u32[]{:S(2)}, u32[]{:S(2)}) collective-permute-start(bf16[520,256]{1,0:T(8,128)(2,1)S(1)} %select.3.f0), channel_id=1, source_target_pairs={{0,2},{1,3},{2,0},{3,1},{4,6},{5,7},{6,4},{7,5},{8,10},{9,11},{10,... | collective-permute-start | bytes 798728 | tf_op jit(solution)/shard_map/ppermute | solution.py:332
  94.0 15.6 %collective-permute-start = (bf16[520,256]{1,0:T(8,128)(2,1)S(1)}, bf16[520,256]{1,0:T(8,128)(2,1)S(1)}, u32[]{:S(2)}, u32[]{:S(2)}) collective-permute-start(bf16[520,256]{1,0:T(8,128)(2,1)S(1)} %select.3.f0), channel_id=1, source_target_pairs={{0,1},{1,2},{2,3},{3,0},{4,5},{5,6},{6,7},{7,4},{8,9},{9,10},{10,1... | collective-permute-start | bytes 798728 | tf_op jit(solution)/shard_map/ppermute | solution.py:332
  98.3 48.7 %all-to-all-start.2 = ((bf16[128,8,256]{2,1,0:T(8,128)(2,1)}), bf16[128,8,256]{2,1,0:T(8,128)(2,1)S(1)}, u32[]{:S(2)}, u32[]{:S(2)}) async-start(bf16[128,8,256]{2,1,0:T(8,128)(2,1)} %bitcast.11), calls=%async_computation.2 | async-start | bytes 1048576 | tf_op jit(solution)/shard_map/all_to_all | solution.py:336
  109.5 37.5 %copy-start.1 = (bf16[256,1024]{1,0:T(8,128)(2,1)S(1)}, bf16[256,1024]{1,0:T(8,128)(2,1)}, u32[]{:S(2)}) copy-start(bf16[256,1024]{1,0:T(8,128)(2,1)} %text_ref.3) | copy-start | bytes 1572868
  109.5 37.5 %copy-start.3 = (bf16[256,1024]{1,0:T(8,128)(2,1)S(1)}, bf16[256,1024]{1,0:T(8,128)(2,1)}, u32[]{:S(2)}) copy-start(bf16[256,1024]{1,0:T(8,128)(2,1)} %image_ref.3) | copy-start | bytes 1572868
  114.4 18.5 %collective-permute-start.3 = (bf16[128,1664]{1,0:T(8,128)(2,1)S(1)}, bf16[128,1664]{1,0:T(8,128)(2,1)S(1)}, u32[]{:S(2)}, u32[]{:S(2)}) collective-permute-start(bf16[128,1664]{1,0:T(8,128)(2,1)S(1)} %get-tuple-element.38), channel_id=1, source_target_pairs={{0,8},{8,16},{16,24},{24,0},{1,9},{9,17},{17,25},{25,1},{2,10},{10... | collective-permute-start | bytes 1277960 | tf_op jit(solution)/shard_map/ppermute | solution.py:332
  118.1 25.6 %collective-permute-start.4 = (bf16[128,1664]{1,0:T(8,128)(2,1)S(1)}, bf16[128,1664]{1,0:T(8,128)(2,1)S(1)}, u32[]{:S(2)}, u32[]{:S(2)}) collective-permute-start(bf16[128,1664]{1,0:T(8,128)(2,1)S(1)} %get-tuple-element.39), channel_id=1, source_target_pairs={{0,16},{8,24},{16,0},{24,8},{1,17},{9,25},{17,1},{25,9},{2,18},{10... | collective-permute-start | bytes 1277960 | tf_op jit(solution)/shard_map/ppermute | solution.py:332
  123.0 21.7 %collective-permute-start.5 = (bf16[128,1664]{1,0:T(8,128)(2,1)S(1)}, bf16[128,1664]{1,0:T(8,128)(2,1)S(1)}, u32[]{:S(2)}, u32[]{:S(2)}) collective-permute-start(bf16[128,1664]{1,0:T(8,128)(2,1)S(1)} %get-tuple-element.40), channel_id=1, source_target_pairs={{0,24},{8,0},{16,8},{24,16},{1,25},{9,1},{17,9},{25,17},{2,26},{10... | collective-permute-start | bytes 1277960 | tf_op jit(solution)/shard_map/ppermute | solution.py:332
Sparse Core Ops, SparseCore 0:
  10.7 89.5 all-gather.2

commit v6 on v5

--- a/solution.py
+++ b/solution.py
@@ -1,3 +1,4 @@
+import functools
 import math
 
 import jax
@@ -202,10 +203,9 @@
     )(ids, grads, text_rows, image_rows)
 
 
-def project_kernel(
-    order_ref, f0, f1, f2, f3, w_ref, own_ref, s1, s2, s3, acc_ref, normed_ref, held_ref, sum_ref, sem
-):
-    tokens = acc_ref.shape[0] // XS
+def project_kernel(shifts, order_ref, f0, f1, f2, f3, w_ref, *refs):
+    outs, (acc_ref, normed_ref, held_ref, sum_ref, sem) = refs[: len(shifts)], refs[len(shifts) :]
+    tokens = acc_ref.shape[0] // len(shifts)
     columns = acc_ref.shape[1]
     width = f0.shape[1]
     parts = (f0, f1, f2, f3)
@@ -219,13 +219,17 @@
         )
         copies[-1].start()
 
-    total = jnp.zeros((XS * tokens, 1), jnp.float32)
-    for k, part in enumerate(parts):
-        value = part[: XS * tokens, :].astype(jnp.float32)
-        gain = part[XS * tokens : XS * tokens + 1, :].astype(jnp.float32)
-        total = total + jnp.sum(value * value, axis=1, keepdims=True)
-        normed_ref[:, k * width : (k + 1) * width] = (value * gain).astype(jnp.bfloat16)
-    sum_ref[...] = jnp.broadcast_to(total, sum_ref.shape)
+    mine = order_ref[XS]
+    for n, shift in enumerate(shifts):
+        rows = slice(n * tokens, (n + 1) * tokens)
+        there = pl.ds(pl.multiple_of(lax.rem(mine + shift, XS) * tokens, tokens), tokens)
+        total = jnp.zeros((tokens, 1), jnp.float32)
+        for k, part in enumerate(parts):
+            value = part[there, :].astype(jnp.float32)
+            gain = part[XS * tokens : XS * tokens + 1, :].astype(jnp.float32)
+            total = total + jnp.sum(value * value, axis=1, keepdims=True)
+            normed_ref[rows, k * width : (k + 1) * width] = (value * gain).astype(jnp.bfloat16)
+        sum_ref[rows, :] = jnp.broadcast_to(total, (tokens, HD))
 
     for copy in copies:
         copy.wait()
@@ -233,46 +237,50 @@
     for at in range(0, columns, tile):
         acc_ref[:, at : at + tile] = pick(normed_ref[...], held_ref[:, at : at + tile])
 
-    mine = order_ref[XS]
     lane = iota((tokens, HD), 1)
-    here = pl.ds(pl.multiple_of(mine * tokens, tokens), tokens)
-    own_ref[:, :columns] = acc_ref[here, :]
-    own_ref[:, columns:] = sum_ref[here, :]
-    for k, out_ref in ((1, s1), (2, s2), (3, s3)):
-        there = pl.ds(pl.multiple_of(lax.rem(mine + k, XS) * tokens, tokens), tokens)
-        out_ref[:, :columns] = acc_ref[there, :].astype(jnp.bfloat16)
-        total = sum_ref[there, :]
-        high = total.astype(jnp.bfloat16).astype(jnp.float32)
-        middle = (total - high).astype(jnp.bfloat16).astype(jnp.float32)
-        low = total - high - middle
-        out_ref[:, columns:] = jnp.where(
-            lane == 0, high, jnp.where(lane == 1, middle, low)
-        ).astype(jnp.bfloat16)
-
-
-def project(order, turns, weights):
+    for n, (shift, out_ref) in enumerate(zip(shifts, outs)):
+        rows = slice(n * tokens, (n + 1) * tokens)
+        total = sum_ref[rows, :]
+        if shift == 0:
+            out_ref[:, :columns] = acc_ref[rows, :]
+            out_ref[:, columns:] = total
+        else:
+            out_ref[:, :columns] = acc_ref[rows, :].astype(jnp.bfloat16)
+            high = total.astype(jnp.bfloat16).astype(jnp.float32)
+            middle = (total - high).astype(jnp.bfloat16).astype(jnp.float32)
+            low = total - high - middle
+            out_ref[:, columns:] = jnp.where(
+                lane == 0, high, jnp.where(lane == 1, middle, low)
+            ).astype(jnp.bfloat16)
+
+
+def project(shifts, order, turns, weights):
     rows, width = turns[0].shape
     tokens = (rows - GAIN_ROWS) // XS
     columns = weights.shape[1]
     vmem = pl.BlockSpec(memory_space=pltpu.VMEM)
     return pl.pallas_call(
-        project_kernel,
-        out_shape=[jax.ShapeDtypeStruct((tokens, columns + HD), jnp.float32)]
-        + [jax.ShapeDtypeStruct((tokens, columns + HD), jnp.bfloat16)] * 3,
+        functools.partial(project_kernel, shifts),
+        out_shape=[
+            jax.ShapeDtypeStruct((tokens, columns + HD), jnp.bfloat16 if shift else jnp.float32)
+            for shift in shifts
+        ],
         in_specs=[pl.BlockSpec(memory_space=pltpu.SMEM)]
         + [vmem] * 4
         + [pl.BlockSpec(memory_space=pltpu.HBM)],
-        out_specs=[vmem] * 4,
+        out_specs=[vmem] * len(shifts),
         scratch_shapes=[
-            pltpu.VMEM((XS * tokens, columns), jnp.float32),
-            pltpu.VMEM((XS * tokens, len(turns) * width), jnp.bfloat16),
+            pltpu.VMEM((len(shifts) * tokens, columns), jnp.float32),
+            pltpu.VMEM((len(shifts) * tokens, len(turns) * width), jnp.bfloat16),
             pltpu.VMEM(weights.shape, jnp.bfloat16),
-            pltpu.VMEM((XS * tokens, HD), jnp.float32),
+            pltpu.VMEM((len(shifts) * tokens, HD), jnp.float32),
             pltpu.SemaphoreType.DMA((len(turns),)),
         ],
         compiler_params=pltpu.CompilerParams(vmem_limit_bytes=VMEM_BYTES),
         cost_estimate=pl.CostEstimate(
-            flops=64 * XS * tokens * weights.size, bytes_accessed=2 * weights.size, transcendentals=0
+            flops=64 * len(shifts) * tokens * weights.size,
+            bytes_accessed=2 * weights.size,
+            transcendentals=0,
         ),
         name="project",
     )(order, *turns, pltpu.with_memory_space_constraint(weights, pltpu.HBM))
@@ -372,20 +380,23 @@
     gain = lax.dynamic_index_in_dim(
         norm_gain.reshape(-1, XS, block), across, 1, keepdims=False
     ).reshape(1, -1)
+    grads = pack(codes, cotangent)
     all_codes = lax.all_gather(codes, "x", axis=0, tiled=True)
     order = jnp.concatenate(
         [(mine - jnp.arange(parts, dtype=jnp.int32)) % parts, across[None]]
     ).astype(jnp.int32)
-    replies, all_codes, gain, order = lax.optimization_barrier((replies, all_codes, gain, order))
+    replies, all_codes, gain, order, grads = lax.optimization_barrier(
+        (replies, all_codes, gain, order, grads)
+    )
     joined = select(all_codes, replies, gain)
     turns = [joined] + [turn(joined, "mp", k) for k in range(1, parts)]
-    codes, cotangent, _ = lax.optimization_barrier((codes, cotangent, joined))
-    got_grads = exchange(pack(codes, cotangent).reshape(packed)).reshape(flat)
-
-    own, *sends = project(order, turns, weights)
-    far = turn(sends[1], "x", 2)
+    grads, _ = lax.optimization_barrier((grads, joined))
+    got_grads = exchange(grads.reshape(packed)).reshape(flat)
+
+    (far,) = project((2,), order, turns, weights)
+    own, after, before = project((0, 1, 3), order, turns, weights)
     context = attend(
-        session_length, own, [turn(sends[0], "x", 1), far, turn(sends[2], "x", 3)]
+        session_length, own, [turn(after, "x", 1), turn(far, "x", 2), turn(before, "x", 3)]
     )
     context, got_grads = lax.optimization_barrier((context, got_grads))
     text_grad, image_grad = credit(got_ids, got_grads, text_rows, image_rows)

time: 157 us -> 154 us (0.981)
  waiting for transfers between devices: 56 us -> 49.3 us
  Pallas kernels: 14.8 us -> 17.1 us
    ppermute x6, waiting for transfers between devices: 18.4 us -> 13.3 us  [turn(): return lax.ppermute(value, axis, [(i, (i + k) % size) for i in range(size)])]
    pallas_call x1 -> x2, Pallas kernels: 4.78 us -> 7.06 us  [project(): pl.pallas_call(functools.partial(project_kernel, shifts), out_shape=[jax....]
  transfers between devices with their start and end apart: 10 -> 10, of which waited for: 5 -> 4; matrix products, arithmetic and copies ran while one was open for 1% -> 1% of each run, Pallas kernels for 7% -> 9%
where the time goes in v6:
time: 154 us; the launch traced here: 153 us
  starting transfers between devices  59.4 us (39%)
  waiting for transfers between devices  49.3 us (32%)
  Pallas kernels  17.1 us (11%)
  between operations  14.9 us (10%)
  blocking collectives  8.55 us (6%)
  local copies, waits for them, and re-layouts  3.66 us (2%)
    all_to_all x3, starting transfers between devices, exchange(): return lax.all_to_all(value, DP, split_axis=0, concat_axis=0, tiled=True)  37.6 us
    all_to_all x3, waiting for transfers between devices, exchange(): return lax.all_to_all(value, DP, split_axis=0, concat_axis=0, tiled=True)  36 us
    ppermute x6, starting transfers between devices, turn(): return lax.ppermute(value, axis, [(i, (i + k) % size) for i in range(size)])  21.8 us
    ppermute x6, waiting for transfers between devices, turn(): return lax.ppermute(value, axis, [(i, (i + k) % size) for i in range(size)])  13.3 us
    all_gather x1, blocking collectives, local(): all_codes = lax.all_gather(codes, 'x', axis=0, tiled=True)  8.55 us
    pallas_call x2, Pallas kernels, project(): pl.pallas_call(functools.partial(project_kernel, shifts), out_shape=[jax....  7.06 us
  transfers between devices with their start and end apart: 10, of which 4 were waited for; matrix products, arithmetic and copies ran while one was open for 1% of the time, Pallas kernels for 9%

profile of v6, /device:TPU:1, one launch (start us, length us, event | category | flops | bytes accessed | tf_op | source)
XLA Modules:
  0.0 153.0 jit_solution(6971416397010297756)
XLA Ops:
  7.2 0.0 copy-start.7
  7.2 0.0 copy-start.6
  7.2 0.0 all-gather.3.cloned.1.call-start
  7.2 1.8 %request.1 = (s32[128,128]{1,0:T(8,128)}, s32[1,128]{1,0:T(1,128)}, bf16[32,1536]{1,0:T(8,128)(2,1)}) custom-call(s32[1,128]{1,0:T(1,128)} %bitcast.22, s32[1,128]{1,0:T(1,128)} %bitcast.23, bf16[32,512]{1,0:T(8,128)(2,1)} %wq_ref.1, bf16[32,512]{1,0:T(8,128)(2,1)} %wk_ref.1, bf16[32,512]{1,0:T(8,128)(2,1)} %wv_ref.1), custom_call_target="tpu_custom_call" | custom-call | tf_op jit(solution)/shard_map/request/pallas_call | solution.py:59
  9.0 0.0 copy-start.5
  9.0 0.0 all-gather.3.cloned.1.call-update
  9.1 20.4 %all-to-all-start = ((s32[128,1,128]{2,1,0:T(1,128)}), s32[128,1,128]{2,1,0:T(1,128)S(1)}, u32[]{:S(2)}, u32[]{:S(2)}) async-start(s32[128,1,128]{2,1,0:T(1,128)} %bitcast.21), calls=%async_computation | async-start | bytes 131072 | tf_op jit(solution)/shard_map/all_to_all | solution.py:344
  29.5 0.7 reshape.42.dir_ref
  30.2 1.0 copy-done
  31.2 1.0 copy-done.2
  32.3 0.7 copy-done.4
  32.9 0.4 join.1.table_ref
  33.3 11.0 %all-to-all-done = s32[128,1,128]{2,1,0:T(1,128)S(1)} async-done(((s32[128,1,128]{2,1,0:T(1,128)}), s32[128,1,128]{2,1,0:T(1,128)S(1)}, u32[]{:S(2)}, u32[]{:S(2)}) %all-to-all-start) | async-done | bytes 65568 | tf_op jit(solution)/shard_map/all_to_all | solution.py:344
  44.3 1.3 answer.1
  45.6 5.7 %all-to-all-start.1 = ((bf16[128,8,256]{2,1,0:T(8,128)(2,1)}), bf16[128,8,256]{2,1,0:T(8,128)(2,1)S(1)}, u32[]{:S(2)}, u32[]{:S(2)}) async-start(bf16[128,8,256]{2,1,0:T(8,128)(2,1)} %bitcast.6), calls=%async_computation.1 | async-start | bytes 1048576 | tf_op jit(solution)/shard_map/all_to_all | solution.py:344
  51.3 0.1 pad_add_fusion.order_ref
  51.4 0.0 copy-done.7
  51.4 0.1 reshape.45
  51.5 0.1 reshape.46.gain_ref
  51.6 0.0 copy-done.5
  51.6 8.5 %all-gather = s32[4,1,128]{2,1,0:T(1,128)S(1)} all-gather(s32[1,1,128]{2,1,0:T(1,128)S(1)} %bitcast.20), channel_id=1, replica_groups=mesh['z'=16,'x'=4,'c'=2,'mp'=4] {'x'}, dimensions={0}, use_global_device_ids=true | all-gather | bytes 2560 | tf_op jit(solution)/shard_map/all_gather | solution.py:384
  60.1 0.0 copy-done.6
  60.1 1.6 %pack.1 = bf16[1024,256]{1,0:T(8,128)(2,1)} custom-call(s32[1,128]{1,0:T(1,128)S(1)} %copy-done.5, bf16[128,1024]{1,0:T(8,128)(2,1)S(1)} %copy-done.6), custom_call_target="tpu_custom_call" | custom-call | flops 2147483648 | bytes 524288 | tf_op jit(solution)/shard_map/pack/pallas_call | solution.py:161
  61.7 25.0 %all-to-all-done.1 = bf16[128,8,256]{2,1,0:T(8,128)(2,1)S(1)} async-done(((bf16[128,8,256]{2,1,0:T(8,128)(2,1)}), bf16[128,8,256]{2,1,0:T(8,128)(2,1)S(1)}, u32[]{:S(2)}, u32[]{:S(2)}) %all-to-all-start.1) | async-done | bytes 524320 | tf_op jit(solution)/shard_map/all_to_all | solution.py:344
  86.7 0.5 select.3.f0
  87.3 2.9 %collective-permute-start = (bf16[520,256]{1,0:T(8,128)(2,1)S(1)}, bf16[520,256]{1,0:T(8,128)(2,1)S(1)}, u32[]{:S(2)}, u32[]{:S(2)}) collective-permute-start(bf16[520,256]{1,0:T(8,128)(2,1)S(1)} %select.3.f0), channel_id=1, source_target_pairs={{0,1},{1,2},{2,3},{3,0},{4,5},{5,6},{6,7},{7,4},{8,9},{9,10},{10,1... | collective-permute-start | bytes 798728 | tf_op jit(solution)/shard_map/ppermute | solution.py:340
  90.1 4.4 %collective-permute-start.1 = (bf16[520,256]{1,0:T(8,128)(2,1)S(1)}, bf16[520,256]{1,0:T(8,128)(2,1)S(1)}, u32[]{:S(2)}, u32[]{:S(2)}) collective-permute-start(bf16[520,256]{1,0:T(8,128)(2,1)S(1)} %select.3.f0), channel_id=1, source_target_pairs={{0,2},{1,3},{2,0},{3,1},{4,6},{5,7},{6,4},{7,5},{8,10},{9,11},{10,... | collective-permute-start | bytes 798728 | tf_op jit(solution)/shard_map/ppermute | solution.py:340
  94.6 3.1 %collective-permute-start.2 = (bf16[520,256]{1,0:T(8,128)(2,1)S(1)}, bf16[520,256]{1,0:T(8,128)(2,1)S(1)}, u32[]{:S(2)}, u32[]{:S(2)}) collective-permute-start(bf16[520,256]{1,0:T(8,128)(2,1)S(1)} %select.3.f0), channel_id=1, source_target_pairs={{0,3},{1,0},{2,1},{3,2},{4,7},{5,4},{6,5},{7,6},{8,11},{9,8},{10,9... | collective-permute-start | bytes 798728 | tf_op jit(solution)/shard_map/ppermute | solution.py:340
  97.7 11.5 %all-to-all-start.2 = ((bf16[128,8,256]{2,1,0:T(8,128)(2,1)}), bf16[128,8,256]{2,1,0:T(8,128)(2,1)S(1)}, u32[]{:S(2)}, u32[]{:S(2)}) async-start(bf16[128,8,256]{2,1,0:T(8,128)(2,1)} %bitcast.11), calls=%async_computation.2 | async-start | bytes 1048576 | tf_op jit(solution)/shard_map/all_to_all | solution.py:344
  109.2 0.0 collective-permute-done.f1
  109.2 0.0 collective-permute-done.1.f2
  109.2 0.0 collective-permute-done.2.f3
  109.2 0.0 all-gather.3.cloned.1.call-done.w_ref
  109.2 3.1 %project.3 = bf16[128,1664]{1,0:T(8,128)(2,1)S(1)} custom-call(s32[5]{0:T(128)S(1)} %pad_add_fusion.order_ref, bf16[520,256]{1,0:T(8,128)(2,1)S(1)} %select.3.f0, bf16[520,256]{1,0:T(8,128)(2,1)S(1)} %collective-permute-done.f1, bf16[520,256]{1,0:T(8,128)(2,1)S(1)} %collective-permute-done.1.f2, bf16[520,256]{1,0:T(8,128)(2,1)S(1)} %collective-permute-done.2.f3, ...), custom_call_target="tpu_custom_call" | custom-call | flops 12884901888 | bytes 3145728 | tf_op jit(solution)/shard_map/project/pallas_call | solution.py:262
  112.3 0.0 copy-start.1
  112.3 0.0 copy-start.3
  112.3 4.9 %collective-permute-start.4 = (bf16[128,1664]{1,0:T(8,128)(2,1)S(1)}, bf16[128,1664]{1,0:T(8,128)(2,1)S(1)}, u32[]{:S(2)}, u32[]{:S(2)}) collective-permute-start(bf16[128,1664]{1,0:T(8,128)(2,1)S(1)} %project.3), channel_id=1, source_target_pairs={{0,16},{8,24},{16,0},{24,8},{1,17},{9,25},{17,1},{25,9},{2,18},{10... | collective-permute-start | bytes 1277960 | tf_op jit(solution)/shard_map/ppermute | solution.py:340
  117.2 4.0 %project.2 = (f32[128,1664]{1,0:T(8,128)S(1)}, bf16[128,1664]{1,0:T(8,128)(2,1)S(1)}, bf16[128,1664]{1,0:T(8,128)(2,1)S(1)}) custom-call(s32[5]{0:T(128)S(1)} %pad_add_fusion.order_ref, bf16[520,256]{1,0:T(8,128)(2,1)S(1)} %select.3.f0, bf16[520,256]{1,0:T(8,128)(2,1)S(1)} %collective-permute-done.f1, bf16[520,256]{1,0:T(8,128)(2,1)S(1)} %collective-permute-done.1.f2, ...), custom_call_target="tpu_custom_call" | custom-call | flops 38654705664 | bytes 3145728 | tf_op jit(solution)/shard_map/project/pallas_call | solution.py:262
  121.3 2.2 %collective-permute-start.3 = (bf16[128,1664]{1,0:T(8,128)(2,1)S(1)}, bf16[128,1664]{1,0:T(8,128)(2,1)S(1)}, u32[]{:S(2)}, u32[]{:S(2)}) collective-permute-start(bf16[128,1664]{1,0:T(8,128)(2,1)S(1)} %get-tuple-element.37), channel_id=1, source_target_pairs={{0,8},{8,16},{16,24},{24,0},{1,9},{9,17},{17,25},{25,1},{2,10},{10... | collective-permute-start | bytes 1277960 | tf_op jit(solution)/shard_map/ppermute | solution.py:340
  123.5 4.3 %collective-permute-start.5 = (bf16[128,1664]{1,0:T(8,128)(2,1)S(1)}, bf16[128,1664]{1,0:T(8,128)(2,1)S(1)}, u32[]{:S(2)}, u32[]{:S(2)}) collective-permute-start(bf16[128,1664]{1,0:T(8,128)(2,1)S(1)} %get-tuple-element.38), channel_id=1, source_target_pairs={{0,24},{8,0},{16,8},{24,16},{1,25},{9,1},{17,9},{25,17},{2,26},{10... | collective-permute-start | bytes 1277960 | tf_op jit(solution)/shard_map/ppermute | solution.py:340
  128.4 0.8 collective-permute-done.4.p2
  129.2 12.5 %collective-permute-done.3.p1 = bf16[128,1664]{1,0:T(8,128)(2,1)S(1)} collective-permute-done((bf16[128,1664]{1,0:T(8,128)(2,1)S(1)}, bf16[128,1664]{1,0:T(8,128)(2,1)S(1)}, u32[]{:S(2)}, u32[]{:S(2)}) %collective-permute-start.3) | collective-permute-done | bytes 426016 | tf_op jit(solution)/shard_map/ppermute | solution.py:340
  141.7 0.0 collective-permute-done.5.p3
  141.7 2.2 %attend.1 = bf16[128,512]{1,0:T(8,128)(2,1)} custom-call(s32[1]{0:T(128)S(6)} %copy.19.length_ref, f32[128,1664]{1,0:T(8,128)S(1)} %get-tuple-element.36.own_ref, bf16[128,1664]{1,0:T(8,128)(2,1)S(1)} %collective-permute-done.3.p1, bf16[128,1664]{1,0:T(8,128)(2,1)S(1)} %collective-permute-done.4.p2, bf16[128,1664]{1,0:T(8,128)(2,1)S(1)} %collective-permute-done.5.p3), custom_call_target="tpu_custom_call" | custom-call | tf_op jit(solution)/shard_map/attend/pallas_call | solution.py:328
  143.9 0.0 all-to-all-done.2
  143.9 0.0 copy-done.1
  143.9 0.0 copy-done.3
  143.9 2.2 %credit.1 = (f32[256,1024]{1,0:T(8,128)}, f32[256,1024]{1,0:T(8,128)}) custom-call(s32[128,128]{1,0:T(8,128)S(1)} %bitcast.17, bf16[1024,256]{1,0:T(8,128)(2,1)S(1)} %bitcast.14, bf16[256,1024]{1,0:T(8,128)(2,1)S(1)} %copy-done.1, bf16[256,1024]{1,0:T(8,128)(2,1)S(1)} %copy-done.3), custom_call_target="tpu_custom_call" | custom-call | tf_op jit(solution)/shard_map/credit/pallas_call | solution.py:198
  (5 shorter events, 0.0 us)
Async XLA Ops:
  7.2 44.2 %copy-start.7 = (bf16[1024]{0:T(1024)(128)(2,1)S(1)}, bf16[1024]{0:T(1024)(128)(2,1)}, u32[]{:S(2)}) copy-start(bf16[1024]{0:T(1024)(128)(2,1)} %param.19) | copy-start | bytes 6148
  7.2 53.0 %copy-start.6 = (bf16[128,1024]{1,0:T(8,128)(2,1)S(1)}, bf16[128,1024]{1,0:T(8,128)(2,1)}, u32[]{:S(2)}) copy-start(bf16[128,1024]{1,0:T(8,128)(2,1)} %grads_ref.1) | copy-start | bytes 786436
  7.2 102.0 %all-gather.3.cloned.1.call-start = ((), (), s32[]{:S(2)}) async-start(), calls=%async_computation.3 | async-start | bytes 3244032 | tf_op jit(solution)/shard_map/all_gather | solution.py:371
  9.0 42.6 %copy-start.5 = (s32[1,128]{1,0:T(1,128)S(1)}, s32[1,128]{1,0:T(1,128)}, u32[]{:S(2)}) copy-start(s32[1,128]{1,0:T(1,128)} %get-tuple-element.29.codes_ref) | copy-start | bytes 1540
  9.1 35.3 %all-to-all-start = ((s32[128,1,128]{2,1,0:T(1,128)}), s32[128,1,128]{2,1,0:T(1,128)S(1)}, u32[]{:S(2)}, u32[]{:S(2)}) async-start(s32[128,1,128]{2,1,0:T(1,128)} %bitcast.21), calls=%async_computation | async-start | bytes 131072 | tf_op jit(solution)/shard_map/all_to_all | solution.py:344
  30.2 1.0 copy-start
  31.2 1.0 copy-start.2
  32.3 0.7 copy-start.4
  45.6 41.1 %all-to-all-start.1 = ((bf16[128,8,256]{2,1,0:T(8,128)(2,1)}), bf16[128,8,256]{2,1,0:T(8,128)(2,1)S(1)}, u32[]{:S(2)}, u32[]{:S(2)}) async-start(bf16[128,8,256]{2,1,0:T(8,128)(2,1)} %bitcast.6), calls=%async_computation.1 | async-start | bytes 1048576 | tf_op jit(solution)/shard_map/all_to_all | solution.py:344
  87.3 21.9 %collective-permute-start = (bf16[520,256]{1,0:T(8,128)(2,1)S(1)}, bf16[520,256]{1,0:T(8,128)(2,1)S(1)}, u32[]{:S(2)}, u32[]{:S(2)}) collective-permute-start(bf16[520,256]{1,0:T(8,128)(2,1)S(1)} %select.3.f0), channel_id=1, source_target_pairs={{0,1},{1,2},{2,3},{3,0},{4,5},{5,6},{6,7},{7,4},{8,9},{9,10},{10,1... | collective-permute-start | bytes 798728 | tf_op jit(solution)/shard_map/ppermute | solution.py:340
  90.1 19.0 %collective-permute-start.1 = (bf16[520,256]{1,0:T(8,128)(2,1)S(1)}, bf16[520,256]{1,0:T(8,128)(2,1)S(1)}, u32[]{:S(2)}, u32[]{:S(2)}) collective-permute-start(bf16[520,256]{1,0:T(8,128)(2,1)S(1)} %select.3.f0), channel_id=1, source_target_pairs={{0,2},{1,3},{2,0},{3,1},{4,6},{5,7},{6,4},{7,5},{8,10},{9,11},{10,... | collective-permute-start | bytes 798728 | tf_op jit(solution)/shard_map/ppermute | solution.py:340
  94.6 14.6 %collective-permute-start.2 = (bf16[520,256]{1,0:T(8,128)(2,1)S(1)}, bf16[520,256]{1,0:T(8,128)(2,1)S(1)}, u32[]{:S(2)}, u32[]{:S(2)}) collective-permute-start(bf16[520,256]{1,0:T(8,128)(2,1)S(1)} %select.3.f0), channel_id=1, source_target_pairs={{0,3},{1,0},{2,1},{3,2},{4,7},{5,4},{6,5},{7,6},{8,11},{9,8},{10,9... | collective-permute-start | bytes 798728 | tf_op jit(solution)/shard_map/ppermute | solution.py:340
  97.7 46.3 %all-to-all-start.2 = ((bf16[128,8,256]{2,1,0:T(8,128)(2,1)}), bf16[128,8,256]{2,1,0:T(8,128)(2,1)S(1)}, u32[]{:S(2)}, u32[]{:S(2)}) async-start(bf16[128,8,256]{2,1,0:T(8,128)(2,1)} %bitcast.11), calls=%async_computation.2 | async-start | bytes 1048576 | tf_op jit(solution)/shard_map/all_to_all | solution.py:344
  112.3 31.6 %copy-start.1 = (bf16[256,1024]{1,0:T(8,128)(2,1)S(1)}, bf16[256,1024]{1,0:T(8,128)(2,1)}, u32[]{:S(2)}) copy-start(bf16[256,1024]{1,0:T(8,128)(2,1)} %text_ref.3) | copy-start | bytes 1572868
  112.3 31.6 %copy-start.3 = (bf16[256,1024]{1,0:T(8,128)(2,1)S(1)}, bf16[256,1024]{1,0:T(8,128)(2,1)}, u32[]{:S(2)}) copy-start(bf16[256,1024]{1,0:T(8,128)(2,1)} %image_ref.3) | copy-start | bytes 1572868
  112.3 16.9 %collective-permute-start.4 = (bf16[128,1664]{1,0:T(8,128)(2,1)S(1)}, bf16[128,1664]{1,0:T(8,128)(2,1)S(1)}, u32[]{:S(2)}, u32[]{:S(2)}) collective-permute-start(bf16[128,1664]{1,0:T(8,128)(2,1)S(1)} %project.3), channel_id=1, source_target_pairs={{0,16},{8,24},{16,0},{24,8},{1,17},{9,25},{17,1},{25,9},{2,18},{10... | collective-permute-start | bytes 1277960 | tf_op jit(solution)/shard_map/ppermute | solution.py:340
  121.3 20.4 %collective-permute-start.3 = (bf16[128,1664]{1,0:T(8,128)(2,1)S(1)}, bf16[128,1664]{1,0:T(8,128)(2,1)S(1)}, u32[]{:S(2)}, u32[]{:S(2)}) collective-permute-start(bf16[128,1664]{1,0:T(8,128)(2,1)S(1)} %get-tuple-element.37), channel_id=1, source_target_pairs={{0,8},{8,16},{16,24},{24,0},{1,9},{9,17},{17,25},{25,1},{2,10},{10... | collective-permute-start | bytes 1277960 | tf_op jit(solution)/shard_map/ppermute | solution.py:340
  123.5 18.2 %collective-permute-start.5 = (bf16[128,1664]{1,0:T(8,128)(2,1)S(1)}, bf16[128,1664]{1,0:T(8,128)(2,1)S(1)}, u32[]{:S(2)}, u32[]{:S(2)}) collective-permute-start(bf16[128,1664]{1,0:T(8,128)(2,1)S(1)} %get-tuple-element.38), channel_id=1, source_target_pairs={{0,24},{8,0},{16,8},{24,16},{1,25},{9,1},{17,9},{25,17},{2,26},{10... | collective-permute-start | bytes 1277960 | tf_op jit(solution)/shard_map/ppermute | solution.py:340
Sparse Core Ops, SparseCore 0:
  10.7 89.4 all-gather.2

commit v7 on v6

--- a/solution.py
+++ b/solution.py
@@ -209,18 +209,15 @@
     columns = acc_ref.shape[1]
     width = f0.shape[1]
     parts = (f0, f1, f2, f3)
+    tile = columns // 6
     copies = []
-    for k in range(len(parts)):
-        there = pl.ds(pl.multiple_of(order_ref[k] * width, width), width)
-        copies.append(
-            pltpu.make_async_copy(
-                w_ref.at[there, :], held_ref.at[k * width : (k + 1) * width, :], sem.at[k]
-            )
-        )
+    for n in range(columns // tile):
+        at = slice(n * tile, (n + 1) * tile)
+        copies.append(pltpu.make_async_copy(w_ref.at[:, at], held_ref.at[:, at], sem.at[n]))
         copies[-1].start()
 
     mine = order_ref[XS]
-    for n, shift in enumerate(shifts):
+    for n, (shift, _) in enumerate(shifts):
         rows = slice(n * tokens, (n + 1) * tokens)
         there = pl.ds(pl.multiple_of(lax.rem(mine + shift, XS) * tokens, tokens), tokens)
         total = jnp.zeros((tokens, 1), jnp.float32)
@@ -228,30 +225,50 @@
             value = part[there, :].astype(jnp.float32)
             gain = part[XS * tokens : XS * tokens + 1, :].astype(jnp.float32)
             total = total + jnp.sum(value * value, axis=1, keepdims=True)
-            normed_ref[rows, k * width : (k + 1) * width] = (value * gain).astype(jnp.bfloat16)
+            held = pl.ds(pl.multiple_of(order_ref[k] * width, width), width)
+            normed_ref[rows, held] = (value * gain).astype(jnp.bfloat16)
         sum_ref[rows, :] = jnp.broadcast_to(total, (tokens, HD))
 
-    for copy in copies:
+    for n, copy in enumerate(copies):
         copy.wait()
-    tile = columns // 6
-    for at in range(0, columns, tile):
-        acc_ref[:, at : at + tile] = pick(normed_ref[...], held_ref[:, at : at + tile])
-
-    lane = iota((tokens, HD), 1)
-    for n, (shift, out_ref) in enumerate(zip(shifts, outs)):
+        at = slice(n * tile, (n + 1) * tile)
+        acc_ref[:, at] = pick(normed_ref[...], held_ref[:, at])
+
+    for n, ((_, wide), out_ref) in enumerate(zip(shifts, outs)):
         rows = slice(n * tokens, (n + 1) * tokens)
-        total = sum_ref[rows, :]
-        if shift == 0:
-            out_ref[:, :columns] = acc_ref[rows, :]
-            out_ref[:, columns:] = total
-        else:
-            out_ref[:, :columns] = acc_ref[rows, :].astype(jnp.bfloat16)
-            high = total.astype(jnp.bfloat16).astype(jnp.float32)
-            middle = (total - high).astype(jnp.bfloat16).astype(jnp.float32)
-            low = total - high - middle
-            out_ref[:, columns:] = jnp.where(
-                lane == 0, high, jnp.where(lane == 1, middle, low)
-            ).astype(jnp.bfloat16)
+        out_ref[:, :columns] = acc_ref[rows, :].astype(out_ref.dtype)
+        out_ref[:, columns:] = sum_ref[rows, :] if wide else pieces(sum_ref[rows, :])
+
+
+def pieces(total):
+    high = total.astype(jnp.bfloat16).astype(jnp.float32)
+    middle = (total - high).astype(jnp.bfloat16).astype(jnp.float32)
+    lane = iota(total.shape, 1)
+    return jnp.where(lane == 0, high, jnp.where(lane == 1, middle, total - high - middle)).astype(
+        jnp.bfloat16
+    )
+
+
+def whole(lanes):
+    value = lanes.astype(jnp.float32)
+    return (value[:, 0:1] + value[:, 1:2]) + value[:, 2:3]
+
+
+def add_kernel(mine_ref, theirs_ref, out_ref):
+    columns = out_ref.shape[1] - HD
+    out_ref[:, :columns] = (
+        mine_ref[:, :columns] + theirs_ref[:, :columns].astype(jnp.float32)
+    ).astype(jnp.bfloat16)
+    out_ref[:, columns:] = pieces(mine_ref[:, columns:] + whole(theirs_ref[:, columns:]))
+
+
+def add(mine, theirs):
+    return pl.pallas_call(
+        add_kernel,
+        out_shape=jax.ShapeDtypeStruct(theirs.shape, theirs.dtype),
+        compiler_params=pltpu.CompilerParams(vmem_limit_bytes=VMEM_BYTES),
+        name="add",
+    )(mine, theirs)
 
 
 def project(shifts, order, turns, weights):
@@ -262,8 +279,8 @@
     return pl.pallas_call(
         functools.partial(project_kernel, shifts),
         out_shape=[
-            jax.ShapeDtypeStruct((tokens, columns + HD), jnp.bfloat16 if shift else jnp.float32)
-            for shift in shifts
+            jax.ShapeDtypeStruct((tokens, columns + HD), jnp.float32 if wide else jnp.bfloat16)
+            for _, wide in shifts
         ],
         in_specs=[pl.BlockSpec(memory_space=pltpu.SMEM)]
         + [vmem] * 4
@@ -274,7 +291,7 @@
             pltpu.VMEM((len(shifts) * tokens, len(turns) * width), jnp.bfloat16),
             pltpu.VMEM(weights.shape, jnp.bfloat16),
             pltpu.VMEM((len(shifts) * tokens, HD), jnp.float32),
-            pltpu.SemaphoreType.DMA((len(turns),)),
+            pltpu.SemaphoreType.DMA((6,)),
         ],
         compiler_params=pltpu.CompilerParams(vmem_limit_bytes=VMEM_BYTES),
         cost_estimate=pl.CostEstimate(
@@ -286,13 +303,12 @@
     )(order, *turns, pltpu.with_memory_space_constraint(weights, pltpu.HBM))
 
 
-def attend_kernel(length_ref, own_ref, p1, p2, p3, out_ref):
+def attend_kernel(length_ref, own_ref, p1, p2, out_ref):
     tokens, width = out_ref.shape
     columns = 3 * width
     total = own_ref[:, columns : columns + 1]
-    for part in (p1, p2, p3):
-        pieces = part[:, columns : columns + HD].astype(jnp.float32)
-        total = total + ((pieces[:, 0:1] + pieces[:, 1:2]) + pieces[:, 2:3])
+    for part in (p1, p2):
+        total = total + whole(part[:, columns:])
     scale = lax.rsqrt(total / (8 * width) + 1e-06)
     length = length_ref[0]
     row = iota((tokens, tokens), 0)
@@ -306,7 +322,6 @@
                     own_ref[:, a : a + HD]
                     + p1[:, a : a + HD].astype(jnp.float32)
                     + p2[:, a : a + HD].astype(jnp.float32)
-                    + p3[:, a : a + HD].astype(jnp.float32)
                 )
                 * scale
             ).astype(jnp.bfloat16)
@@ -328,7 +343,7 @@
     return pl.pallas_call(
         attend_kernel,
         out_shape=jax.ShapeDtypeStruct((tokens, (columns - HD) // 3), jnp.bfloat16),
-        in_specs=[pl.BlockSpec(memory_space=pltpu.SMEM)] + [vmem] * 4,
+        in_specs=[pl.BlockSpec(memory_space=pltpu.SMEM)] + [vmem] * 3,
         out_specs=vmem,
         compiler_params=pltpu.CompilerParams(vmem_limit_bytes=VMEM_BYTES),
         name="attend",
@@ -393,13 +408,13 @@
     grads, _ = lax.optimization_barrier((grads, joined))
     got_grads = exchange(grads.reshape(packed)).reshape(flat)
 
-    (far,) = project((2,), order, turns, weights)
-    own, after, before = project((0, 1, 3), order, turns, weights)
-    context = attend(
-        session_length, own, [turn(after, "x", 1), turn(far, "x", 2), turn(before, "x", 3)]
-    )
-    context, got_grads = lax.optimization_barrier((context, got_grads))
+    (far,) = project(((2, False),), order, turns, weights)
+    far = turn(far, "x", 3)
+    own, after, before = project(((0, True), (1, False), (3, True)), order, turns, weights)
+    after = turn(after, "x", 1)
+    before = turn(add(before, far), "x", 3)
     text_grad, image_grad = credit(got_ids, got_grads, text_rows, image_rows)
+    context = attend(session_length, own, (after, before))
     return (context, text_grad, image_grad)
 
 

time: 154 us -> 155 us (level)
  waiting for transfers between devices: 49.3 us -> 45.2 us
  Pallas kernels: 17.1 us -> 20.4 us
    ppermute x6, waiting for transfers between devices: 13.3 us -> 5.66 us  [turn(): return lax.ppermute(value, axis, [(i, (i + k) % size) for i in range(size)])]
    all_to_all x3, waiting for transfers between devices: 36 us -> 39.5 us  [exchange(): return lax.all_to_all(value, DP, split_axis=0, concat_axis=0, tiled=True)]
    pallas_call x2, Pallas kernels: 7.06 us -> 9.32 us  [project(): pl.pallas_call(functools.partial(project_kernel, shifts), out_shape=[jax....]
    unnamed x16 -> x20, local copies, waits for them, and re-layouts: 2.79 us -> 3.39 us
  transfers between devices with their start and end apart: 10 -> 10, of which waited for: 4 -> 5; matrix products, arithmetic and copies ran while one was open for 1% -> 1% of each run, Pallas kernels for 9% -> 11%
where the time goes in v7:
time: 155 us; the launch traced here: 153 us
  starting transfers between devices  60.1 us (39%)
  waiting for transfers between devices  45.2 us (29%)
  Pallas kernels  20.4 us (13%)
  between operations  14.9 us (10%)
  blocking collectives  8.54 us (6%)
  local copies, waits for them, and re-layouts  4.27 us (3%)
    all_to_all x3, waiting for transfers between devices, exchange(): return lax.all_to_all(value, DP, split_axis=0, concat_axis=0, tiled=True)  39.5 us
    all_to_all x3, starting transfers between devices, exchange(): return lax.all_to_all(value, DP, split_axis=0, concat_axis=0, tiled=True)  37.6 us
    ppermute x6, starting transfers between devices, turn(): return lax.ppermute(value, axis, [(i, (i + k) % size) for i in range(size)])  22.5 us
    pallas_call x2, Pallas kernels, project(): pl.pallas_call(functools.partial(project_kernel, shifts), out_shape=[jax....  9.32 us
    all_gather x1, blocking collectives, local(): all_codes = lax.all_gather(codes, 'x', axis=0, tiled=True)  8.54 us
    ppermute x6, waiting for transfers between devices, turn(): return lax.ppermute(value, axis, [(i, (i + k) % size) for i in range(size)])  5.66 us
    unnamed x20, local copies, waits for them, and re-layouts  3.39 us
  transfers between devices with their start and end apart: 10, of which 5 were waited for; matrix products, arithmetic and copies ran while one was open for 1% of the time, Pallas kernels for 11%

profile of v7, /device:TPU:1, one launch (start us, length us, event | category | flops | bytes accessed | tf_op | source)
XLA Modules:
  0.0 153.5 jit_solution(3825818922353812579)
XLA Ops:
  7.2 0.0 copy-start.9
  7.2 0.0 copy-start.6
  7.2 0.0 all-gather.3.cloned.1.call-start
  7.2 1.8 %request.1 = (s32[128,128]{1,0:T(8,128)}, s32[1,128]{1,0:T(1,128)}, bf16[32,1536]{1,0:T(8,128)(2,1)}) custom-call(s32[1,128]{1,0:T(1,128)} %bitcast.22, s32[1,128]{1,0:T(1,128)} %bitcast.23, bf16[32,512]{1,0:T(8,128)(2,1)} %wq_ref.1, bf16[32,512]{1,0:T(8,128)(2,1)} %wk_ref.1, bf16[32,512]{1,0:T(8,128)(2,1)} %wv_ref.1), custom_call_target="tpu_custom_call" | custom-call | tf_op jit(solution)/shard_map/request/pallas_call | solution.py:59
  9.0 0.0 all-gather.3.cloned.1.call-update
  9.1 20.4 %all-to-all-start = ((s32[128,1,128]{2,1,0:T(1,128)}), s32[128,1,128]{2,1,0:T(1,128)S(1)}, u32[]{:S(2)}, u32[]{:S(2)}) async-start(s32[128,1,128]{2,1,0:T(1,128)} %bitcast.21), calls=%async_computation | async-start | bytes 131072 | tf_op jit(solution)/shard_map/all_to_all | solution.py:359
  29.5 0.7 reshape.42.dir_ref
  30.2 1.0 copy-done
  31.2 1.0 copy-done.2
  32.3 0.7 copy-done.4
  32.9 0.4 join.1.table_ref
  33.3 11.0 %all-to-all-done = s32[128,1,128]{2,1,0:T(1,128)S(1)} async-done(((s32[128,1,128]{2,1,0:T(1,128)}), s32[128,1,128]{2,1,0:T(1,128)S(1)}, u32[]{:S(2)}, u32[]{:S(2)}) %all-to-all-start) | async-done | bytes 65568 | tf_op jit(solution)/shard_map/all_to_all | solution.py:359
  44.3 1.3 answer.1
  45.6 5.7 %all-to-all-start.1 = ((bf16[128,8,256]{2,1,0:T(8,128)(2,1)}), bf16[128,8,256]{2,1,0:T(8,128)(2,1)S(1)}, u32[]{:S(2)}, u32[]{:S(2)}) async-start(bf16[128,8,256]{2,1,0:T(8,128)(2,1)} %bitcast.6), calls=%async_computation.1 | async-start | bytes 1048576 | tf_op jit(solution)/shard_map/all_to_all | solution.py:359
  51.3 0.1 pad_add_fusion.order_ref
  51.4 0.0 copy-done.9
  51.4 0.1 reshape.45
  51.5 0.1 reshape.46.gain_ref
  51.6 0.0 copy-done.5
  51.6 8.5 %all-gather = s32[4,1,128]{2,1,0:T(1,128)S(1)} all-gather(s32[1,1,128]{2,1,0:T(1,128)S(1)} %bitcast.20), channel_id=1, replica_groups=mesh['z'=16,'x'=4,'c'=2,'mp'=4] {'x'}, dimensions={0}, use_global_device_ids=true | all-gather | bytes 2560 | tf_op jit(solution)/shard_map/all_gather | solution.py:399
  60.1 1.6 %pack.1 = bf16[1024,256]{1,0:T(8,128)(2,1)} custom-call(s32[1,128]{1,0:T(1,128)S(1)} %copy-done.5, bf16[128,1024]{1,0:T(8,128)(2,1)S(1)} %copy-done.6), custom_call_target="tpu_custom_call" | custom-call | flops 2147483648 | bytes 524288 | tf_op jit(solution)/shard_map/pack/pallas_call | solution.py:161
  61.7 25.0 %all-to-all-done.1 = bf16[128,8,256]{2,1,0:T(8,128)(2,1)S(1)} async-done(((bf16[128,8,256]{2,1,0:T(8,128)(2,1)}), bf16[128,8,256]{2,1,0:T(8,128)(2,1)S(1)}, u32[]{:S(2)}, u32[]{:S(2)}) %all-to-all-start.1) | async-done | bytes 524320 | tf_op jit(solution)/shard_map/all_to_all | solution.py:359
  86.7 0.5 select.3.f0
  87.3 2.9 %collective-permute-start = (bf16[520,256]{1,0:T(8,128)(2,1)S(1)}, bf16[520,256]{1,0:T(8,128)(2,1)S(1)}, u32[]{:S(2)}, u32[]{:S(2)}) collective-permute-start(bf16[520,256]{1,0:T(8,128)(2,1)S(1)} %select.3.f0), channel_id=1, source_target_pairs={{0,1},{1,2},{2,3},{3,0},{4,5},{5,6},{6,7},{7,4},{8,9},{9,10},{10,1... | collective-permute-start | bytes 798728 | tf_op jit(solution)/shard_map/ppermute | solution.py:355
  90.1 4.4 %collective-permute-start.1 = (bf16[520,256]{1,0:T(8,128)(2,1)S(1)}, bf16[520,256]{1,0:T(8,128)(2,1)S(1)}, u32[]{:S(2)}, u32[]{:S(2)}) collective-permute-start(bf16[520,256]{1,0:T(8,128)(2,1)S(1)} %select.3.f0), channel_id=1, source_target_pairs={{0,2},{1,3},{2,0},{3,1},{4,6},{5,7},{6,4},{7,5},{8,10},{9,11},{10,... | collective-permute-start | bytes 798728 | tf_op jit(solution)/shard_map/ppermute | solution.py:355
  94.6 3.1 %collective-permute-start.2 = (bf16[520,256]{1,0:T(8,128)(2,1)S(1)}, bf16[520,256]{1,0:T(8,128)(2,1)S(1)}, u32[]{:S(2)}, u32[]{:S(2)}) collective-permute-start(bf16[520,256]{1,0:T(8,128)(2,1)S(1)} %select.3.f0), channel_id=1, source_target_pairs={{0,3},{1,0},{2,1},{3,2},{4,7},{5,4},{6,5},{7,6},{8,11},{9,8},{10,9... | collective-permute-start | bytes 798728 | tf_op jit(solution)/shard_map/ppermute | solution.py:355
  97.7 11.5 %all-to-all-start.2 = ((bf16[128,8,256]{2,1,0:T(8,128)(2,1)}), bf16[128,8,256]{2,1,0:T(8,128)(2,1)S(1)}, u32[]{:S(2)}, u32[]{:S(2)}) async-start(bf16[128,8,256]{2,1,0:T(8,128)(2,1)} %bitcast.11), calls=%async_computation.2 | async-start | bytes 1048576 | tf_op jit(solution)/shard_map/all_to_all | solution.py:359
  109.2 0.0 collective-permute-done.f1
  109.2 0.0 collective-permute-done.1.f2
  109.2 0.0 collective-permute-done.2.f3
  109.2 0.0 all-gather.3.cloned.1.call-done.w_ref
  109.2 0.0 copy-done.7
  109.2 3.4 %project.3 = bf16[128,1664]{1,0:T(8,128)(2,1)S(1)} custom-call(s32[5]{0:T(128)S(1)} %pad_add_fusion.order_ref, bf16[520,256]{1,0:T(8,128)(2,1)S(1)} %select.3.f0, bf16[520,256]{1,0:T(8,128)(2,1)S(1)} %collective-permute-done.f1, bf16[520,256]{1,0:T(8,128)(2,1)S(1)} %collective-permute-done.1.f2, bf16[520,256]{1,0:T(8,128)(2,1)S(1)} %collective-permute-done.2.f3, ...), custom_call_target="tpu_custom_call" | custom-call | flops 12884901888 | bytes 3145728 | tf_op jit(solution)/shard_map/project/pallas_call | solution.py:279
  112.6 0.0 copy-start.1
  112.6 0.0 copy-start.3
  112.6 4.6 %collective-permute-start.4 = (bf16[128,1664]{1,0:T(8,128)(2,1)S(1)}, bf16[128,1664]{1,0:T(8,128)(2,1)S(1)}, u32[]{:S(2)}, u32[]{:S(2)}) collective-permute-start(bf16[128,1664]{1,0:T(8,128)(2,1)S(1)} %project.3), channel_id=1, source_target_pairs={{0,24},{8,0},{16,8},{24,16},{1,25},{9,1},{17,9},{25,17},{2,26},{10... | collective-permute-start | bytes 1277960 | tf_op jit(solution)/shard_map/ppermute | solution.py:355
  117.3 0.6 copy-done.8
  117.9 5.9 %project.2 = (f32[128,1664]{1,0:T(8,128)S(1)}, bf16[128,1664]{1,0:T(8,128)(2,1)}, f32[128,1664]{1,0:T(8,128)S(1)}) custom-call(s32[5]{0:T(128)S(1)} %copy-done.8, bf16[520,256]{1,0:T(8,128)(2,1)S(1)} %select.3.f0, bf16[520,256]{1,0:T(8,128)(2,1)S(1)} %collective-permute-done.f1, bf16[520,256]{1,0:T(8,128)(2,1)S(1)} %collective-permute-done.1.f2, ...), custom_call_target="tpu_custom_call" | custom-call | flops 38654705664 | bytes 3145728 | tf_op jit(solution)/shard_map/project/pallas_call | solution.py:279
  123.9 1.9 %collective-permute-start.3 = (bf16[128,1664]{1,0:T(8,128)(2,1)}, bf16[128,1664]{1,0:T(8,128)(2,1)S(1)}, u32[]{:S(2)}, u32[]{:S(2)}) collective-permute-start(bf16[128,1664]{1,0:T(8,128)(2,1)} %get-tuple-element.35), channel_id=1, source_target_pairs={{0,8},{8,16},{16,24},{24,0},{1,9},{9,17},{17,25},{25,1},{2,10},{10... | collective-permute-start | bytes 1277960 | tf_op jit(solution)/shard_map/ppermute | solution.py:355
  125.8 3.5 %collective-permute-done.4.theirs_ref = bf16[128,1664]{1,0:T(8,128)(2,1)S(1)} collective-permute-done((bf16[128,1664]{1,0:T(8,128)(2,1)S(1)}, bf16[128,1664]{1,0:T(8,128)(2,1)S(1)}, u32[]{:S(2)}, u32[]{:S(2)}) %collective-permute-start.4) | collective-permute-done | bytes 426016 | tf_op jit(solution)/shard_map/ppermute | solution.py:355
  129.2 1.0 add.17
  130.3 5.5 %collective-permute-start.5 = (bf16[128,1664]{1,0:T(8,128)(2,1)}, bf16[128,1664]{1,0:T(8,128)(2,1)S(1)}, u32[]{:S(2)}, u32[]{:S(2)}) collective-permute-start(bf16[128,1664]{1,0:T(8,128)(2,1)} %add.17), channel_id=1, source_target_pairs={{0,24},{8,0},{16,8},{24,16},{1,25},{9,1},{17,9},{25,17},{2,26},{10... | collective-permute-start | bytes 1277960 | tf_op jit(solution)/shard_map/ppermute | solution.py:355
  136.5 3.5 %all-to-all-done.2 = bf16[128,8,256]{2,1,0:T(8,128)(2,1)S(1)} async-done(((bf16[128,8,256]{2,1,0:T(8,128)(2,1)}), bf16[128,8,256]{2,1,0:T(8,128)(2,1)S(1)}, u32[]{:S(2)}, u32[]{:S(2)}) %all-to-all-start.2) | async-done | bytes 524320 | tf_op jit(solution)/shard_map/all_to_all | solution.py:359
  140.0 0.0 copy-done.3
  140.0 2.2 %credit.1 = (f32[256,1024]{1,0:T(8,128)}, f32[256,1024]{1,0:T(8,128)}) custom-call(s32[128,128]{1,0:T(8,128)S(1)} %bitcast.17, bf16[1024,256]{1,0:T(8,128)(2,1)S(1)} %bitcast.14, bf16[256,1024]{1,0:T(8,128)(2,1)S(1)} %copy-done.1, bf16[256,1024]{1,0:T(8,128)(2,1)S(1)} %copy-done.3), custom_call_target="tpu_custom_call" | custom-call | tf_op jit(solution)/shard_map/credit/pallas_call | solution.py:198
  142.2 0.0 collective-permute-done.3.p1
  142.2 2.2 %collective-permute-done.5.p2 = bf16[128,1664]{1,0:T(8,128)(2,1)S(1)} collective-permute-done((bf16[128,1664]{1,0:T(8,128)(2,1)}, bf16[128,1664]{1,0:T(8,128)(2,1)S(1)}, u32[]{:S(2)}, u32[]{:S(2)}) %collective-permute-start.5) | collective-permute-done | bytes 426016 | tf_op jit(solution)/shard_map/ppermute | solution.py:355
  144.4 2.2 %attend.1 = bf16[128,512]{1,0:T(8,128)(2,1)} custom-call(s32[1]{0:T(128)S(6)} %copy.19.length_ref, f32[128,1664]{1,0:T(8,128)S(1)} %get-tuple-element.34.own_ref, bf16[128,1664]{1,0:T(8,128)(2,1)S(1)} %collective-permute-done.3.p1, bf16[128,1664]{1,0:T(8,128)(2,1)S(1)} %collective-permute-done.5.p2), custom_call_target="tpu_custom_call" | custom-call | tf_op jit(solution)/shard_map/attend/pallas_call | solution.py:343
  (10 shorter events, 0.1 us)
Async XLA Ops:
  7.2 44.2 %copy-start.9 = (bf16[1024]{0:T(1024)(128)(2,1)S(1)}, bf16[1024]{0:T(1024)(128)(2,1)}, u32[]{:S(2)}) copy-start(bf16[1024]{0:T(1024)(128)(2,1)} %param.19) | copy-start | bytes 6148
  7.2 53.0 %copy-start.6 = (bf16[128,1024]{1,0:T(8,128)(2,1)S(1)}, bf16[128,1024]{1,0:T(8,128)(2,1)}, u32[]{:S(2)}) copy-start(bf16[128,1024]{1,0:T(8,128)(2,1)} %grads_ref.1) | copy-start | bytes 786436
  7.2 102.0 %all-gather.3.cloned.1.call-start = ((), (), s32[]{:S(2)}) async-start(), calls=%async_computation.3 | async-start | bytes 3244032 | tf_op jit(solution)/shard_map/all_gather | solution.py:386
  9.0 42.6 %copy-start.5 = (s32[1,128]{1,0:T(1,128)S(1)}, s32[1,128]{1,0:T(1,128)}, u32[]{:S(2)}) copy-start(s32[1,128]{1,0:T(1,128)} %get-tuple-element.27.codes_ref) | copy-start | bytes 1540
  9.1 35.3 %all-to-all-start = ((s32[128,1,128]{2,1,0:T(1,128)}), s32[128,1,128]{2,1,0:T(1,128)S(1)}, u32[]{:S(2)}, u32[]{:S(2)}) async-start(s32[128,1,128]{2,1,0:T(1,128)} %bitcast.21), calls=%async_computation | async-start | bytes 131072 | tf_op jit(solution)/shard_map/all_to_all | solution.py:359
  30.2 1.0 copy-start
  31.2 1.0 copy-start.2
  32.3 0.7 copy-start.4
  45.6 41.1 %all-to-all-start.1 = ((bf16[128,8,256]{2,1,0:T(8,128)(2,1)}), bf16[128,8,256]{2,1,0:T(8,128)(2,1)S(1)}, u32[]{:S(2)}, u32[]{:S(2)}) async-start(bf16[128,8,256]{2,1,0:T(8,128)(2,1)} %bitcast.6), calls=%async_computation.1 | async-start | bytes 1048576 | tf_op jit(solution)/shard_map/all_to_all | solution.py:359
  51.4 57.8 %copy-start.7 = (s32[5]{0:T(128)}, s32[5]{0:T(128)S(1)}, u32[]{:S(2)}) copy-start(s32[5]{0:T(128)S(1)} %pad_add_fusion.order_ref) | copy-start | bytes 64
  87.3 21.9 %collective-permute-start = (bf16[520,256]{1,0:T(8,128)(2,1)S(1)}, bf16[520,256]{1,0:T(8,128)(2,1)S(1)}, u32[]{:S(2)}, u32[]{:S(2)}) collective-permute-start(bf16[520,256]{1,0:T(8,128)(2,1)S(1)} %select.3.f0), channel_id=1, source_target_pairs={{0,1},{1,2},{2,3},{3,0},{4,5},{5,6},{6,7},{7,4},{8,9},{9,10},{10,1... | collective-permute-start | bytes 798728 | tf_op jit(solution)/shard_map/ppermute | solution.py:355
  90.1 19.0 %collective-permute-start.1 = (bf16[520,256]{1,0:T(8,128)(2,1)S(1)}, bf16[520,256]{1,0:T(8,128)(2,1)S(1)}, u32[]{:S(2)}, u32[]{:S(2)}) collective-permute-start(bf16[520,256]{1,0:T(8,128)(2,1)S(1)} %select.3.f0), channel_id=1, source_target_pairs={{0,2},{1,3},{2,0},{3,1},{4,6},{5,7},{6,4},{7,5},{8,10},{9,11},{10,... | collective-permute-start | bytes 798728 | tf_op jit(solution)/shard_map/ppermute | solution.py:355
  94.6 14.6 %collective-permute-start.2 = (bf16[520,256]{1,0:T(8,128)(2,1)S(1)}, bf16[520,256]{1,0:T(8,128)(2,1)S(1)}, u32[]{:S(2)}, u32[]{:S(2)}) collective-permute-start(bf16[520,256]{1,0:T(8,128)(2,1)S(1)} %select.3.f0), channel_id=1, source_target_pairs={{0,3},{1,0},{2,1},{3,2},{4,7},{5,4},{6,5},{7,6},{8,11},{9,8},{10,9... | collective-permute-start | bytes 798728 | tf_op jit(solution)/shard_map/ppermute | solution.py:355
  97.7 42.3 %all-to-all-start.2 = ((bf16[128,8,256]{2,1,0:T(8,128)(2,1)}), bf16[128,8,256]{2,1,0:T(8,128)(2,1)S(1)}, u32[]{:S(2)}, u32[]{:S(2)}) async-start(bf16[128,8,256]{2,1,0:T(8,128)(2,1)} %bitcast.11), calls=%async_computation.2 | async-start | bytes 1048576 | tf_op jit(solution)/shard_map/all_to_all | solution.py:359
  112.6 27.4 %copy-start.1 = (bf16[256,1024]{1,0:T(8,128)(2,1)S(1)}, bf16[256,1024]{1,0:T(8,128)(2,1)}, u32[]{:S(2)}) copy-start(bf16[256,1024]{1,0:T(8,128)(2,1)} %text_ref.3) | copy-start | bytes 1572868
  112.6 27.4 %copy-start.3 = (bf16[256,1024]{1,0:T(8,128)(2,1)S(1)}, bf16[256,1024]{1,0:T(8,128)(2,1)}, u32[]{:S(2)}) copy-start(bf16[256,1024]{1,0:T(8,128)(2,1)} %image_ref.3) | copy-start | bytes 1572868
  112.6 16.6 %collective-permute-start.4 = (bf16[128,1664]{1,0:T(8,128)(2,1)S(1)}, bf16[128,1664]{1,0:T(8,128)(2,1)S(1)}, u32[]{:S(2)}, u32[]{:S(2)}) collective-permute-start(bf16[128,1664]{1,0:T(8,128)(2,1)S(1)} %project.3), channel_id=1, source_target_pairs={{0,24},{8,0},{16,8},{24,16},{1,25},{9,1},{17,9},{25,17},{2,26},{10... | collective-permute-start | bytes 1277960 | tf_op jit(solution)/shard_map/ppermute | solution.py:355
  117.3 0.6 copy-start.8
  123.9 18.4 %collective-permute-start.3 = (bf16[128,1664]{1,0:T(8,128)(2,1)}, bf16[128,1664]{1,0:T(8,128)(2,1)S(1)}, u32[]{:S(2)}, u32[]{:S(2)}) collective-permute-start(bf16[128,1664]{1,0:T(8,128)(2,1)} %get-tuple-element.35), channel_id=1, source_target_pairs={{0,8},{8,16},{16,24},{24,0},{1,9},{9,17},{17,25},{25,1},{2,10},{10... | collective-permute-start | bytes 1277960 | tf_op jit(solution)/shard_map/ppermute | solution.py:355
  130.3 14.1 %collective-permute-start.5 = (bf16[128,1664]{1,0:T(8,128)(2,1)}, bf16[128,1664]{1,0:T(8,128)(2,1)S(1)}, u32[]{:S(2)}, u32[]{:S(2)}) collective-permute-start(bf16[128,1664]{1,0:T(8,128)(2,1)} %add.17), channel_id=1, source_target_pairs={{0,24},{8,0},{16,8},{24,16},{1,25},{9,1},{17,9},{25,17},{2,26},{10... | collective-permute-start | bytes 1277960 | tf_op jit(solution)/shard_map/ppermute | solution.py:355
Sparse Core Ops, SparseCore 0:
  10.7 89.4 all-gather.2

commit v8 on v6

--- a/solution.py
+++ b/solution.py
@@ -169,9 +169,8 @@
     )(codes, grads)
 
 
-def credit_kernel(ids_ref, grads_ref, text_ref, image_ref, text_out, image_out):
-    peers, table_rows = ids_ref.shape[0], text_ref.shape[0]
-    rows, width = grads_ref.shape
+def name_kernel(ids_ref, out_ref):
+    peers, rows = ids_ref.shape[0], out_ref.shape[1]
     spread = jnp.where(
         iota((peers, rows), 0) == iota((peers, rows), 1) // (2 * XS), 1.0, 0.0
     ).astype(jnp.bfloat16)
@@ -183,24 +182,44 @@
     )
     turn_of = lax.rem(iota(both.shape, 1), 2 * XS) // XS
     ids = jnp.sum(jnp.where(iota(both.shape, 0) == turn_of, both, 0.0), axis=0, keepdims=True)
-    number = iota((table_rows, rows), 1)
-    named = iota((table_rows, rows), 0) == ids.astype(jnp.int32)
+    out_ref[...] = ids.astype(jnp.int32)
+
+
+def name(ids):
+    return pl.pallas_call(
+        name_kernel,
+        out_shape=jax.ShapeDtypeStruct((1, 2 * XS * ids.shape[0]), jnp.int32),
+        compiler_params=pltpu.CompilerParams(vmem_limit_bytes=VMEM_BYTES),
+        name="name",
+    )(ids)
+
+
+def credit_kernel(named_ref, grads_ref, text_ref, image_ref, text_out, image_out):
+    table_rows = text_ref.shape[0]
+    rows, width = grads_ref.shape
+    block = lax.rem(iota((1, rows), 1), XS)
+    row = iota((table_rows, rows), 0)
     for q in range(XS):
         at = slice(q * width, (q + 1) * width)
-        chosen = jnp.where(named & (lax.rem(number, XS) == q), 1.0, 0.0).astype(jnp.bfloat16)
-        total = pick(chosen, grads_ref[...])
+        named = jnp.where(block == q, named_ref[...], -1)
+        total = pick(jnp.where(row == named, 1.0, 0.0).astype(jnp.bfloat16), grads_ref[...])
         text_out[:, at] = total * image_ref[:, at].astype(jnp.float32)
         image_out[:, at] = total * text_ref[:, at].astype(jnp.float32)
 
 
-def credit(ids, grads, text_rows, image_rows):
+def credit(named, grads, text_rows, image_rows):
     out = jax.ShapeDtypeStruct(text_rows.shape, jnp.float32)
     return pl.pallas_call(
         credit_kernel,
         out_shape=[out, out],
         compiler_params=pltpu.CompilerParams(vmem_limit_bytes=VMEM_BYTES),
         name="credit",
-    )(ids, grads, text_rows, image_rows)
+    )(
+        named,
+        grads,
+        pltpu.with_memory_space_constraint(text_rows, pltpu.HBM),
+        pltpu.with_memory_space_constraint(image_rows, pltpu.HBM),
+    )
 
 
 def project_kernel(shifts, order_ref, f0, f1, f2, f3, w_ref, *refs):
@@ -371,8 +390,8 @@
     weights = lax.all_gather(joint, ("z", "c"), axis=0, tiled=True)
     table = join(text_rows, image_rows, price, price_dir)
     got_ids, table = lax.optimization_barrier((got_ids, table))
-    replies, codes, norm_gain = lax.optimization_barrier(
-        (answer(got_ids, table), codes, norm_gain)
+    replies, codes, norm_gain, got_ids = lax.optimization_barrier(
+        (answer(got_ids, table), codes, norm_gain, got_ids)
     )
     packed = (peers, XS * capacity, col_width // XS)
     flat = (peers * XS * capacity, col_width // XS)
@@ -381,12 +400,13 @@
         norm_gain.reshape(-1, XS, block), across, 1, keepdims=False
     ).reshape(1, -1)
     grads = pack(codes, cotangent)
+    named = name(got_ids)
     all_codes = lax.all_gather(codes, "x", axis=0, tiled=True)
     order = jnp.concatenate(
         [(mine - jnp.arange(parts, dtype=jnp.int32)) % parts, across[None]]
     ).astype(jnp.int32)
-    replies, all_codes, gain, order, grads = lax.optimization_barrier(
-        (replies, all_codes, gain, order, grads)
+    replies, all_codes, gain, order, grads, named = lax.optimization_barrier(
+        (replies, all_codes, gain, order, grads, named)
     )
     joined = select(all_codes, replies, gain)
     turns = [joined] + [turn(joined, "mp", k) for k in range(1, parts)]
@@ -395,11 +415,11 @@
 
     (far,) = project((2,), order, turns, weights)
     own, after, before = project((0, 1, 3), order, turns, weights)
-    context = attend(
-        session_length, own, [turn(after, "x", 1), turn(far, "x", 2), turn(before, "x", 3)]
-    )
-    context, got_grads = lax.optimization_barrier((context, got_grads))
-    text_grad, image_grad = credit(got_ids, got_grads, text_rows, image_rows)
+    far = turn(far, "x", 2)
+    far, got_grads = lax.optimization_barrier((far, got_grads))
+    received = (turn(after, "x", 1), far, turn(before, "x", 3))
+    text_grad, image_grad = credit(named, got_grads, text_rows, image_rows)
+    context = attend(session_length, own, received)
     return (context, text_grad, image_grad)
 
 

time: 154 us -> 154 us (level)
  waiting for transfers between devices: 49.3 us -> 44.1 us
  Pallas kernels: 17.1 us -> 19.2 us
    ppermute x6, waiting for transfers between devices: 13.3 us -> 0.62 us  [turn(): return lax.ppermute(value, axis, [(i, (i + k) % size) for i in range(size)])]
    all_to_all x3, waiting for transfers between devices: 36 us -> 43.5 us  [exchange(): return lax.all_to_all(value, DP, split_axis=0, concat_axis=0, tiled=True)]
  transfers between devices with their start and end apart: 10 -> 10, of which waited for: 4 -> 4; matrix products, arithmetic and copies ran while one was open for 1% -> 1% of each run, Pallas kernels for 9% -> 10%
where the time goes in v8:
time: 154 us; the launch traced here: 152 us
  starting transfers between devices  60.3 us (39%)
  waiting for transfers between devices  44.1 us (29%)
  Pallas kernels  19.2 us (12%)
  between operations  14.9 us (10%)
  blocking collectives  8.61 us (6%)
  local copies, waits for them, and re-layouts  4.6 us (3%)
    all_to_all x3, waiting for transfers between devices, exchange(): return lax.all_to_all(value, DP, split_axis=0, concat_axis=0, tiled=True)  43.5 us
    all_to_all x3, starting transfers between devices, exchange(): return lax.all_to_all(value, DP, split_axis=0, concat_axis=0, tiled=True)  37.3 us
    ppermute x6, starting transfers between devices, turn(): return lax.ppermute(value, axis, [(i, (i + k) % size) for i in range(size)])  22.9 us
    all_gather x1, blocking collectives, local(): all_codes = lax.all_gather(codes, 'x', axis=0, tiled=True)  8.61 us
    pallas_call x2, Pallas kernels, project(): pl.pallas_call(functools.partial(project_kernel, shifts), out_shape=[jax....  7.81 us
    unnamed x16, local copies, waits for them, and re-layouts  3.72 us
    pallas_call x1, Pallas kernels, credit(): pl.pallas_call(credit_kernel, out_shape=[out, out], compiler_params=pltpu...  3.28 us
  transfers between devices with their start and end apart: 10, of which 4 were waited for; matrix products, arithmetic and copies ran while one was open for 1% of the time, Pallas kernels for 10%

profile of v8, /device:TPU:1, one launch (start us, length us, event | category | flops | bytes accessed | tf_op | source)
XLA Modules:
  0.0 151.7 jit_solution(11595014136563792542)
XLA Ops:
  7.2 0.0 copy-start.7
  7.2 0.0 copy-start.6
  7.2 0.0 all-gather.3.cloned.1.call-start
  7.2 1.8 %request.1 = (s32[128,128]{1,0:T(8,128)}, s32[1,128]{1,0:T(1,128)}, bf16[32,1536]{1,0:T(8,128)(2,1)}) custom-call(s32[1,128]{1,0:T(1,128)} %bitcast.22, s32[1,128]{1,0:T(1,128)} %bitcast.23, bf16[32,512]{1,0:T(8,128)(2,1)} %wq_ref.1, bf16[32,512]{1,0:T(8,128)(2,1)} %wk_ref.1, bf16[32,512]{1,0:T(8,128)(2,1)} %wv_ref.1), custom_call_target="tpu_custom_call" | custom-call | tf_op jit(solution)/shard_map/request/pallas_call | solution.py:59
  9.0 0.0 copy-start.3
  9.0 0.0 all-gather.3.cloned.1.call-update
  9.1 20.4 %all-to-all-start = ((s32[128,1,128]{2,1,0:T(1,128)}), s32[128,1,128]{2,1,0:T(1,128)S(1)}, u32[]{:S(2)}, u32[]{:S(2)}) async-start(s32[128,1,128]{2,1,0:T(1,128)} %bitcast.21), calls=%async_computation | async-start | bytes 131072 | tf_op jit(solution)/shard_map/all_to_all | solution.py:363
  29.5 0.7 reshape.42.dir_ref
  30.2 0.0 copy-start
  30.2 1.0 copy-done
  31.2 1.0 copy-done.1
  32.3 0.7 copy-done.2
  32.9 0.4 join.1.table_ref
  33.3 11.0 %all-to-all-done = s32[128,1,128]{2,1,0:T(1,128)S(1)} async-done(((s32[128,1,128]{2,1,0:T(1,128)}), s32[128,1,128]{2,1,0:T(1,128)S(1)}, u32[]{:S(2)}, u32[]{:S(2)}) %all-to-all-start) | async-done | bytes 65568 | tf_op jit(solution)/shard_map/all_to_all | solution.py:363
  44.3 1.3 answer.1
  45.6 5.7 %all-to-all-start.1 = ((bf16[128,8,256]{2,1,0:T(8,128)(2,1)}), bf16[128,8,256]{2,1,0:T(8,128)(2,1)S(1)}, u32[]{:S(2)}, u32[]{:S(2)}) async-start(bf16[128,8,256]{2,1,0:T(8,128)(2,1)} %bitcast.6), calls=%async_computation.1 | async-start | bytes 1048576 | tf_op jit(solution)/shard_map/all_to_all | solution.py:363
  51.3 0.1 pad_add_fusion.order_ref
  51.4 0.0 copy-done.7
  51.4 0.1 reshape.45
  51.5 0.1 reshape.46.gain_ref
  51.6 0.3 name.1.named_ref
  51.9 0.0 copy-done.3
  51.9 8.6 %all-gather = s32[4,1,128]{2,1,0:T(1,128)S(1)} all-gather(s32[1,1,128]{2,1,0:T(1,128)S(1)} %bitcast.20), channel_id=1, replica_groups=mesh['z'=16,'x'=4,'c'=2,'mp'=4] {'x'}, dimensions={0}, use_global_device_ids=true | all-gather | bytes 2560 | tf_op jit(solution)/shard_map/all_gather | solution.py:404
  60.5 0.0 copy-done.6
  60.5 1.6 %pack.1 = bf16[1024,256]{1,0:T(8,128)(2,1)} custom-call(s32[1,128]{1,0:T(1,128)S(1)} %copy-done.3, bf16[128,1024]{1,0:T(8,128)(2,1)S(1)} %copy-done.6), custom_call_target="tpu_custom_call" | custom-call | flops 2147483648 | bytes 524288 | tf_op jit(solution)/shard_map/pack/pallas_call | solution.py:161
  62.0 24.7 %all-to-all-done.1 = bf16[128,8,256]{2,1,0:T(8,128)(2,1)S(1)} async-done(((bf16[128,8,256]{2,1,0:T(8,128)(2,1)}), bf16[128,8,256]{2,1,0:T(8,128)(2,1)S(1)}, u32[]{:S(2)}, u32[]{:S(2)}) %all-to-all-start.1) | async-done | bytes 524320 | tf_op jit(solution)/shard_map/all_to_all | solution.py:363
  86.7 0.5 select.3.f0
  87.2 4.2 %collective-permute-start.2 = (bf16[520,256]{1,0:T(8,128)(2,1)S(1)}, bf16[520,256]{1,0:T(8,128)(2,1)S(1)}, u32[]{:S(2)}, u32[]{:S(2)}) collective-permute-start(bf16[520,256]{1,0:T(8,128)(2,1)S(1)} %select.3.f0), channel_id=1, source_target_pairs={{0,3},{1,0},{2,1},{3,2},{4,7},{5,4},{6,5},{7,6},{8,11},{9,8},{10,9... | collective-permute-start | bytes 798728 | tf_op jit(solution)/shard_map/ppermute | solution.py:359
  91.5 2.5 %collective-permute-start.1 = (bf16[520,256]{1,0:T(8,128)(2,1)S(1)}, bf16[520,256]{1,0:T(8,128)(2,1)S(1)}, u32[]{:S(2)}, u32[]{:S(2)}) collective-permute-start(bf16[520,256]{1,0:T(8,128)(2,1)S(1)} %select.3.f0), channel_id=1, source_target_pairs={{0,2},{1,3},{2,0},{3,1},{4,6},{5,7},{6,4},{7,5},{8,10},{9,11},{10,... | collective-permute-start | bytes 798728 | tf_op jit(solution)/shard_map/ppermute | solution.py:359
  94.0 2.8 %collective-permute-start = (bf16[520,256]{1,0:T(8,128)(2,1)S(1)}, bf16[520,256]{1,0:T(8,128)(2,1)S(1)}, u32[]{:S(2)}, u32[]{:S(2)}) collective-permute-start(bf16[520,256]{1,0:T(8,128)(2,1)S(1)} %select.3.f0), channel_id=1, source_target_pairs={{0,1},{1,2},{2,3},{3,0},{4,5},{5,6},{6,7},{7,4},{8,9},{9,10},{10,1... | collective-permute-start | bytes 798728 | tf_op jit(solution)/shard_map/ppermute | solution.py:359
  96.7 11.2 %all-to-all-start.2 = ((bf16[128,8,256]{2,1,0:T(8,128)(2,1)}), bf16[128,8,256]{2,1,0:T(8,128)(2,1)S(1)}, u32[]{:S(2)}, u32[]{:S(2)}) async-start(bf16[128,8,256]{2,1,0:T(8,128)(2,1)} %bitcast.11), calls=%async_computation.2 | async-start | bytes 1048576 | tf_op jit(solution)/shard_map/all_to_all | solution.py:363
  108.0 0.0 collective-permute-done.2.f3
  108.0 0.0 collective-permute-done.1.f2
  108.0 0.0 collective-permute-done.f1
  108.0 3.8 %project.3 = bf16[128,1664]{1,0:T(8,128)(2,1)} custom-call(s32[5]{0:T(128)S(1)} %pad_add_fusion.order_ref, bf16[520,256]{1,0:T(8,128)(2,1)S(1)} %select.3.f0, bf16[520,256]{1,0:T(8,128)(2,1)S(1)} %collective-permute-done.f1, bf16[520,256]{1,0:T(8,128)(2,1)S(1)} %collective-permute-done.1.f2, bf16[520,256]{1,0:T(8,128)(2,1)S(1)} %collective-permute-done.2.f3, ...), custom_call_target="tpu_custom_call" | custom-call | flops 12884901888 | bytes 3145728 | tf_op jit(solution)/shard_map/project/pallas_call | solution.py:281
  111.8 0.0 copy-done.4
  111.9 7.0 %collective-permute-start.4 = (bf16[128,1664]{1,0:T(8,128)(2,1)}, bf16[128,1664]{1,0:T(8,128)(2,1)S(1)}, u32[]{:S(2)}, u32[]{:S(2)}) collective-permute-start(bf16[128,1664]{1,0:T(8,128)(2,1)} %project.3), channel_id=1, source_target_pairs={{0,16},{8,24},{16,0},{24,8},{1,17},{9,25},{17,1},{25,9},{2,18},{10... | collective-permute-start | bytes 1277960 | tf_op jit(solution)/shard_map/ppermute | solution.py:359
  118.8 0.0 copy-start.5
  118.9 0.9 copy-done.5
  119.8 4.0 %project.2 = (f32[128,1664]{1,0:T(8,128)S(1)}, bf16[128,1664]{1,0:T(8,128)(2,1)S(1)}, bf16[128,1664]{1,0:T(8,128)(2,1)S(1)}) custom-call(s32[5]{0:T(128)S(1)} %pad_add_fusion.order_ref, bf16[520,256]{1,0:T(8,128)(2,1)S(1)} %select.3.f0, bf16[520,256]{1,0:T(8,128)(2,1)S(1)} %copy-done.5, bf16[520,256]{1,0:T(8,128)(2,1)S(1)} %collective-permute-done.1.f2, ...), custom_call_target="tpu_custom_call" | custom-call | flops 38654705664 | bytes 3145728 | tf_op jit(solution)/shard_map/project/pallas_call | solution.py:281
  123.8 2.5 %collective-permute-start.3 = (bf16[128,1664]{1,0:T(8,128)(2,1)S(1)}, bf16[128,1664]{1,0:T(8,128)(2,1)S(1)}, u32[]{:S(2)}, u32[]{:S(2)}) collective-permute-start(bf16[128,1664]{1,0:T(8,128)(2,1)S(1)} %get-tuple-element.40), channel_id=1, source_target_pairs={{0,8},{8,16},{16,24},{24,0},{1,9},{9,17},{17,25},{25,1},{2,10},{10... | collective-permute-start | bytes 1277960 | tf_op jit(solution)/shard_map/ppermute | solution.py:359
  126.3 4.0 %collective-permute-start.5 = (bf16[128,1664]{1,0:T(8,128)(2,1)S(1)}, bf16[128,1664]{1,0:T(8,128)(2,1)S(1)}, u32[]{:S(2)}, u32[]{:S(2)}) collective-permute-start(bf16[128,1664]{1,0:T(8,128)(2,1)S(1)} %get-tuple-element.44), channel_id=1, source_target_pairs={{0,24},{8,0},{16,8},{24,16},{1,25},{9,1},{17,9},{25,17},{2,26},{10... | collective-permute-start | bytes 1277960 | tf_op jit(solution)/shard_map/ppermute | solution.py:359
  131.0 7.8 %all-to-all-done.2 = bf16[128,8,256]{2,1,0:T(8,128)(2,1)S(1)} async-done(((bf16[128,8,256]{2,1,0:T(8,128)(2,1)}), bf16[128,8,256]{2,1,0:T(8,128)(2,1)S(1)}, u32[]{:S(2)}, u32[]{:S(2)}) %all-to-all-start.2) | async-done | bytes 524320 | tf_op jit(solution)/shard_map/all_to_all | solution.py:363
  138.8 0.0 collective-permute-done.4.p2
  138.8 3.3 %credit.1 = (f32[256,1024]{1,0:T(8,128)}, f32[256,1024]{1,0:T(8,128)}) custom-call(s32[1,1024]{1,0:T(1,128)S(1)} %name.1.named_ref, bf16[1024,256]{1,0:T(8,128)(2,1)S(1)} %bitcast.14, bf16[256,1024]{1,0:T(8,128)(2,1)} %text_ref.3, bf16[256,1024]{1,0:T(8,128)(2,1)} %image_ref.3), custom_call_target="tpu_custom_call" | custom-call | tf_op jit(solution)/shard_map/credit/pallas_call | solution.py:212
  142.1 0.6 collective-permute-done.3.p1
  142.6 0.0 collective-permute-done.5.p3
  142.6 2.2 %attend.1 = bf16[128,512]{1,0:T(8,128)(2,1)} custom-call(s32[1]{0:T(128)S(6)} %copy.19.length_ref, f32[128,1664]{1,0:T(8,128)S(1)} %get-tuple-element.39.own_ref, bf16[128,1664]{1,0:T(8,128)(2,1)S(1)} %collective-permute-done.3.p1, bf16[128,1664]{1,0:T(8,128)(2,1)S(1)} %collective-permute-done.4.p2, bf16[128,1664]{1,0:T(8,128)(2,1)S(1)} %collective-permute-done.5.p3), custom_call_target="tpu_custom_call" | custom-call | tf_op jit(solution)/shard_map/attend/pallas_call | solution.py:347
  (6 shorter events, 0.0 us)
Async XLA Ops:
  7.2 44.2 %copy-start.7 = (bf16[1024]{0:T(1024)(128)(2,1)S(1)}, bf16[1024]{0:T(1024)(128)(2,1)}, u32[]{:S(2)}) copy-start(bf16[1024]{0:T(1024)(128)(2,1)} %param.19) | copy-start | bytes 6148
  7.2 53.3 %copy-start.6 = (bf16[128,1024]{1,0:T(8,128)(2,1)S(1)}, bf16[128,1024]{1,0:T(8,128)(2,1)}, u32[]{:S(2)}) copy-start(bf16[128,1024]{1,0:T(8,128)(2,1)} %grads_ref.1) | copy-start | bytes 786436
  7.2 100.8 %all-gather.3.cloned.1.call-start = ((), (), s32[]{:S(2)}) async-start(), calls=%async_computation.3 | async-start | bytes 3244032 | tf_op jit(solution)/shard_map/all_gather | solution.py:390
  9.0 42.8 %copy-start.3 = (s32[1,128]{1,0:T(1,128)S(1)}, s32[1,128]{1,0:T(1,128)}, u32[]{:S(2)}) copy-start(s32[1,128]{1,0:T(1,128)} %get-tuple-element.31.codes_ref) | copy-start | bytes 1540
  9.1 35.3 %all-to-all-start = ((s32[128,1,128]{2,1,0:T(1,128)}), s32[128,1,128]{2,1,0:T(1,128)S(1)}, u32[]{:S(2)}, u32[]{:S(2)}) async-start(s32[128,1,128]{2,1,0:T(1,128)} %bitcast.21), calls=%async_computation | async-start | bytes 131072 | tf_op jit(solution)/shard_map/all_to_all | solution.py:363
  30.2 1.0 copy-start
  31.2 1.0 copy-start.1
  32.3 0.7 copy-start.2
  45.6 41.1 %all-to-all-start.1 = ((bf16[128,8,256]{2,1,0:T(8,128)(2,1)}), bf16[128,8,256]{2,1,0:T(8,128)(2,1)S(1)}, u32[]{:S(2)}, u32[]{:S(2)}) async-start(bf16[128,8,256]{2,1,0:T(8,128)(2,1)} %bitcast.6), calls=%async_computation.1 | async-start | bytes 1048576 | tf_op jit(solution)/shard_map/all_to_all | solution.py:363
  87.2 20.7 %collective-permute-start.2 = (bf16[520,256]{1,0:T(8,128)(2,1)S(1)}, bf16[520,256]{1,0:T(8,128)(2,1)S(1)}, u32[]{:S(2)}, u32[]{:S(2)}) collective-permute-start(bf16[520,256]{1,0:T(8,128)(2,1)S(1)} %select.3.f0), channel_id=1, source_target_pairs={{0,3},{1,0},{2,1},{3,2},{4,7},{5,4},{6,5},{7,6},{8,11},{9,8},{10,9... | collective-permute-start | bytes 798728 | tf_op jit(solution)/shard_map/ppermute | solution.py:359
  91.5 16.5 %collective-permute-start.1 = (bf16[520,256]{1,0:T(8,128)(2,1)S(1)}, bf16[520,256]{1,0:T(8,128)(2,1)S(1)}, u32[]{:S(2)}, u32[]{:S(2)}) collective-permute-start(bf16[520,256]{1,0:T(8,128)(2,1)S(1)} %select.3.f0), channel_id=1, source_target_pairs={{0,2},{1,3},{2,0},{3,1},{4,6},{5,7},{6,4},{7,5},{8,10},{9,11},{10,... | collective-permute-start | bytes 798728 | tf_op jit(solution)/shard_map/ppermute | solution.py:359
  94.0 14.0 %collective-permute-start = (bf16[520,256]{1,0:T(8,128)(2,1)S(1)}, bf16[520,256]{1,0:T(8,128)(2,1)S(1)}, u32[]{:S(2)}, u32[]{:S(2)}) collective-permute-start(bf16[520,256]{1,0:T(8,128)(2,1)S(1)} %select.3.f0), channel_id=1, source_target_pairs={{0,1},{1,2},{2,3},{3,0},{4,5},{5,6},{6,7},{7,4},{8,9},{9,10},{10,1... | collective-permute-start | bytes 798728 | tf_op jit(solution)/shard_map/ppermute | solution.py:359
  96.7 42.0 %all-to-all-start.2 = ((bf16[128,8,256]{2,1,0:T(8,128)(2,1)}), bf16[128,8,256]{2,1,0:T(8,128)(2,1)S(1)}, u32[]{:S(2)}, u32[]{:S(2)}) async-start(bf16[128,8,256]{2,1,0:T(8,128)(2,1)} %bitcast.11), calls=%async_computation.2 | async-start | bytes 1048576 | tf_op jit(solution)/shard_map/all_to_all | solution.py:363
  108.0 3.8 %copy-start.4 = (bf16[520,256]{1,0:T(8,128)(2,1)}, bf16[520,256]{1,0:T(8,128)(2,1)S(1)}, u32[]{:S(2)}) copy-start(bf16[520,256]{1,0:T(8,128)(2,1)S(1)} %collective-permute-done.f1) | copy-start | bytes 798724
  111.9 26.9 %collective-permute-start.4 = (bf16[128,1664]{1,0:T(8,128)(2,1)}, bf16[128,1664]{1,0:T(8,128)(2,1)S(1)}, u32[]{:S(2)}, u32[]{:S(2)}) collective-permute-start(bf16[128,1664]{1,0:T(8,128)(2,1)} %project.3), channel_id=1, source_target_pairs={{0,16},{8,24},{16,0},{24,8},{1,17},{9,25},{17,1},{25,9},{2,18},{10... | collective-permute-start | bytes 1277960 | tf_op jit(solution)/shard_map/ppermute | solution.py:359
  118.8 1.0 copy-start.5
  123.8 18.8 %collective-permute-start.3 = (bf16[128,1664]{1,0:T(8,128)(2,1)S(1)}, bf16[128,1664]{1,0:T(8,128)(2,1)S(1)}, u32[]{:S(2)}, u32[]{:S(2)}) collective-permute-start(bf16[128,1664]{1,0:T(8,128)(2,1)S(1)} %get-tuple-element.40), channel_id=1, source_target_pairs={{0,8},{8,16},{16,24},{24,0},{1,9},{9,17},{17,25},{25,1},{2,10},{10... | collective-permute-start | bytes 1277960 | tf_op jit(solution)/shard_map/ppermute | solution.py:359
  126.3 16.3 %collective-permute-start.5 = (bf16[128,1664]{1,0:T(8,128)(2,1)S(1)}, bf16[128,1664]{1,0:T(8,128)(2,1)S(1)}, u32[]{:S(2)}, u32[]{:S(2)}) collective-permute-start(bf16[128,1664]{1,0:T(8,128)(2,1)S(1)} %get-tuple-element.44), channel_id=1, source_target_pairs={{0,24},{8,0},{16,8},{24,16},{1,25},{9,1},{17,9},{25,17},{2,26},{10... | collective-permute-start | bytes 1277960 | tf_op jit(solution)/shard_map/ppermute | solution.py:359
Sparse Core Ops, SparseCore 0:
  10.7 89.4 all-gather.2

commit v9 on v8

--- a/solution.py
+++ b/solution.py
@@ -214,12 +214,7 @@
         out_shape=[out, out],
         compiler_params=pltpu.CompilerParams(vmem_limit_bytes=VMEM_BYTES),
         name="credit",
-    )(
-        named,
-        grads,
-        pltpu.with_memory_space_constraint(text_rows, pltpu.HBM),
-        pltpu.with_memory_space_constraint(image_rows, pltpu.HBM),
-    )
+    )(named, grads, text_rows, image_rows)
 
 
 def project_kernel(shifts, order_ref, f0, f1, f2, f3, w_ref, *refs):

time: 154 us -> 155 us (level)
  local copies, waits for them, and re-layouts: 4.6 us -> 6.99 us
    all_to_all x3, waiting for transfers between devices: 43.5 us -> 40.1 us  [exchange(): return lax.all_to_all(value, DP, split_axis=0, concat_axis=0, tiled=True)]
    unnamed x16 -> x24, local copies, waits for them, and re-layouts: 3.72 us -> 6.11 us
    ppermute x6, waiting for transfers between devices: 0.62 us -> 2.9 us  [turn(): return lax.ppermute(value, axis, [(i, (i + k) % size) for i in range(size)])]
where the time goes in v9:
time: 155 us; the launch traced here: 154 us
  starting transfers between devices  60.4 us (39%)
  waiting for transfers between devices  43 us (28%)
  Pallas kernels  19.9 us (13%)
  between operations  14.9 us (10%)
  blocking collectives  8.61 us (6%)
  local copies, waits for them, and re-layouts  6.99 us (5%)
    all_to_all x3, waiting for transfers between devices, exchange(): return lax.all_to_all(value, DP, split_axis=0, concat_axis=0, tiled=True)  40.1 us
    all_to_all x3, starting transfers between devices, exchange(): return lax.all_to_all(value, DP, split_axis=0, concat_axis=0, tiled=True)  37.3 us
    ppermute x6, starting transfers between devices, turn(): return lax.ppermute(value, axis, [(i, (i + k) % size) for i in range(size)])  23.1 us
    pallas_call x2, Pallas kernels, project(): pl.pallas_call(functools.partial(project_kernel, shifts), out_shape=[jax....  8.69 us
    all_gather x1, blocking collectives, local(): all_codes = lax.all_gather(codes, 'x', axis=0, tiled=True)  8.61 us
    unnamed x24, local copies, waits for them, and re-layouts  6.11 us
    pallas_call x1, Pallas kernels, attend(): pl.pallas_call(attend_kernel, out_shape=jax.ShapeDtypeStruct((tokens, (co...  3.25 us
  transfers between devices with their start and end apart: 10, of which 4 were waited for; matrix products, arithmetic and copies ran while one was open for 1% of the time, Pallas kernels for 10%

profile of v9, /device:TPU:1, one launch (start us, length us, event | category | flops | bytes accessed | tf_op | source)
XLA Modules:
  0.0 153.8 jit_solution(4595489930132947675)
XLA Ops:
  7.2 0.0 copy-start.11
  7.2 0.0 copy-start.10
  7.2 0.0 all-gather.3.cloned.1.call-start
  7.2 1.8 %request.1 = (s32[128,128]{1,0:T(8,128)}, s32[1,128]{1,0:T(1,128)}, bf16[32,1536]{1,0:T(8,128)(2,1)}) custom-call(s32[1,128]{1,0:T(1,128)} %bitcast.22, s32[1,128]{1,0:T(1,128)} %bitcast.23, bf16[32,512]{1,0:T(8,128)(2,1)} %wq_ref.1, bf16[32,512]{1,0:T(8,128)(2,1)} %wk_ref.1, bf16[32,512]{1,0:T(8,128)(2,1)} %wv_ref.1), custom_call_target="tpu_custom_call" | custom-call | tf_op jit(solution)/shard_map/request/pallas_call | solution.py:59
  9.0 0.0 all-gather.3.cloned.1.call-update
  9.1 20.4 %all-to-all-start = ((s32[128,1,128]{2,1,0:T(1,128)}), s32[128,1,128]{2,1,0:T(1,128)S(1)}, u32[]{:S(2)}, u32[]{:S(2)}) async-start(s32[128,1,128]{2,1,0:T(1,128)} %bitcast.21), calls=%async_computation | async-start | bytes 131072 | tf_op jit(solution)/shard_map/all_to_all | solution.py:358
  29.5 0.7 reshape.42.dir_ref
  30.2 1.0 copy-done
  31.2 1.0 copy-done.2
  32.3 0.7 copy-done.4
  32.9 0.4 join.1.table_ref
  33.3 11.0 %all-to-all-done = s32[128,1,128]{2,1,0:T(1,128)S(1)} async-done(((s32[128,1,128]{2,1,0:T(1,128)}), s32[128,1,128]{2,1,0:T(1,128)S(1)}, u32[]{:S(2)}, u32[]{:S(2)}) %all-to-all-start) | async-done | bytes 65568 | tf_op jit(solution)/shard_map/all_to_all | solution.py:358
  44.3 1.3 answer.1
  45.6 5.7 %all-to-all-start.1 = ((bf16[128,8,256]{2,1,0:T(8,128)(2,1)}), bf16[128,8,256]{2,1,0:T(8,128)(2,1)S(1)}, u32[]{:S(2)}, u32[]{:S(2)}) async-start(bf16[128,8,256]{2,1,0:T(8,128)(2,1)} %bitcast.6), calls=%async_computation.1 | async-start | bytes 1048576 | tf_op jit(solution)/shard_map/all_to_all | solution.py:358
  51.3 0.1 pad_add_fusion.order_ref
  51.4 0.0 copy-done.11
  51.4 0.1 reshape.45
  51.5 0.1 reshape.46.gain_ref
  51.6 0.3 name.1.named_ref
  51.9 0.0 copy-done.5
  51.9 8.6 %all-gather = s32[4,1,128]{2,1,0:T(1,128)S(1)} all-gather(s32[1,1,128]{2,1,0:T(1,128)S(1)} %bitcast.20), channel_id=1, replica_groups=mesh['z'=16,'x'=4,'c'=2,'mp'=4] {'x'}, dimensions={0}, use_global_device_ids=true | all-gather | bytes 2560 | tf_op jit(solution)/shard_map/all_gather | solution.py:399
  60.5 0.0 copy-done.10
  60.5 1.6 %pack.1 = bf16[1024,256]{1,0:T(8,128)(2,1)} custom-call(s32[1,128]{1,0:T(1,128)S(1)} %copy-done.5, bf16[128,1024]{1,0:T(8,128)(2,1)S(1)} %copy-done.10), custom_call_target="tpu_custom_call" | custom-call | flops 2147483648 | bytes 524288 | tf_op jit(solution)/shard_map/pack/pallas_call | solution.py:161
  62.0 24.7 %all-to-all-done.1 = bf16[128,8,256]{2,1,0:T(8,128)(2,1)S(1)} async-done(((bf16[128,8,256]{2,1,0:T(8,128)(2,1)}), bf16[128,8,256]{2,1,0:T(8,128)(2,1)S(1)}, u32[]{:S(2)}, u32[]{:S(2)}) %all-to-all-start.1) | async-done | bytes 524320 | tf_op jit(solution)/shard_map/all_to_all | solution.py:358
  86.7 0.5 select.3.f0
  87.2 4.2 %collective-permute-start.2 = (bf16[520,256]{1,0:T(8,128)(2,1)S(1)}, bf16[520,256]{1,0:T(8,128)(2,1)S(1)}, u32[]{:S(2)}, u32[]{:S(2)}) collective-permute-start(bf16[520,256]{1,0:T(8,128)(2,1)S(1)} %select.3.f0), channel_id=1, source_target_pairs={{0,3},{1,0},{2,1},{3,2},{4,7},{5,4},{6,5},{7,6},{8,11},{9,8},{10,9... | collective-permute-start | bytes 798728 | tf_op jit(solution)/shard_map/ppermute | solution.py:354
  91.5 2.5 %collective-permute-start.1 = (bf16[520,256]{1,0:T(8,128)(2,1)S(1)}, bf16[520,256]{1,0:T(8,128)(2,1)S(1)}, u32[]{:S(2)}, u32[]{:S(2)}) collective-permute-start(bf16[520,256]{1,0:T(8,128)(2,1)S(1)} %select.3.f0), channel_id=1, source_target_pairs={{0,2},{1,3},{2,0},{3,1},{4,6},{5,7},{6,4},{7,5},{8,10},{9,11},{10,... | collective-permute-start | bytes 798728 | tf_op jit(solution)/shard_map/ppermute | solution.py:354
  94.0 2.8 %collective-permute-start = (bf16[520,256]{1,0:T(8,128)(2,1)S(1)}, bf16[520,256]{1,0:T(8,128)(2,1)S(1)}, u32[]{:S(2)}, u32[]{:S(2)}) collective-permute-start(bf16[520,256]{1,0:T(8,128)(2,1)S(1)} %select.3.f0), channel_id=1, source_target_pairs={{0,1},{1,2},{2,3},{3,0},{4,5},{5,6},{6,7},{7,4},{8,9},{9,10},{10,1... | collective-permute-start | bytes 798728 | tf_op jit(solution)/shard_map/ppermute | solution.py:354
  96.7 11.2 %all-to-all-start.2 = ((bf16[128,8,256]{2,1,0:T(8,128)(2,1)}), bf16[128,8,256]{2,1,0:T(8,128)(2,1)S(1)}, u32[]{:S(2)}, u32[]{:S(2)}) async-start(bf16[128,8,256]{2,1,0:T(8,128)(2,1)} %bitcast.11), calls=%async_computation.2 | async-start | bytes 1048576 | tf_op jit(solution)/shard_map/all_to_all | solution.py:358
  108.0 0.0 collective-permute-done.2.f3
  108.0 0.0 collective-permute-done.1.f2
  108.0 0.0 collective-permute-done.f1
  108.0 3.8 %project.3 = bf16[128,1664]{1,0:T(8,128)(2,1)} custom-call(s32[5]{0:T(128)S(1)} %pad_add_fusion.order_ref, bf16[520,256]{1,0:T(8,128)(2,1)S(1)} %select.3.f0, bf16[520,256]{1,0:T(8,128)(2,1)S(1)} %collective-permute-done.f1, bf16[520,256]{1,0:T(8,128)(2,1)S(1)} %collective-permute-done.1.f2, bf16[520,256]{1,0:T(8,128)(2,1)S(1)} %collective-permute-done.2.f3, ...), custom_call_target="tpu_custom_call" | custom-call | flops 12884901888 | bytes 3145728 | tf_op jit(solution)/shard_map/project/pallas_call | solution.py:276
  111.8 0.7 copy-done.6
  112.6 0.7 copy-done.8
  113.3 7.1 %collective-permute-start.4 = (bf16[128,1664]{1,0:T(8,128)(2,1)}, bf16[128,1664]{1,0:T(8,128)(2,1)S(1)}, u32[]{:S(2)}, u32[]{:S(2)}) collective-permute-start(bf16[128,1664]{1,0:T(8,128)(2,1)} %project.3), channel_id=1, source_target_pairs={{0,16},{8,24},{16,0},{24,8},{1,17},{9,25},{17,1},{25,9},{2,18},{10... | collective-permute-start | bytes 1277960 | tf_op jit(solution)/shard_map/ppermute | solution.py:354
  120.4 0.9 copy-done.7
  121.4 0.9 copy-done.9
  122.3 4.9 %project.2 = (f32[128,1664]{1,0:T(8,128)S(1)}, bf16[128,1664]{1,0:T(8,128)(2,1)}, bf16[128,1664]{1,0:T(8,128)(2,1)}) custom-call(s32[5]{0:T(128)S(1)} %pad_add_fusion.order_ref, bf16[520,256]{1,0:T(8,128)(2,1)S(1)} %select.3.f0, bf16[520,256]{1,0:T(8,128)(2,1)S(1)} %copy-done.9, bf16[520,256]{1,0:T(8,128)(2,1)S(1)} %copy-done.7, ...), custom_call_target="tpu_custom_call" | custom-call | flops 38654705664 | bytes 3145728 | tf_op jit(solution)/shard_map/project/pallas_call | solution.py:276
  127.2 2.5 %collective-permute-start.3 = (bf16[128,1664]{1,0:T(8,128)(2,1)}, bf16[128,1664]{1,0:T(8,128)(2,1)S(1)}, u32[]{:S(2)}, u32[]{:S(2)}) collective-permute-start(bf16[128,1664]{1,0:T(8,128)(2,1)} %get-tuple-element.40), channel_id=1, source_target_pairs={{0,8},{8,16},{16,24},{24,0},{1,9},{9,17},{17,25},{25,1},{2,10},{10... | collective-permute-start | bytes 1277960 | tf_op jit(solution)/shard_map/ppermute | solution.py:354
  129.7 4.0 %collective-permute-start.5 = (bf16[128,1664]{1,0:T(8,128)(2,1)}, bf16[128,1664]{1,0:T(8,128)(2,1)}, u32[]{:S(2)}, u32[]{:S(2)}) collective-permute-start(bf16[128,1664]{1,0:T(8,128)(2,1)} %get-tuple-element.44), channel_id=1, source_target_pairs={{0,24},{8,0},{16,8},{24,16},{1,25},{9,1},{17,9},{25,17},{2,26},{10... | collective-permute-start | bytes 1277960 | tf_op jit(solution)/shard_map/ppermute | solution.py:354
  134.4 4.4 %all-to-all-done.2 = bf16[128,8,256]{2,1,0:T(8,128)(2,1)S(1)} async-done(((bf16[128,8,256]{2,1,0:T(8,128)(2,1)}), bf16[128,8,256]{2,1,0:T(8,128)(2,1)S(1)}, u32[]{:S(2)}, u32[]{:S(2)}) %all-to-all-start.2) | async-done | bytes 524320 | tf_op jit(solution)/shard_map/all_to_all | solution.py:358
  138.8 0.0 collective-permute-done.4.p2
  138.8 0.0 copy-done.3
  138.8 2.1 %credit.1 = (f32[256,1024]{1,0:T(8,128)}, f32[256,1024]{1,0:T(8,128)}) custom-call(s32[1,1024]{1,0:T(1,128)S(1)} %name.1.named_ref, bf16[1024,256]{1,0:T(8,128)(2,1)S(1)} %bitcast.14, bf16[256,1024]{1,0:T(8,128)(2,1)S(1)} %copy-done.1, bf16[256,1024]{1,0:T(8,128)(2,1)S(1)} %copy-done.3), custom_call_target="tpu_custom_call" | custom-call | tf_op jit(solution)/shard_map/credit/pallas_call | solution.py:212
  140.9 2.8 %collective-permute-done.3.p1 = bf16[128,1664]{1,0:T(8,128)(2,1)S(1)} collective-permute-done((bf16[128,1664]{1,0:T(8,128)(2,1)}, bf16[128,1664]{1,0:T(8,128)(2,1)S(1)}, u32[]{:S(2)}, u32[]{:S(2)}) %collective-permute-start.3) | collective-permute-done | bytes 426016 | tf_op jit(solution)/shard_map/ppermute | solution.py:354
  143.7 0.0 collective-permute-done.5.p3
  143.7 3.2 %attend.1 = bf16[128,512]{1,0:T(8,128)(2,1)} custom-call(s32[1]{0:T(128)S(6)} %copy.19.length_ref, f32[128,1664]{1,0:T(8,128)S(1)} %get-tuple-element.39.own_ref, bf16[128,1664]{1,0:T(8,128)(2,1)S(1)} %collective-permute-done.3.p1, bf16[128,1664]{1,0:T(8,128)(2,1)S(1)} %collective-permute-done.4.p2, bf16[128,1664]{1,0:T(8,128)(2,1)} %collective-permute-done.5.p3), custom_call_target="tpu_custom_call" | custom-call | tf_op jit(solution)/shard_map/attend/pallas_call | solution.py:342
  (14 shorter events, 0.1 us)
Async XLA Ops:
  7.2 44.2 %copy-start.11 = (bf16[1024]{0:T(1024)(128)(2,1)S(1)}, bf16[1024]{0:T(1024)(128)(2,1)}, u32[]{:S(2)}) copy-start(bf16[1024]{0:T(1024)(128)(2,1)} %param.19) | copy-start | bytes 6148
  7.2 53.3 %copy-start.10 = (bf16[128,1024]{1,0:T(8,128)(2,1)S(1)}, bf16[128,1024]{1,0:T(8,128)(2,1)}, u32[]{:S(2)}) copy-start(bf16[128,1024]{1,0:T(8,128)(2,1)} %grads_ref.1) | copy-start | bytes 786436
  7.2 100.8 %all-gather.3.cloned.1.call-start = ((), (), s32[]{:S(2)}) async-start(), calls=%async_computation.3 | async-start | bytes 3244032 | tf_op jit(solution)/shard_map/all_gather | solution.py:385
  9.0 42.8 %copy-start.5 = (s32[1,128]{1,0:T(1,128)S(1)}, s32[1,128]{1,0:T(1,128)}, u32[]{:S(2)}) copy-start(s32[1,128]{1,0:T(1,128)} %get-tuple-element.31.codes_ref) | copy-start | bytes 1540
  9.1 35.3 %all-to-all-start = ((s32[128,1,128]{2,1,0:T(1,128)}), s32[128,1,128]{2,1,0:T(1,128)S(1)}, u32[]{:S(2)}, u32[]{:S(2)}) async-start(s32[128,1,128]{2,1,0:T(1,128)} %bitcast.21), calls=%async_computation | async-start | bytes 131072 | tf_op jit(solution)/shard_map/all_to_all | solution.py:358
  30.2 1.0 copy-start
  31.2 1.0 copy-start.2
  32.3 0.7 copy-start.4
  45.6 41.1 %all-to-all-start.1 = ((bf16[128,8,256]{2,1,0:T(8,128)(2,1)}), bf16[128,8,256]{2,1,0:T(8,128)(2,1)S(1)}, u32[]{:S(2)}, u32[]{:S(2)}) async-start(bf16[128,8,256]{2,1,0:T(8,128)(2,1)} %bitcast.6), calls=%async_computation.1 | async-start | bytes 1048576 | tf_op jit(solution)/shard_map/all_to_all | solution.py:358
  87.2 20.7 %collective-permute-start.2 = (bf16[520,256]{1,0:T(8,128)(2,1)S(1)}, bf16[520,256]{1,0:T(8,128)(2,1)S(1)}, u32[]{:S(2)}, u32[]{:S(2)}) collective-permute-start(bf16[520,256]{1,0:T(8,128)(2,1)S(1)} %select.3.f0), channel_id=1, source_target_pairs={{0,3},{1,0},{2,1},{3,2},{4,7},{5,4},{6,5},{7,6},{8,11},{9,8},{10,9... | collective-permute-start | bytes 798728 | tf_op jit(solution)/shard_map/ppermute | solution.py:354
  91.5 16.5 %collective-permute-start.1 = (bf16[520,256]{1,0:T(8,128)(2,1)S(1)}, bf16[520,256]{1,0:T(8,128)(2,1)S(1)}, u32[]{:S(2)}, u32[]{:S(2)}) collective-permute-start(bf16[520,256]{1,0:T(8,128)(2,1)S(1)} %select.3.f0), channel_id=1, source_target_pairs={{0,2},{1,3},{2,0},{3,1},{4,6},{5,7},{6,4},{7,5},{8,10},{9,11},{10,... | collective-permute-start | bytes 798728 | tf_op jit(solution)/shard_map/ppermute | solution.py:354
  94.0 14.0 %collective-permute-start = (bf16[520,256]{1,0:T(8,128)(2,1)S(1)}, bf16[520,256]{1,0:T(8,128)(2,1)S(1)}, u32[]{:S(2)}, u32[]{:S(2)}) collective-permute-start(bf16[520,256]{1,0:T(8,128)(2,1)S(1)} %select.3.f0), channel_id=1, source_target_pairs={{0,1},{1,2},{2,3},{3,0},{4,5},{5,6},{6,7},{7,4},{8,9},{9,10},{10,1... | collective-permute-start | bytes 798728 | tf_op jit(solution)/shard_map/ppermute | solution.py:354
  96.7 42.0 %all-to-all-start.2 = ((bf16[128,8,256]{2,1,0:T(8,128)(2,1)}), bf16[128,8,256]{2,1,0:T(8,128)(2,1)S(1)}, u32[]{:S(2)}, u32[]{:S(2)}) async-start(bf16[128,8,256]{2,1,0:T(8,128)(2,1)} %bitcast.11), calls=%async_computation.2 | async-start | bytes 1048576 | tf_op jit(solution)/shard_map/all_to_all | solution.py:358
  111.8 0.7 copy-start.6
  112.6 0.7 copy-start.8
  113.3 25.5 %copy-start.1 = (bf16[256,1024]{1,0:T(8,128)(2,1)S(1)}, bf16[256,1024]{1,0:T(8,128)(2,1)}, u32[]{:S(2)}) copy-start(bf16[256,1024]{1,0:T(8,128)(2,1)} %text_ref.3) | copy-start | bytes 1572868
  113.3 25.5 %copy-start.3 = (bf16[256,1024]{1,0:T(8,128)(2,1)S(1)}, bf16[256,1024]{1,0:T(8,128)(2,1)}, u32[]{:S(2)}) copy-start(bf16[256,1024]{1,0:T(8,128)(2,1)} %image_ref.3) | copy-start | bytes 1572868
  113.3 25.5 %collective-permute-start.4 = (bf16[128,1664]{1,0:T(8,128)(2,1)}, bf16[128,1664]{1,0:T(8,128)(2,1)S(1)}, u32[]{:S(2)}, u32[]{:S(2)}) collective-permute-start(bf16[128,1664]{1,0:T(8,128)(2,1)} %project.3), channel_id=1, source_target_pairs={{0,16},{8,24},{16,0},{24,8},{1,17},{9,25},{17,1},{25,9},{2,18},{10... | collective-permute-start | bytes 1277960 | tf_op jit(solution)/shard_map/ppermute | solution.py:354
  120.4 1.0 copy-start.7
  121.4 1.0 copy-start.9
  127.2 16.5 %collective-permute-start.3 = (bf16[128,1664]{1,0:T(8,128)(2,1)}, bf16[128,1664]{1,0:T(8,128)(2,1)S(1)}, u32[]{:S(2)}, u32[]{:S(2)}) collective-permute-start(bf16[128,1664]{1,0:T(8,128)(2,1)} %get-tuple-element.40), channel_id=1, source_target_pairs={{0,8},{8,16},{16,24},{24,0},{1,9},{9,17},{17,25},{25,1},{2,10},{10... | collective-permute-start | bytes 1277960 | tf_op jit(solution)/shard_map/ppermute | solution.py:354
  129.7 14.0 %collective-permute-start.5 = (bf16[128,1664]{1,0:T(8,128)(2,1)}, bf16[128,1664]{1,0:T(8,128)(2,1)}, u32[]{:S(2)}, u32[]{:S(2)}) collective-permute-start(bf16[128,1664]{1,0:T(8,128)(2,1)} %get-tuple-element.44), channel_id=1, source_target_pairs={{0,24},{8,0},{16,8},{24,16},{1,25},{9,1},{17,9},{25,17},{2,26},{10... | collective-permute-start | bytes 1277960 | tf_op jit(solution)/shard_map/ppermute | solution.py:354
Sparse Core Ops, SparseCore 0:
  10.7 89.4 all-gather.2

commit v10 on v9

--- a/solution.py
+++ b/solution.py
@@ -410,11 +410,10 @@
 
     (far,) = project((2,), order, turns, weights)
     own, after, before = project((0, 1, 3), order, turns, weights)
-    far = turn(far, "x", 2)
-    far, got_grads = lax.optimization_barrier((far, got_grads))
-    received = (turn(after, "x", 1), far, turn(before, "x", 3))
+    received = (turn(after, "x", 1), turn(far, "x", 2), turn(before, "x", 3))
+    context = attend(session_length, own, received)
+    context, got_grads = lax.optimization_barrier((context, got_grads))
     text_grad, image_grad = credit(named, got_grads, text_rows, image_rows)
-    context = attend(session_length, own, received)
     return (context, text_grad, image_grad)
 
 

time: 155 us -> 154 us (level)
  waiting for transfers between devices: 43 us -> 49 us
  local copies, waits for them, and re-layouts: 6.99 us -> 3.66 us
  Pallas kernels: 19.9 us -> 17.2 us
    ppermute x6, waiting for transfers between devices: 2.9 us -> 13.3 us  [turn(): return lax.ppermute(value, axis, [(i, (i + k) % size) for i in range(size)])]
    all_to_all x3, waiting for transfers between devices: 40.1 us -> 35.7 us  [exchange(): return lax.all_to_all(value, DP, split_axis=0, concat_axis=0, tiled=True)]
    unnamed x24 -> x16, local copies, waits for them, and re-layouts: 6.11 us -> 2.79 us
    pallas_call x2, Pallas kernels: 8.69 us -> 7.05 us  [project(): pl.pallas_call(functools.partial(project_kernel, shifts), out_shape=[jax....]
  transfers between devices with their start and end apart: 10 -> 10, of which waited for: 4 -> 4; matrix products, arithmetic and copies ran while one was open for 1% -> 1% of each run, Pallas kernels for 10% -> 9%
where the time goes in v10:
time: 154 us; the launch traced here: 153 us
  starting transfers between devices  59.4 us (39%)
  waiting for transfers between devices  49 us (32%)
  Pallas kernels  17.2 us (11%)
  between operations  14.9 us (10%)
  blocking collectives  8.61 us (6%)
  local copies, waits for them, and re-layouts  3.66 us (2%)
    all_to_all x3, starting transfers between devices, exchange(): return lax.all_to_all(value, DP, split_axis=0, concat_axis=0, tiled=True)  37.3 us
    all_to_all x3, waiting for transfers between devices, exchange(): return lax.all_to_all(value, DP, split_axis=0, concat_axis=0, tiled=True)  35.7 us
    ppermute x6, starting transfers between devices, turn(): return lax.ppermute(value, axis, [(i, (i + k) % size) for i in range(size)])  22.1 us
    ppermute x6, waiting for transfers between devices, turn(): return lax.ppermute(value, axis, [(i, (i + k) % size) for i in range(size)])  13.3 us
    all_gather x1, blocking collectives, local(): all_codes = lax.all_gather(codes, 'x', axis=0, tiled=True)  8.61 us
    pallas_call x2, Pallas kernels, project(): pl.pallas_call(functools.partial(project_kernel, shifts), out_shape=[jax....  7.05 us
  transfers between devices with their start and end apart: 10, of which 4 were waited for; matrix products, arithmetic and copies ran while one was open for 1% of the time, Pallas kernels for 9%

profile of v10, /device:TPU:1, one launch (start us, length us, event | category | flops | bytes accessed | tf_op | source)
XLA Modules:
  0.0 152.9 jit_solution(9929877080006767865)
XLA Ops:
  7.2 0.0 copy-start.7
  7.2 0.0 copy-start.6
  7.2 0.0 all-gather.3.cloned.1.call-start
  7.2 1.8 %request.1 = (s32[128,128]{1,0:T(8,128)}, s32[1,128]{1,0:T(1,128)}, bf16[32,1536]{1,0:T(8,128)(2,1)}) custom-call(s32[1,128]{1,0:T(1,128)} %bitcast.22, s32[1,128]{1,0:T(1,128)} %bitcast.23, bf16[32,512]{1,0:T(8,128)(2,1)} %wq_ref.1, bf16[32,512]{1,0:T(8,128)(2,1)} %wk_ref.1, bf16[32,512]{1,0:T(8,128)(2,1)} %wv_ref.1), custom_call_target="tpu_custom_call" | custom-call | tf_op jit(solution)/shard_map/request/pallas_call | solution.py:59
  9.0 0.0 all-gather.3.cloned.1.call-update
  9.1 20.4 %all-to-all-start = ((s32[128,1,128]{2,1,0:T(1,128)}), s32[128,1,128]{2,1,0:T(1,128)S(1)}, u32[]{:S(2)}, u32[]{:S(2)}) async-start(s32[128,1,128]{2,1,0:T(1,128)} %bitcast.21), calls=%async_computation | async-start | bytes 131072 | tf_op jit(solution)/shard_map/all_to_all | solution.py:358
  29.5 0.7 reshape.42.dir_ref
  30.2 1.0 copy-done
  31.2 1.0 copy-done.2
  32.3 0.7 copy-done.4
  32.9 0.4 join.1.table_ref
  33.3 11.0 %all-to-all-done = s32[128,1,128]{2,1,0:T(1,128)S(1)} async-done(((s32[128,1,128]{2,1,0:T(1,128)}), s32[128,1,128]{2,1,0:T(1,128)S(1)}, u32[]{:S(2)}, u32[]{:S(2)}) %all-to-all-start) | async-done | bytes 65568 | tf_op jit(solution)/shard_map/all_to_all | solution.py:358
  44.3 1.3 answer.1
  45.6 5.7 %all-to-all-start.1 = ((bf16[128,8,256]{2,1,0:T(8,128)(2,1)}), bf16[128,8,256]{2,1,0:T(8,128)(2,1)S(1)}, u32[]{:S(2)}, u32[]{:S(2)}) async-start(bf16[128,8,256]{2,1,0:T(8,128)(2,1)} %bitcast.6), calls=%async_computation.1 | async-start | bytes 1048576 | tf_op jit(solution)/shard_map/all_to_all | solution.py:358
  51.3 0.1 pad_add_fusion.order_ref
  51.4 0.0 copy-done.7
  51.4 0.1 reshape.45
  51.5 0.1 reshape.46.gain_ref
  51.6 0.3 name.1.named_ref
  51.9 0.0 copy-done.5
  51.9 8.6 %all-gather = s32[4,1,128]{2,1,0:T(1,128)S(1)} all-gather(s32[1,1,128]{2,1,0:T(1,128)S(1)} %bitcast.20), channel_id=1, replica_groups=mesh['z'=16,'x'=4,'c'=2,'mp'=4] {'x'}, dimensions={0}, use_global_device_ids=true | all-gather | bytes 2560 | tf_op jit(solution)/shard_map/all_gather | solution.py:399
  60.5 0.0 copy-done.6
  60.5 1.6 %pack.1 = bf16[1024,256]{1,0:T(8,128)(2,1)} custom-call(s32[1,128]{1,0:T(1,128)S(1)} %copy-done.5, bf16[128,1024]{1,0:T(8,128)(2,1)S(1)} %copy-done.6), custom_call_target="tpu_custom_call" | custom-call | flops 2147483648 | bytes 524288 | tf_op jit(solution)/shard_map/pack/pallas_call | solution.py:161
  62.0 24.7 %all-to-all-done.1 = bf16[128,8,256]{2,1,0:T(8,128)(2,1)S(1)} async-done(((bf16[128,8,256]{2,1,0:T(8,128)(2,1)}), bf16[128,8,256]{2,1,0:T(8,128)(2,1)S(1)}, u32[]{:S(2)}, u32[]{:S(2)}) %all-to-all-start.1) | async-done | bytes 524320 | tf_op jit(solution)/shard_map/all_to_all | solution.py:358
  86.7 0.5 select.3.f0
  87.3 2.9 %collective-permute-start = (bf16[520,256]{1,0:T(8,128)(2,1)S(1)}, bf16[520,256]{1,0:T(8,128)(2,1)S(1)}, u32[]{:S(2)}, u32[]{:S(2)}) collective-permute-start(bf16[520,256]{1,0:T(8,128)(2,1)S(1)} %select.3.f0), channel_id=1, source_target_pairs={{0,1},{1,2},{2,3},{3,0},{4,5},{5,6},{6,7},{7,4},{8,9},{9,10},{10,1... | collective-permute-start | bytes 798728 | tf_op jit(solution)/shard_map/ppermute | solution.py:354
  90.2 4.4 %collective-permute-start.1 = (bf16[520,256]{1,0:T(8,128)(2,1)S(1)}, bf16[520,256]{1,0:T(8,128)(2,1)S(1)}, u32[]{:S(2)}, u32[]{:S(2)}) collective-permute-start(bf16[520,256]{1,0:T(8,128)(2,1)S(1)} %select.3.f0), channel_id=1, source_target_pairs={{0,2},{1,3},{2,0},{3,1},{4,6},{5,7},{6,4},{7,5},{8,10},{9,11},{10,... | collective-permute-start | bytes 798728 | tf_op jit(solution)/shard_map/ppermute | solution.py:354
  94.6 3.4 %collective-permute-start.2 = (bf16[520,256]{1,0:T(8,128)(2,1)S(1)}, bf16[520,256]{1,0:T(8,128)(2,1)S(1)}, u32[]{:S(2)}, u32[]{:S(2)}) collective-permute-start(bf16[520,256]{1,0:T(8,128)(2,1)S(1)} %select.3.f0), channel_id=1, source_target_pairs={{0,3},{1,0},{2,1},{3,2},{4,7},{5,4},{6,5},{7,6},{8,11},{9,8},{10,9... | collective-permute-start | bytes 798728 | tf_op jit(solution)/shard_map/ppermute | solution.py:354
  98.0 11.2 %all-to-all-start.2 = ((bf16[128,8,256]{2,1,0:T(8,128)(2,1)}), bf16[128,8,256]{2,1,0:T(8,128)(2,1)S(1)}, u32[]{:S(2)}, u32[]{:S(2)}) async-start(bf16[128,8,256]{2,1,0:T(8,128)(2,1)} %bitcast.11), calls=%async_computation.2 | async-start | bytes 1048576 | tf_op jit(solution)/shard_map/all_to_all | solution.py:358
  109.2 0.0 collective-permute-done.f1
  109.2 0.0 collective-permute-done.1.f2
  109.2 0.0 collective-permute-done.2.f3
  109.2 0.0 all-gather.3.cloned.1.call-done.w_ref
  109.2 3.0 %project.3 = bf16[128,1664]{1,0:T(8,128)(2,1)S(1)} custom-call(s32[5]{0:T(128)S(1)} %pad_add_fusion.order_ref, bf16[520,256]{1,0:T(8,128)(2,1)S(1)} %select.3.f0, bf16[520,256]{1,0:T(8,128)(2,1)S(1)} %collective-permute-done.f1, bf16[520,256]{1,0:T(8,128)(2,1)S(1)} %collective-permute-done.1.f2, bf16[520,256]{1,0:T(8,128)(2,1)S(1)} %collective-permute-done.2.f3, ...), custom_call_target="tpu_custom_call" | custom-call | flops 12884901888 | bytes 3145728 | tf_op jit(solution)/shard_map/project/pallas_call | solution.py:276
  112.3 0.0 copy-start.1
  112.3 0.0 copy-start.3
  112.3 4.9 %collective-permute-start.4 = (bf16[128,1664]{1,0:T(8,128)(2,1)S(1)}, bf16[128,1664]{1,0:T(8,128)(2,1)S(1)}, u32[]{:S(2)}, u32[]{:S(2)}) collective-permute-start(bf16[128,1664]{1,0:T(8,128)(2,1)S(1)} %project.3), channel_id=1, source_target_pairs={{0,16},{8,24},{16,0},{24,8},{1,17},{9,25},{17,1},{25,9},{2,18},{10... | collective-permute-start | bytes 1277960 | tf_op jit(solution)/shard_map/ppermute | solution.py:354
  117.2 4.0 %project.2 = (f32[128,1664]{1,0:T(8,128)S(1)}, bf16[128,1664]{1,0:T(8,128)(2,1)S(1)}, bf16[128,1664]{1,0:T(8,128)(2,1)S(1)}) custom-call(s32[5]{0:T(128)S(1)} %pad_add_fusion.order_ref, bf16[520,256]{1,0:T(8,128)(2,1)S(1)} %select.3.f0, bf16[520,256]{1,0:T(8,128)(2,1)S(1)} %collective-permute-done.f1, bf16[520,256]{1,0:T(8,128)(2,1)S(1)} %collective-permute-done.1.f2, ...), custom_call_target="tpu_custom_call" | custom-call | flops 38654705664 | bytes 3145728 | tf_op jit(solution)/shard_map/project/pallas_call | solution.py:276
  121.3 2.2 %collective-permute-start.3 = (bf16[128,1664]{1,0:T(8,128)(2,1)S(1)}, bf16[128,1664]{1,0:T(8,128)(2,1)S(1)}, u32[]{:S(2)}, u32[]{:S(2)}) collective-permute-start(bf16[128,1664]{1,0:T(8,128)(2,1)S(1)} %get-tuple-element.40), channel_id=1, source_target_pairs={{0,8},{8,16},{16,24},{24,0},{1,9},{9,17},{17,25},{25,1},{2,10},{10... | collective-permute-start | bytes 1277960 | tf_op jit(solution)/shard_map/ppermute | solution.py:354
  123.5 4.3 %collective-permute-start.5 = (bf16[128,1664]{1,0:T(8,128)(2,1)S(1)}, bf16[128,1664]{1,0:T(8,128)(2,1)S(1)}, u32[]{:S(2)}, u32[]{:S(2)}) collective-permute-start(bf16[128,1664]{1,0:T(8,128)(2,1)S(1)} %get-tuple-element.41), channel_id=1, source_target_pairs={{0,24},{8,0},{16,8},{24,16},{1,25},{9,1},{17,9},{25,17},{2,26},{10... | collective-permute-start | bytes 1277960 | tf_op jit(solution)/shard_map/ppermute | solution.py:354
  128.4 0.8 collective-permute-done.4.p2
  129.2 12.5 %collective-permute-done.3.p1 = bf16[128,1664]{1,0:T(8,128)(2,1)S(1)} collective-permute-done((bf16[128,1664]{1,0:T(8,128)(2,1)S(1)}, bf16[128,1664]{1,0:T(8,128)(2,1)S(1)}, u32[]{:S(2)}, u32[]{:S(2)}) %collective-permute-start.3) | collective-permute-done | bytes 426016 | tf_op jit(solution)/shard_map/ppermute | solution.py:354
  141.7 0.0 collective-permute-done.5.p3
  141.7 2.2 %attend.1 = bf16[128,512]{1,0:T(8,128)(2,1)} custom-call(s32[1]{0:T(128)S(6)} %copy.19.length_ref, f32[128,1664]{1,0:T(8,128)S(1)} %get-tuple-element.39.own_ref, bf16[128,1664]{1,0:T(8,128)(2,1)S(1)} %collective-permute-done.3.p1, bf16[128,1664]{1,0:T(8,128)(2,1)S(1)} %collective-permute-done.4.p2, bf16[128,1664]{1,0:T(8,128)(2,1)S(1)} %collective-permute-done.5.p3), custom_call_target="tpu_custom_call" | custom-call | tf_op jit(solution)/shard_map/attend/pallas_call | solution.py:342
  143.9 0.0 all-to-all-done.2
  143.9 0.0 copy-done.1
  143.9 0.0 copy-done.3
  143.9 2.1 %credit.1 = (f32[256,1024]{1,0:T(8,128)}, f32[256,1024]{1,0:T(8,128)}) custom-call(s32[1,1024]{1,0:T(1,128)S(1)} %name.1.named_ref, bf16[1024,256]{1,0:T(8,128)(2,1)S(1)} %bitcast.14, bf16[256,1024]{1,0:T(8,128)(2,1)S(1)} %copy-done.1, bf16[256,1024]{1,0:T(8,128)(2,1)S(1)} %copy-done.3), custom_call_target="tpu_custom_call" | custom-call | tf_op jit(solution)/shard_map/credit/pallas_call | solution.py:212
  (6 shorter events, 0.0 us)
Async XLA Ops:
  7.2 44.2 %copy-start.7 = (bf16[1024]{0:T(1024)(128)(2,1)S(1)}, bf16[1024]{0:T(1024)(128)(2,1)}, u32[]{:S(2)}) copy-start(bf16[1024]{0:T(1024)(128)(2,1)} %param.19) | copy-start | bytes 6148
  7.2 53.3 %copy-start.6 = (bf16[128,1024]{1,0:T(8,128)(2,1)S(1)}, bf16[128,1024]{1,0:T(8,128)(2,1)}, u32[]{:S(2)}) copy-start(bf16[128,1024]{1,0:T(8,128)(2,1)} %grads_ref.1) | copy-start | bytes 786436
  7.2 102.0 %all-gather.3.cloned.1.call-start = ((), (), s32[]{:S(2)}) async-start(), calls=%async_computation.3 | async-start | bytes 3244032 | tf_op jit(solution)/shard_map/all_gather | solution.py:385
  9.0 42.8 %copy-start.5 = (s32[1,128]{1,0:T(1,128)S(1)}, s32[1,128]{1,0:T(1,128)}, u32[]{:S(2)}) copy-start(s32[1,128]{1,0:T(1,128)} %get-tuple-element.31.codes_ref) | copy-start | bytes 1540
  9.1 35.3 %all-to-all-start = ((s32[128,1,128]{2,1,0:T(1,128)}), s32[128,1,128]{2,1,0:T(1,128)S(1)}, u32[]{:S(2)}, u32[]{:S(2)}) async-start(s32[128,1,128]{2,1,0:T(1,128)} %bitcast.21), calls=%async_computation | async-start | bytes 131072 | tf_op jit(solution)/shard_map/all_to_all | solution.py:358
  30.2 1.0 copy-start
  31.2 1.0 copy-start.2
  32.3 0.7 copy-start.4
  45.6 41.1 %all-to-all-start.1 = ((bf16[128,8,256]{2,1,0:T(8,128)(2,1)}), bf16[128,8,256]{2,1,0:T(8,128)(2,1)S(1)}, u32[]{:S(2)}, u32[]{:S(2)}) async-start(bf16[128,8,256]{2,1,0:T(8,128)(2,1)} %bitcast.6), calls=%async_computation.1 | async-start | bytes 1048576 | tf_op jit(solution)/shard_map/all_to_all | solution.py:358
  87.3 21.9 %collective-permute-start = (bf16[520,256]{1,0:T(8,128)(2,1)S(1)}, bf16[520,256]{1,0:T(8,128)(2,1)S(1)}, u32[]{:S(2)}, u32[]{:S(2)}) collective-permute-start(bf16[520,256]{1,0:T(8,128)(2,1)S(1)} %select.3.f0), channel_id=1, source_target_pairs={{0,1},{1,2},{2,3},{3,0},{4,5},{5,6},{6,7},{7,4},{8,9},{9,10},{10,1... | collective-permute-start | bytes 798728 | tf_op jit(solution)/shard_map/ppermute | solution.py:354
  90.2 19.0 %collective-permute-start.1 = (bf16[520,256]{1,0:T(8,128)(2,1)S(1)}, bf16[520,256]{1,0:T(8,128)(2,1)S(1)}, u32[]{:S(2)}, u32[]{:S(2)}) collective-permute-start(bf16[520,256]{1,0:T(8,128)(2,1)S(1)} %select.3.f0), channel_id=1, source_target_pairs={{0,2},{1,3},{2,0},{3,1},{4,6},{5,7},{6,4},{7,5},{8,10},{9,11},{10,... | collective-permute-start | bytes 798728 | tf_op jit(solution)/shard_map/ppermute | solution.py:354
  94.6 14.6 %collective-permute-start.2 = (bf16[520,256]{1,0:T(8,128)(2,1)S(1)}, bf16[520,256]{1,0:T(8,128)(2,1)S(1)}, u32[]{:S(2)}, u32[]{:S(2)}) collective-permute-start(bf16[520,256]{1,0:T(8,128)(2,1)S(1)} %select.3.f0), channel_id=1, source_target_pairs={{0,3},{1,0},{2,1},{3,2},{4,7},{5,4},{6,5},{7,6},{8,11},{9,8},{10,9... | collective-permute-start | bytes 798728 | tf_op jit(solution)/shard_map/ppermute | solution.py:354
  98.0 46.0 %all-to-all-start.2 = ((bf16[128,8,256]{2,1,0:T(8,128)(2,1)}), bf16[128,8,256]{2,1,0:T(8,128)(2,1)S(1)}, u32[]{:S(2)}, u32[]{:S(2)}) async-start(bf16[128,8,256]{2,1,0:T(8,128)(2,1)} %bitcast.11), calls=%async_computation.2 | async-start | bytes 1048576 | tf_op jit(solution)/shard_map/all_to_all | solution.py:358
  112.3 31.6 %copy-start.1 = (bf16[256,1024]{1,0:T(8,128)(2,1)S(1)}, bf16[256,1024]{1,0:T(8,128)(2,1)}, u32[]{:S(2)}) copy-start(bf16[256,1024]{1,0:T(8,128)(2,1)} %text_ref.3) | copy-start | bytes 1572868
  112.3 31.6 %copy-start.3 = (bf16[256,1024]{1,0:T(8,128)(2,1)S(1)}, bf16[256,1024]{1,0:T(8,128)(2,1)}, u32[]{:S(2)}) copy-start(bf16[256,1024]{1,0:T(8,128)(2,1)} %image_ref.3) | copy-start | bytes 1572868
  112.3 16.9 %collective-permute-start.4 = (bf16[128,1664]{1,0:T(8,128)(2,1)S(1)}, bf16[128,1664]{1,0:T(8,128)(2,1)S(1)}, u32[]{:S(2)}, u32[]{:S(2)}) collective-permute-start(bf16[128,1664]{1,0:T(8,128)(2,1)S(1)} %project.3), channel_id=1, source_target_pairs={{0,16},{8,24},{16,0},{24,8},{1,17},{9,25},{17,1},{25,9},{2,18},{10... | collective-permute-start | bytes 1277960 | tf_op jit(solution)/shard_map/ppermute | solution.py:354
  121.3 20.4 %collective-permute-start.3 = (bf16[128,1664]{1,0:T(8,128)(2,1)S(1)}, bf16[128,1664]{1,0:T(8,128)(2,1)S(1)}, u32[]{:S(2)}, u32[]{:S(2)}) collective-permute-start(bf16[128,1664]{1,0:T(8,128)(2,1)S(1)} %get-tuple-element.40), channel_id=1, source_target_pairs={{0,8},{8,16},{16,24},{24,0},{1,9},{9,17},{17,25},{25,1},{2,10},{10... | collective-permute-start | bytes 1277960 | tf_op jit(solution)/shard_map/ppermute | solution.py:354
  123.5 18.2 %collective-permute-start.5 = (bf16[128,1664]{1,0:T(8,128)(2,1)S(1)}, bf16[128,1664]{1,0:T(8,128)(2,1)S(1)}, u32[]{:S(2)}, u32[]{:S(2)}) collective-permute-start(bf16[128,1664]{1,0:T(8,128)(2,1)S(1)} %get-tuple-element.41), channel_id=1, source_target_pairs={{0,24},{8,0},{16,8},{24,16},{1,25},{9,1},{17,9},{25,17},{2,26},{10... | collective-permute-start | bytes 1277960 | tf_op jit(solution)/shard_map/ppermute | solution.py:354
Sparse Core Ops, SparseCore 0:
  10.7 89.4 all-gather.2
